TPU v7x, 768 devices: a whole 4x8x12 slice. The times are simulated.
768 devices in a mesh: mem: 6 (over z_hi, core), lat: 128 (over y, x, z_lo).
Axes of the slice: x: 4, y: 8, z: 12 (z_hi: 3, z_lo: 4; z = z_hi * 4 + z_lo), core: 2. Of those that a mesh axis runs over, the one named last changes fastest.
Arguments:
- perturbations: bfloat16 [96, 2, 12, 512, 1440], P('mem', None, None, 'lat'), may hold values from -1 to 1
- gradient_held: float32 [2, 12, 512, 1440], P(None, 'mem', 'lat'), may hold values from -6 to 6
- block_owner: int32 [12], replicated, may hold values from 0 to 11, each once
Outputs:
- increment_held: float32 [2, 12, 512, 1440], P(None, 'mem', 'lat')
Inputs may be any that keep to these rules, and one draw needn't show every extreme that they name: `block_owner`: each value appears exactly once.
All inputs are finite; a program needn't handle non-finite values.
Results may differ from a plain program's by a relative error of at most 0.0022.
Values may be sent and summed in bfloat16 or wider, within the bound.
No kernel may reach another device: no remote copies, remote signals or barrier semaphores. Data moves between devices by JAX's collectives and lax.ppermute only.
A program may use at most 128 MiB of HBM per device.

v0:
```python
import math

import jax
import jax.numpy as jnp
from jax import lax
from jax.sharding import PartitionSpec as P


def extended_2(block, sides, width):
    for axis, dim in sides:
        count = lax.axis_size(axis)
        forward = [(i, i + 1) for i in range(count - 1)]
        backward = [(target, source) for source, target in forward]
        low = lax.ppermute(
            lax.slice_in_dim(block, block.shape[dim] - width, None, axis=dim), axis, forward
        )
        high = lax.ppermute(lax.slice_in_dim(block, 0, width, axis=dim), axis, backward)
        block = jnp.concatenate([low, block, high], axis=dim)
    return block


def weights_for(spread_cells):
    return [
        math.exp(-(offset * offset) / (2.0 * spread_cells * spread_cells))
        for offset in range(-4, 5)
    ]


def smooth_periodic(source, along_dim, weights):
    summed = jnp.zeros_like(source)
    for offset in range(-4, 5):
        summed = summed + weights[offset + 4] * jnp.roll(source, -offset, axis=along_dim)
    return summed


def smooth_bounded(source, along_dim, weights):
    length = source.shape[along_dim]
    widths = [(0, 0)] * source.ndim
    widths[along_dim] = (4, 4)
    padded = jnp.pad(source, widths)
    summed = jnp.zeros_like(source)
    for offset in range(-4, 5):
        summed = summed + weights[offset + 4] * lax.slice_in_dim(
            padded, 4 + offset, 4 + offset + length, axis=along_dim
        )
    return summed


def lat_rows(extended, weights, rows_here):
    summed = jnp.zeros(extended.shape[:1] + (rows_here,) + extended.shape[2:], jnp.float32)
    for offset in range(-4, 5):
        summed = summed + weights[offset + 4] * lax.slice_in_dim(
            extended, 4 + offset, 4 + offset + rows_here, axis=1
        )
    return summed


def local(perturbations, gradient_held, block_owner):
    gathered = lax.all_gather(gradient_held, "mem", axis=1, tiled=True)
    slot_count, levels, rows_here, lon_count = gathered.shape
    places = jnp.arange(levels, dtype=jnp.int32)
    inverse = jnp.sum(
        jnp.where(block_owner[None, :] == places[:, None], places[None, :], 0), axis=1
    )
    gradient = jnp.take(gathered, inverse, axis=1)
    lon_weights = weights_for(3.0)
    lev_weights = weights_for(2.0)
    lat_weights = weights_for(2.5)

    def lon_lev(field):
        smoothed_part = smooth_periodic(field.astype(jnp.float32), 2, lon_weights)
        return smooth_bounded(smoothed_part, 0, lev_weights)

    control = perturbations[:, 0].astype(jnp.float32) * gradient[0]
    control = control + perturbations[:, 1].astype(jnp.float32) * gradient[1]
    control = control.astype(jnp.bfloat16)
    start = jnp.zeros((slot_count, levels, rows_here, lon_count), jnp.float32)
    partial_field = lax.map(lon_lev, control)
    extended = extended_2(partial_field, (("lat", 2),), 4)

    def member_step(summed, pair):
        rows_ext, member = pair
        smoothed = lat_rows(rows_ext, lat_weights, rows_here)
        return (summed + member.astype(jnp.float32) * smoothed[None], None)

    increment_terms, unused = lax.scan(member_step, start, (extended, perturbations))
    ordered = jnp.take(increment_terms, block_owner, axis=1)
    return lax.psum_scatter(ordered, "mem", scatter_dimension=1, tiled=True)


def solution(mesh):
    placed = (P("mem", None, None, "lat", None), P(None, "mem", "lat", None), P())
    return jax.shard_map(
        local, mesh=mesh, in_specs=placed, out_specs=P(None, "mem", "lat", None), check_vma=False
    )
```

profile of v0, /device:TPU:1, one launch (start us, length us, event | category | flops | bytes accessed | tf_op | source)
XLA Modules:
  0.0 457.3 jit_solution(16722855853459697788)
XLA Ops:
  7.3 27.4 %all_gather.3 = f32[2,12,4,1440]{3,2,1,0:T(4,128)S(1)} all-gather(f32[2,2,4,1440]{3,2,1,0:T(4,128)} %param.10), channel_id=1, replica_groups=mesh['mem'=6,'lat'=128] {'mem'}, dimensions={1}, use_global_device_ids=true | all-gather | bytes 645120 | tf_op jit(solution)/shard_map/all_gather | solution.py:59
  35.9 3.5 fusion.33
  39.4 47.4 %while.23 = (s32[]{:T(128)}, f32[16,12,4,1440]{3,2,1,0:T(4,128)}, bf16[16,12,4,1440]{3,2,1,0:T(4,128)(2,1)S(1)}, s32[]{:T(128)}) while((s32[]{:T(128)}, f32[16,12,4,1440]{3,2,1,0:T(4,128)}, bf16[16,12,4,1440]{3,2,1,0:T(4,128)(2,1)S(1)}, s32[]{:T(128)}) %tuple.69), condition=%wide.region_2.4_spmd, body=%wide.region_1.3_spmd.sunk | while | flops 2903042 | bytes 8036925 | solution.py:78
  50.3 0.9 bitcast_dynamic-update-slice_fusion.2
  53.3 1.0 bitcast_dynamic-update-slice_fusion.2
  56.3 1.0 bitcast_dynamic-update-slice_fusion.2
  85.9 0.9 bitcast_dynamic-update-slice_fusion.2
  86.8 5.2 %collective-permute-start = (f32[16,12,4,1440]{3,2,1,0:T(4,128)}, f32[16,12,4,1440]{3,2,1,0:T(4,128)}, u32[]{:S(2)}, u32[]{:S(2)}) collective-permute-start(f32[16,12,4,1440]{3,2,1,0:T(4,128)} %get-tuple-element.69), channel_id=1, source_target_pairs={{0,1},{1,2},{2,3},{3,4},{4,5},{5,6},{6,7},{7,8},{8,9},{9,10},{10,1... | collective-permute-start | bytes 13271048 | tf_op jit(solution)/shard_map/ppermute | solution.py:14
  92.0 1.3 collective-permute-start.1
  93.4 97.8 %collective-permute-done = f32[16,12,4,1440]{3,2,1,0:T(4,128)} collective-permute-done((f32[16,12,4,1440]{3,2,1,0:T(4,128)}, f32[16,12,4,1440]{3,2,1,0:T(4,128)}, u32[]{:S(2)}, u32[]{:S(2)}) %collective-permute-start) | collective-permute-done | bytes 4423712 | tf_op jit(solution)/shard_map/ppermute | solution.py:14
  191.2 106.6 %collective-permute-done.1 = f32[16,12,4,1440]{3,2,1,0:T(4,128)} collective-permute-done((f32[16,12,4,1440]{3,2,1,0:T(4,128)}, f32[16,12,4,1440]{3,2,1,0:T(4,128)}, u32[]{:S(2)}, u32[]{:S(2)}) %collective-permute-start.1) | collective-permute-done | bytes 4423712 | tf_op jit(solution)/shard_map/ppermute | solution.py:17
  297.8 12.2 %pad_maximum_fusion = f32[16,12,12,1440]{3,2,1,0:T(8,128)} fusion(f32[16,12,4,1440]{3,2,1,0:T(4,128)} %collective-permute-done.1, f32[16,12,4,1440]{3,2,1,0:T(4,128)} %get-tuple-element.69, f32[16,12,4,1440]{3,2,1,0:T(4,128)} %collective-permute-done), kind=kLoop, calls=%fused_computation.63 | loop fusion | flops 6635520 | bytes 26542080 | tf_op jit(solution)/shard_map/concatenate | solution.py:18
  309.9 54.4 %while.24 = (s32[]{:T(128)}, f32[2,12,4,1440]{3,2,1,0:T(4,128)S(1)}, bf16[16,2,12,4,1440]{4,3,2,1,0:T(4,128)(2,1)}, f32[16,12,12,1440]{3,2,1,0:T(8,128)}, s32[]{:T(128)}, /*index=5*/s32[]{:T(128)}) while((s32[]{:T(128)}, f32[2,12,4,1440]{3,2,1,0:T(4,128)S(1)}, bf16[16,2,12,4,1440]{4,3,2,1,0:T(4,128)(2,1)}, ...), condition=%wide.region_4.6_spmd.clone, body=%wide.region_3.5_spmd.clone.sunk | while | flops 1658883 | bytes 6082647 | solution.py:86
  309.9 1.3 dynamic-slice_bitcast_fusion.2
  311.9 1.4 fusion.63
  313.3 1.4 dynamic-slice_bitcast_fusion.2
  315.3 1.4 fusion.63
  316.7 1.4 dynamic-slice_bitcast_fusion.2
  318.7 1.4 fusion.63
  320.1 1.4 dynamic-slice_bitcast_fusion.2
  322.1 1.4 fusion.63
  323.5 1.4 dynamic-slice_bitcast_fusion.2
  325.5 1.4 fusion.63
  326.9 1.4 dynamic-slice_bitcast_fusion.2
  328.9 1.4 fusion.63
  330.3 1.4 dynamic-slice_bitcast_fusion.2
  332.3 1.4 fusion.63
  333.7 1.4 dynamic-slice_bitcast_fusion.2
  335.7 1.4 fusion.63
  337.2 1.4 dynamic-slice_bitcast_fusion.2
  339.1 1.4 fusion.63
  340.6 1.4 dynamic-slice_bitcast_fusion.2
  342.5 1.4 fusion.63
  344.0 1.4 dynamic-slice_bitcast_fusion.2
  345.9 1.4 fusion.63
  347.4 1.4 dynamic-slice_bitcast_fusion.2
  349.3 1.4 fusion.63
  350.8 1.4 dynamic-slice_bitcast_fusion.2
  352.7 1.4 fusion.63
  354.2 1.4 dynamic-slice_bitcast_fusion.2
  356.1 1.4 fusion.63
  357.6 1.4 dynamic-slice_bitcast_fusion.2
  359.5 1.4 fusion.63
  361.0 1.4 dynamic-slice_bitcast_fusion.2
  362.9 1.4 fusion.63
  365.3 1.0 select_bitcast_fusion
  366.3 1.3 dynamic-slice
  368.3 80.6 %all-reduce.4.cloned.1.call-done = f32[2,12,4,1440]{3,2,0,1:T(4,128)} async-done(((f32[2,12,4,1440]{3,2,0,1:T(4,128)}), f32[2,12,4,1440]{3,2,0,1:T(4,128)}) %all-reduce.4.cloned.1.call-update) | async-done | bytes 552976
  (207 shorter events, 57.0 us)
Async XLA Ops:
  6.5 442.4 %all-reduce.4.cloned.1.call-start = ((), (), s32[]{:S(2)}) async-start(), calls=%async_computation | async-start | bytes 1179648
  39.4 53.9 %copy-start = (s32[12]{0:T(128)S(1)}, s32[12]{0:T(128)}, u32[]{:S(2)}) copy-start(s32[12]{0:T(128)} %param.11) | copy-start | bytes 148
  86.8 104.4 %collective-permute-start = (f32[16,12,4,1440]{3,2,1,0:T(4,128)}, f32[16,12,4,1440]{3,2,1,0:T(4,128)}, u32[]{:S(2)}, u32[]{:S(2)}) collective-permute-start(f32[16,12,4,1440]{3,2,1,0:T(4,128)} %get-tuple-element.69), channel_id=1, source_target_pairs={{0,1},{1,2},{2,3},{3,4},{4,5},{5,6},{6,7},{7,8},{8,9},{9,10},{10,1... | collective-permute-start | bytes 13271048 | tf_op jit(solution)/shard_map/ppermute | solution.py:14
  92.0 205.7 %collective-permute-start.1 = (f32[16,12,4,1440]{3,2,1,0:T(4,128)}, f32[16,12,4,1440]{3,2,1,0:T(4,128)}, u32[]{:S(2)}, u32[]{:S(2)}) collective-permute-start(f32[16,12,4,1440]{3,2,1,0:T(4,128)} %get-tuple-element.69), channel_id=1, source_target_pairs={{1,0},{2,1},{3,2},{4,3},{5,4},{6,5},{7,6},{8,7},{9,8},{10,9},{11,1... | collective-permute-start | bytes 13271048 | tf_op jit(solution)/shard_map/ppermute | solution.py:17
Sparse Core Ops, SparseCore 0:
  366.5 82.3 all-reduce.3
where the time goes:
time: 459 us; the launch traced here: 457 us
  waiting for transfers between devices  285 us (62%)
  other arithmetic  77.9 us (17%)
  local copies, waits for them, and re-layouts  45.6 us (10%)
  blocking collectives  27.4 us (6%)
  between operations  14.2 us (3%)
  starting transfers between devices  6.51 us (1%)
    ppermute x1, waiting for transfers between devices, extended_2(): lax.ppermute(lax.slice_in_dim(block, 0, width, axis=dim), axis, backward)  107 us
    ppermute x1, waiting for transfers between devices, extended_2(): lax.ppermute(lax.slice_in_dim(block, block.shape[dim] - width, None, axis...  97.8 us
    unnamed x2, waiting for transfers between devices  80.6 us
    all_gather x1, blocking collectives, local(): gathered = lax.all_gather(gradient_held, 'mem', axis=1, tiled=True)  27.4 us
    add x16, other arithmetic, member_step(): return (summed + member.astype(jnp.float32) * smoothed[None], None)  23.1 us
    squeeze x16, local copies, waits for them, and re-layouts, local(): lax.scan(member_step, start, (extended, perturbations))  21.6 us
    slice x128, local copies, waits for them, and re-layouts, smooth_periodic(): jnp.roll(source, -offset, axis=along_dim)  19.3 us
    dynamic_update_slice x16, other arithmetic, local(): partial_field = lax.map(lon_lev, control)  15 us
  transfers between devices with their start and end apart: 3, of which 3 were waited for; matrix products, arithmetic and copies ran while one was open for 0% of the time, Pallas kernels for 0%

commit v1 on v0

v1 whole, which is shorter than its diff:
```python
import functools
import math

import jax
import jax.numpy as jnp
from jax import lax
from jax.experimental import pallas as pl
from jax.experimental.pallas import tpu as pltpu
from jax.sharding import PartitionSpec as P

LANES = 128
VMEM_LIMIT = 24 * 1024 * 1024
COST = pl.CostEstimate(flops=1000, bytes_accessed=1000, transcendentals=0)


def weights_for(spread_cells):
    return [
        math.exp(-(offset * offset) / (2.0 * spread_cells * spread_cells))
        for offset in range(-4, 5)
    ]


LON_W = weights_for(3.0)
LEV_W = weights_for(2.0)
LAT_W = weights_for(2.5)


def prepare_kernel(levels_ref, pert_ref, grad_ref, *refs):
    turned_ref, packed_ref = refs[-2:]
    slots, rows, lon = grad_ref.shape[1], grad_ref.shape[3], grad_ref.shape[4]
    full = lon // LANES
    for slot in range(slots):
        turned = jnp.transpose(pert_ref[:, slot, 0].astype(jnp.float32), (1, 0, 2))
        turned_ref[0, :, slot] = turned.astype(jnp.bfloat16)
    tails = []
    for row in range(rows):
        for tile in range(full + 1):
            lanes = slice(tile * LANES, min((tile + 1) * LANES, lon))
            value = None
            for slot in range(slots):
                term = (
                    turned_ref[0, row, slot, :, lanes].astype(jnp.float32)
                    * grad_ref[0, slot, 0, row : row + 1, lanes]
                )
                value = term if value is None else value + term
            if tile < full:
                packed_ref[0, row * full + tile] = value.astype(jnp.bfloat16)
            else:
                tails.append(value)
    packed_ref[0, rows * full] = jnp.concatenate(tails, axis=1).astype(jnp.bfloat16)


def prepare(first, size, levels, perturbations, gradient, turned=None, limit=VMEM_LIMIT):
    members, slots, count, rows, lon = perturbations.shape
    entries = rows * (lon // LANES) + 1
    inputs = [perturbations, gradient]
    in_specs = [
        pl.BlockSpec(
            (members, slots, 1, rows, lon), lambda i, lev: (0, 0, lev[i], 0, 0)
        ),
        pl.BlockSpec((1, slots, 1, rows, lon), lambda i, lev: (i // 2, 0, i % 2, 0, 0)),
    ]
    aliases = {}
    if turned is not None:
        inputs.append(turned)
        in_specs.append(pl.BlockSpec(memory_space=pl.ANY))
        aliases = {3: 0}
    return pl.pallas_call(
        prepare_kernel,
        out_shape=(
            jax.ShapeDtypeStruct((count, rows, slots, members, lon), jnp.bfloat16),
            jax.ShapeDtypeStruct((size, entries, members, LANES), jnp.bfloat16),
        ),
        grid_spec=pltpu.PrefetchScalarGridSpec(
            num_scalar_prefetch=1,
            grid=(size,),
            in_specs=in_specs,
            out_specs=(
                pl.BlockSpec(
                    (1, rows, slots, members, lon),
                    lambda i, lev: (2 * first + i, 0, 0, 0, 0),
                ),
                pl.BlockSpec((1, entries, members, LANES), lambda i, lev: (i, 0, 0, 0)),
            ),
        ),
        input_output_aliases=aliases,
        name="prepare",
        cost_estimate=COST,
        compiler_params=pltpu.CompilerParams(vmem_limit_bytes=limit),
    )(levels, *inputs)


def smooth_level(refs, out_ref, level, wide_ref, rows, lon):
    full, rest = lon // LANES, lon % LANES
    members = refs[0].shape[2]
    for tile in range(full + 1):
        if tile < full:
            source = [
                ref[0, row * full + tile].astype(jnp.float32) for ref in refs for row in range(rows)
            ]
        else:
            tails = [ref[0, rows * full].astype(jnp.float32) for ref in refs]
            source = [
                tail if row == 0 else pltpu.roll(tail, LANES - row * rest, 1)
                for tail in tails
                for row in range(rows)
            ]
        for row in range(rows):
            total = LAT_W[4] * source[row + 4]
            for step in range(1, 5):
                total = total + LAT_W[4 + step] * (source[row + 4 - step] + source[row + 4 + step])
            wide_ref[row, :, tile * LANES : (tile + 1) * LANES] = total
    half = 8
    lane = lax.broadcasted_iota(jnp.int32, (half, LANES), 1)
    for row in range(rows):
        for part in range(members // half):
            some = slice(part * half, (part + 1) * half)
            tiles = [
                wide_ref[row, some, tile * LANES : (tile + 1) * LANES] for tile in range(full + 1)
            ]
            before = pltpu.roll(tiles[full], LANES - rest, 1)
            tiles[full] = jnp.where(lane < rest, tiles[full], pltpu.roll(tiles[0], rest, 1))
            tiles = [before] + tiles
            totals = [LON_W[4] * tile for tile in tiles[1:]]
            for step in range(1, 5):
                right = [pltpu.roll(tile, step, 1) for tile in tiles]
                left = [pltpu.roll(tile, LANES - step, 1) for tile in tiles[1:]]
                left.append(left[-1])
                for tile in range(full + 1):
                    both = jnp.where(lane < step, right[tile], right[tile + 1]) + jnp.where(
                        lane < LANES - step, left[tile], left[tile + 1]
                    )
                    totals[tile] = totals[tile] + LON_W[4 + step] * both
            for tile in range(full + 1):
                out_ref[level, row, some, tile * LANES : (tile + 1) * LANES] = totals[tile]


def sums_of(arrays, sub):
    for width in (1, 2, 4):
        low = (sub & width) == 0
        arrays = [
            jnp.where(low, even, odd) + pltpu.roll(jnp.where(low, odd, even), width, 0)
            for even, odd in zip(arrays[::2], arrays[1::2])
        ]
    return arrays[0]


def collect_pair(pair, first, fields_ref, weight_ref, pert_ref, before_ref, out_ref, lon):
    size, rows, members, _ = fields_ref.shape
    full = lon // LANES
    slots = out_ref.shape[0]
    weights = [
        [weight_ref[2 * pair + i, 2 * first + source] for source in range(size)]
        for i in range(2)
    ]
    for tile in range(full + 1):
        lanes = slice(tile * LANES, min((tile + 1) * LANES, lon))
        across = min((tile + 1) * LANES, lon) - tile * LANES
        sub = lax.broadcasted_iota(jnp.int32, (8, across), 0)
        products = [[[None] * rows for _ in range(slots)] for _ in range(2)]
        for row in range(rows):
            values = [fields_ref[source, row, :, lanes] for source in range(size)]
            for i in range(2):
                total = weights[i][0] * values[0]
                for source in range(1, size):
                    total = total + weights[i][source] * values[source]
                for slot in range(slots):
                    product = total * pert_ref[i, row, slot, :, lanes].astype(jnp.float32)
                    product = product.reshape(members // 8, 8, across)
                    part = product[0]
                    for other in range(1, members // 8):
                        part = part + product[other]
                    products[i][slot][row] = part
        for i in range(2):
            value = sums_of(products[i][0] + products[i][1], sub)
            for slot in range(slots):
                piece = value[slot * rows : (slot + 1) * rows]
                if before_ref is not None:
                    piece = piece + before_ref[slot, i, :, lanes]
                out_ref[slot, i, :, lanes] = piece


def collect_kernel(weight_ref, low_ref, own_ref, high_ref, pert_ref, *refs, first, lon):
    theirs_ref, ours_ref, fields_ref, wide_ref = refs[-4:]
    theirs_before, ours_before = refs[:2] if len(refs) > 4 else (None, None)
    size, rows = fields_ref.shape[:2]
    step = pl.program_id(0)
    half = (pl.num_programs(0) - size) // 2

    @pl.when(step < size)
    def _():
        smooth_level((low_ref, own_ref, high_ref), fields_ref, step, wide_ref, rows, lon)

    @pl.when((step >= size) & (step < size + half))
    def _():
        pair = step - size + half
        collect_pair(
            pair, first, fields_ref, weight_ref, pert_ref, theirs_before, theirs_ref, lon
        )

    @pl.when(step >= size + half)
    def _():
        pair = step - size - half
        collect_pair(pair, first, fields_ref, weight_ref, pert_ref, ours_before, ours_ref, lon)


def collect(first, weights, low, own, high, turned, before):
    count, rows, slots, members, lon = turned.shape
    size, entries = own.shape[:2]
    pairs = count // 2
    half = pairs // 2
    width = (lon // LANES + 1) * LANES
    level = pl.BlockSpec(
        (1, entries, members, LANES), lambda i, w: (jnp.minimum(i, size - 1), 0, 0, 0)
    )
    theirs = pl.BlockSpec(
        (slots, 2, rows, lon), lambda i, w: (0, jnp.clip(i - size, 0, half - 1), 0, 0)
    )
    ours = pl.BlockSpec(
        (slots, 2, rows, lon), lambda i, w: (0, jnp.clip(i - size - half, 0, half - 1), 0, 0)
    )
    pert = pl.BlockSpec(
        (2, rows, slots, members, lon),
        lambda i, w: ((jnp.maximum(i - size, 0) + half) % pairs, 0, 0, 0, 0),
    )
    result = jax.ShapeDtypeStruct((slots, count // 2, rows, lon), jnp.float32)
    return pl.pallas_call(
        functools.partial(collect_kernel, first=first, lon=lon),
        out_shape=(result, result),
        grid_spec=pltpu.PrefetchScalarGridSpec(
            num_scalar_prefetch=1,
            grid=(size + pairs,),
            in_specs=[level] * 3 + [pert] + ([] if before is None else [theirs, ours]),
            out_specs=(theirs, ours),
            scratch_shapes=[
                pltpu.VMEM((size, rows, members, width), jnp.float32),
                pltpu.VMEM((rows, members, width), jnp.float32),
            ],
        ),
        name="collect",
        cost_estimate=COST,
        compiler_params=pltpu.CompilerParams(vmem_limit_bytes=VMEM_LIMIT),
    )(weights, low, own, high, turned, *(() if before is None else before))


def local(perturbations, gradient_held, block_owner):
    members, slots, levels, rows, lon = perturbations.shape
    across = lax.axis_size("mem") // 2
    place = lax.axis_index("mem")
    high, core = place // 2, place % 2

    swap = [(2 * z + c, 2 * z + 1 - c) for z in range(across) for c in range(2)]
    down = [(2 * ((z + 1) % across) + c, 2 * z + c) for z in range(across) for c in range(2)]
    up = [(2 * z + c, 2 * ((z + 1) % across) + c) for z in range(across) for c in range(2)]
    count = lax.axis_size("lat")
    forward = [(i, i + 1) for i in range(count - 1)]
    backward = [(i + 1, i) for i in range(count - 1)]

    index = jnp.arange(levels, dtype=jnp.int32)
    pair = index // 2
    shift = jnp.where(pair % 3 == 0, 0, jnp.where(pair % 3 == 1, 1, across - 1))
    flip = jnp.where(pair >= 3, 1 - core, core)
    positions = 2 * (2 * ((high + shift) % across) + flip) + index % 2
    order = jnp.sum(
        jnp.where(
            positions[:, None] == index[None, :], block_owner.astype(jnp.int32)[None, :], 0
        ),
        axis=1,
    ).astype(jnp.int32)
    apart = jnp.abs(order[:, None] - order[None, :])
    weights = jnp.zeros((levels, levels), jnp.float32)
    for step in range(5):
        weights = jnp.where(apart == step, LEV_W[4 + step], weights)

    def halos(control, after=None):
        lower, upper = control, control
        if after is not None:
            lower, _ = lax.optimization_barrier((control, after[0]))
            upper, _ = lax.optimization_barrier((control, after[1]))
        return lax.ppermute(lower, "lat", forward), lax.ppermute(upper, "lat", backward)

    held = lax.dynamic_slice_in_dim(block_owner.astype(jnp.int32), 2 * place, 2)
    turned, own = prepare(
        0, 2, held, perturbations, gradient_held[None], limit=57 * 1024 * 1024
    )
    own_low, own_high = halos(own)
    near = [
        lax.ppermute(gradient_held, "mem", down),
        lax.ppermute(gradient_held, "mem", up),
        lax.ppermute(gradient_held, "mem", swap),
    ]
    near = jnp.stack(near)
    far = lax.ppermute(near, "mem", swap)
    turned, mid = prepare(1, 6, order[2:8], perturbations, near, turned)
    mid_low, mid_high = halos(mid, (own_low, own_high))
    turned, last = prepare(4, 4, order[8:], perturbations, far, turned)
    last_low, last_high = halos(last)

    sums = collect(0, weights, own_low, own, own_high, turned, None)
    sums = collect(1, weights, mid_low, mid, mid_high, turned, sums)
    theirs, ours = collect(4, weights, last_low, last, last_high, turned, sums)
    kept = ours + lax.ppermute(theirs, "mem", swap)
    from_below = lax.ppermute(kept[:, 2:4].astype(jnp.bfloat16), "mem", up)
    from_above = lax.ppermute(kept[:, 4:6].astype(jnp.bfloat16), "mem", down)
    return kept[:, :2] + from_below.astype(jnp.float32) + from_above.astype(jnp.float32)


def solution(mesh):
    placed = (P("mem", None, None, "lat", None), P(None, "mem", "lat", None), P())
    return jax.shard_map(
        local, mesh=mesh, in_specs=placed, out_specs=P(None, "mem", "lat", None), check_vma=False
    )
```

time: 459 us -> 162 us (0.35)
  the two profiles are of different devices: /device:TPU:1 before, /device:TPU:31 now
where the time goes in v1:
time: 162 us
  starting transfers between devices  58.9 us (36%)
  waiting for transfers between devices  54.4 us (34%)
  Pallas kernels  36.5 us (23%)
  local copies, waits for them, and re-layouts  10.6 us (7%)
    ppermute x3, waiting for transfers between devices, halos(): lax.ppermute(upper, 'lat', backward)  43.9 us
    pallas_call x3, Pallas kernels, collect(): pl.pallas_call(functools.partial(collect_kernel, first=first, lon=lon), o...  28.7 us
    ppermute x3, starting transfers between devices, halos(): lax.ppermute(upper, 'lat', backward)  17.2 us
    ppermute x1, starting transfers between devices, local(): lax.ppermute(gradient_held, 'mem', down)  14.4 us
    unnamed x12, local copies, waits for them, and re-layouts  9.13 us
    ppermute x1, waiting for transfers between devices, local(): from_above = lax.ppermute(kept[:, 4:6].astype(jnp.bfloat16), 'mem', down)  8.15 us
    ppermute x3, starting transfers between devices, halos(): lax.ppermute(lower, 'lat', forward)  7.85 us
    pallas_call x3, Pallas kernels, prepare(): pl.pallas_call(prepare_kernel, out_shape=(jax.ShapeDtypeStruct((count, ro...  7.75 us
  transfers between devices with their start and end apart: 13, of which 6 were waited for; matrix products, arithmetic and copies ran while one was open for 1% of the time, Pallas kernels for 17%

profile of v1, /device:TPU:31, one launch (start us, length us, event | category | flops | bytes accessed | tf_op | source)
XLA Modules:
  0.0 161.7 jit_solution(13834777833393584155)
XLA Ops:
  0.0 14.4 %collective-permute-start = (f32[2,2,4,1440]{3,2,1,0:T(4,128)}, f32[2,2,4,1440]{3,2,1,0:T(4,128)S(1)}, u32[]{:S(2)}, u32[]{:S(2)}) collective-permute-start(f32[2,2,4,1440]{3,2,1,0:T(4,128)} %param.4), channel_id=1, source_target_pairs={{256,0},{384,128},{512,256},{640,384},{0,512},{128,640},{257,1},{3... | collective-permute-start | bytes 276488 | tf_op jit(solution)/shard_map/ppermute | solution.py:288
  14.4 1.9 %collective-permute-start.1 = (f32[2,2,4,1440]{3,2,1,0:T(4,128)}, f32[2,2,4,1440]{3,2,1,0:T(4,128)S(1)}, u32[]{:S(2)}, u32[]{:S(2)}) collective-permute-start(f32[2,2,4,1440]{3,2,1,0:T(4,128)} %param.4), channel_id=1, source_target_pairs={{0,256},{128,384},{256,512},{384,640},{512,0},{640,128},{1,257},{1... | collective-permute-start | bytes 276488 | tf_op jit(solution)/shard_map/ppermute | solution.py:289
  16.3 2.9 %collective-permute-start.2 = (f32[2,2,4,1440]{3,2,1,0:T(4,128)}, f32[2,2,4,1440]{3,2,1,0:T(4,128)S(1)}, u32[]{:S(2)}, u32[]{:S(2)}) collective-permute-start(f32[2,2,4,1440]{3,2,1,0:T(4,128)} %param.4), channel_id=1, source_target_pairs={{0,128},{128,0},{256,384},{384,256},{512,640},{640,512},{1,129},{1... | collective-permute-start | bytes 276488 | tf_op jit(solution)/shard_map/ppermute | solution.py:290
  19.2 1.2 dynamic_slice.3.levels_ref
  20.5 3.0 %prepare.3 = (bf16[12,4,2,16,1440]{4,3,2,1,0:T(8,128)(2,1)}, bf16[2,45,16,128]{3,2,1,0:T(8,128)(2,1)}) custom-call(s32[2]{0:T(128)} %dynamic_slice.3.levels_ref, bf16[16,2,12,4,1440]{4,3,2,1,0:T(4,128)(2,1)} %pert_ref.5, f32[1,2,2,4,1440]{4,3,2,1,0:T(4,128)} %bitcast.7), custom_call_target="tpu_custom_call" | custom-call | flops 1000 | bytes 1000 | tf_op jit(solution)/shard_map/prepare/pallas_call | solution.py:68
  23.5 3.1 %collective-permute-start.6 = (bf16[2,45,16,128]{3,2,1,0:T(8,128)(2,1)}, bf16[2,45,16,128]{3,2,1,0:T(8,128)(2,1)S(1)}, u32[]{:S(2)}, u32[]{:S(2)}) collective-permute-start(bf16[2,45,16,128]{3,2,1,0:T(8,128)(2,1)} %get-tuple-element.24.own_ref), channel_id=1, source_target_pairs={{0,1},{1,2},{2,3},{3,4},{4,5},{5,6},{6,7},{7,8},{8,9},{9,10},{10,1... | collective-permute-start | bytes 1105928 | tf_op jit(solution)/shard_map/ppermute | solution.py:280
  26.6 4.9 %collective-permute-start.8 = (bf16[2,45,16,128]{3,2,1,0:T(8,128)(2,1)}, bf16[2,45,16,128]{3,2,1,0:T(8,128)(2,1)S(1)}, u32[]{:S(2)}, u32[]{:S(2)}) collective-permute-start(bf16[2,45,16,128]{3,2,1,0:T(8,128)(2,1)} %get-tuple-element.24.own_ref), channel_id=1, source_target_pairs={{1,0},{2,1},{3,2},{4,3},{5,4},{6,5},{7,6},{8,7},{9,8},{10,9},{11,1... | collective-permute-start | bytes 1105928 | tf_op jit(solution)/shard_map/ppermute | solution.py:280
  31.5 0.0 copy-done.5
  31.5 0.2 select_reduce_fusion
  31.7 0.1 slice.18.levels_ref
  31.8 0.0 collective-permute-done
  31.8 0.0 collective-permute-done.1
  31.8 0.0 collective-permute-done.2
  31.8 0.1 pad_maximum_fusion.grad_ref
  31.9 0.0 copy-start
  31.9 2.3 %copy-done = bf16[12,4,2,16,1440]{4,3,2,1,0:T(8,128)(2,1)S(1)} copy-done((bf16[12,4,2,16,1440]{4,3,2,1,0:T(8,128)(2,1)S(1)}, bf16[12,4,2,16,1440]{4,3,2,1,0:T(8,128)(2,1)}, u32[]{:S(2)}) %copy-start) | copy-done | bytes 4423704
  34.2 2.3 %copy-done.3 = bf16[16,2,12,4,1440]{4,3,2,1,0:T(4,128)(2,1)S(1)} copy-done((bf16[16,2,12,4,1440]{4,3,2,1,0:T(4,128)(2,1)S(1)}, bf16[16,2,12,4,1440]{4,3,2,1,0:T(4,128)(2,1)}, u32[]{:S(2)}) %copy-start.3) | copy-done | bytes 4423704
  36.6 2.7 %prepare.4 = (bf16[12,4,2,16,1440]{4,3,2,1,0:T(8,128)(2,1)S(1)}, bf16[6,45,16,128]{3,2,1,0:T(8,128)(2,1)S(1)}) custom-call(s32[6]{0:T(128)S(1)} %slice.18.levels_ref, bf16[16,2,12,4,1440]{4,3,2,1,0:T(4,128)(2,1)S(1)} %copy-done.3, f32[3,2,2,4,1440]{4,3,2,1,0:T(4,128)S(1)} %pad_maximum_fusion.grad_ref, ...), custom_call_target="tpu_custom_call", output_to_operand_aliasing={{0}: (3, {})} | custom-call | flops 1000 | bytes 1000 | tf_op jit(solution)/shard_map/prepare/pallas_call | solution.py:68
  39.3 0.0 collective-permute-done.6.low_ref
  39.3 2.9 %collective-permute-start.7 = (bf16[6,45,16,128]{3,2,1,0:T(8,128)(2,1)S(1)}, bf16[6,45,16,128]{3,2,1,0:T(8,128)(2,1)S(1)}, u32[]{:S(2)}, u32[]{:S(2)}) collective-permute-start(bf16[6,45,16,128]{3,2,1,0:T(8,128)(2,1)S(1)} %get-tuple-element.26.own_ref), channel_id=1, source_target_pairs={{0,1},{1,2},{2,3},{3,4},{4,5},{5,6},{6,7},{7,8},{8,9},{9,10},{10,1... | collective-permute-start | bytes 3317768 | tf_op jit(solution)/shard_map/ppermute | solution.py:280
  42.2 4.3 %collective-permute-done.8.high_ref = bf16[2,45,16,128]{3,2,1,0:T(8,128)(2,1)S(1)} collective-permute-done((bf16[2,45,16,128]{3,2,1,0:T(8,128)(2,1)}, bf16[2,45,16,128]{3,2,1,0:T(8,128)(2,1)S(1)}, u32[]{:S(2)}, u32[]{:S(2)}) %collective-permute-start.8) | collective-permute-done | bytes 368672 | tf_op jit(solution)/shard_map/ppermute | solution.py:280
  46.5 6.3 %collective-permute-start.9 = (bf16[6,45,16,128]{3,2,1,0:T(8,128)(2,1)S(1)}, bf16[6,45,16,128]{3,2,1,0:T(8,128)(2,1)S(1)}, u32[]{:S(2)}, u32[]{:S(2)}) collective-permute-start(bf16[6,45,16,128]{3,2,1,0:T(8,128)(2,1)S(1)} %get-tuple-element.26.own_ref), channel_id=1, source_target_pairs={{1,0},{2,1},{3,2},{4,3},{5,4},{6,5},{7,6},{8,7},{9,8},{10,9},{11,1... | collective-permute-start | bytes 3317768 | tf_op jit(solution)/shard_map/ppermute | solution.py:280
  52.8 2.7 %collective-permute-start.3 = (f32[3,2,2,4,1440]{4,3,2,1,0:T(4,128)S(1)}, f32[3,2,2,4,1440]{4,3,2,1,0:T(4,128)S(1)}, u32[]{:S(2)}, u32[]{:S(2)}) collective-permute-start(f32[3,2,2,4,1440]{4,3,2,1,0:T(4,128)S(1)} %pad_maximum_fusion.grad_ref), channel_id=1, source_target_pairs={{0,128},{128,0},{256,384},{384,256},{512,640},{640,512},{1,129},{1... | collective-permute-start | bytes 829448 | tf_op jit(solution)/shard_map/ppermute | solution.py:293
  55.5 0.1 slice.17.levels_ref
  55.6 1.1 collective-permute-done.3.grad_ref
  56.7 2.0 %prepare.5 = (bf16[12,4,2,16,1440]{4,3,2,1,0:T(8,128)(2,1)S(1)}, bf16[4,45,16,128]{3,2,1,0:T(8,128)(2,1)S(1)}) custom-call(s32[4]{0:T(128)S(1)} %slice.17.levels_ref, bf16[16,2,12,4,1440]{4,3,2,1,0:T(4,128)(2,1)S(1)} %copy-done.3, f32[3,2,2,4,1440]{4,3,2,1,0:T(4,128)S(1)} %collective-permute-done.3.grad_ref, ...), custom_call_target="tpu_custom_call", output_to_operand_aliasing={{0}: (3, {})} | custom-call | flops 1000 | bytes 1000 | tf_op jit(solution)/shard_map/prepare/pallas_call | solution.py:68
  58.7 0.0 copy-start.1
  58.8 2.1 %copy-done.1 = bf16[12,4,2,16,1440]{4,3,2,1,0:T(8,128)(2,1)} copy-done((bf16[12,4,2,16,1440]{4,3,2,1,0:T(8,128)(2,1)}, bf16[12,4,2,16,1440]{4,3,2,1,0:T(8,128)(2,1)S(1)}, u32[]{:S(2)}) %copy-start.1) | copy-done | bytes 4423704
  60.9 1.9 %collective-permute-start.4 = (bf16[4,45,16,128]{3,2,1,0:T(8,128)(2,1)S(1)}, bf16[4,45,16,128]{3,2,1,0:T(8,128)(2,1)S(1)}, u32[]{:S(2)}, u32[]{:S(2)}) collective-permute-start(bf16[4,45,16,128]{3,2,1,0:T(8,128)(2,1)S(1)} %get-tuple-element.21.own_ref), channel_id=1, source_target_pairs={{0,1},{1,2},{2,3},{3,4},{4,5},{5,6},{6,7},{7,8},{8,9},{9,10},{10,1... | collective-permute-start | bytes 2211848 | tf_op jit(solution)/shard_map/ppermute | solution.py:280
  62.8 6.1 %collective-permute-start.5 = (bf16[4,45,16,128]{3,2,1,0:T(8,128)(2,1)S(1)}, bf16[4,45,16,128]{3,2,1,0:T(8,128)(2,1)S(1)}, u32[]{:S(2)}, u32[]{:S(2)}) collective-permute-start(bf16[4,45,16,128]{3,2,1,0:T(8,128)(2,1)S(1)} %get-tuple-element.21.own_ref), channel_id=1, source_target_pairs={{1,0},{2,1},{3,2},{4,3},{5,4},{6,5},{7,6},{8,7},{9,8},{10,9},{11,1... | collective-permute-start | bytes 2211848 | tf_op jit(solution)/shard_map/ppermute | solution.py:280
  68.9 0.1 select_select_fusion.weight_ref
  68.9 0.0 copy-done.4
  69.0 2.3 %copy-done.2 = bf16[12,4,2,16,1440]{4,3,2,1,0:T(8,128)(2,1)S(1)} copy-done((bf16[12,4,2,16,1440]{4,3,2,1,0:T(8,128)(2,1)S(1)}, bf16[12,4,2,16,1440]{4,3,2,1,0:T(8,128)(2,1)}, u32[]{:S(2)}) %copy-start.2) | copy-done | bytes 4423704
  71.3 5.8 %collect.3 = (f32[2,6,4,1440]{3,2,1,0:T(4,128)S(1)}, f32[2,6,4,1440]{3,2,1,0:T(4,128)S(1)}) custom-call(f32[12,12]{1,0:T(8,128)S(1)} %select_select_fusion.weight_ref, bf16[2,45,16,128]{3,2,1,0:T(8,128)(2,1)S(1)} %collective-permute-done.6.low_ref, bf16[2,45,16,128]{3,2,1,0:T(8,128)(2,1)S(1)} %copy-done.4, ...), custom_call_target="tpu_custom_call" | custom-call | flops 1000 | bytes 1000 | tf_op jit(solution)/shard_map/collect/pallas_call | solution.py:227
  77.1 0.0 collective-permute-done.7.low_ref
  77.1 22.2 %collective-permute-done.9.high_ref = bf16[6,45,16,128]{3,2,1,0:T(8,128)(2,1)S(1)} collective-permute-done((bf16[6,45,16,128]{3,2,1,0:T(8,128)(2,1)S(1)}, bf16[6,45,16,128]{3,2,1,0:T(8,128)(2,1)S(1)}, u32[]{:S(2)}, u32[]{:S(2)}) %collective-permute-start.9) | collective-permute-done | bytes 1105952 | tf_op jit(solution)/shard_map/ppermute | solution.py:280
  99.3 13.3 %collect.4 = (f32[2,6,4,1440]{3,2,1,0:T(4,128)S(1)}, f32[2,6,4,1440]{3,2,1,0:T(4,128)S(1)}) custom-call(f32[12,12]{1,0:T(8,128)S(1)} %select_select_fusion.weight_ref, bf16[6,45,16,128]{3,2,1,0:T(8,128)(2,1)S(1)} %collective-permute-done.7.low_ref, bf16[6,45,16,128]{3,2,1,0:T(8,128)(2,1)S(1)} %get-tuple-element.26.own_ref, ...), custom_call_target="tpu_custom_call" | custom-call | flops 1000 | bytes 1000 | tf_op jit(solution)/shard_map/collect/pallas_call | solution.py:227
  112.7 0.0 collective-permute-done.4.low_ref
  112.7 17.3 %collective-permute-done.5.high_ref = bf16[4,45,16,128]{3,2,1,0:T(8,128)(2,1)S(1)} collective-permute-done((bf16[4,45,16,128]{3,2,1,0:T(8,128)(2,1)S(1)}, bf16[4,45,16,128]{3,2,1,0:T(8,128)(2,1)S(1)}, u32[]{:S(2)}, u32[]{:S(2)}) %collective-permute-start.5) | collective-permute-done | bytes 737312 | tf_op jit(solution)/shard_map/ppermute | solution.py:280
  130.1 9.5 %collect.5 = (f32[2,6,4,1440]{3,2,1,0:T(4,128)S(1)}, f32[2,6,4,1440]{3,2,1,0:T(4,128)S(1)}) custom-call(f32[12,12]{1,0:T(8,128)S(1)} %select_select_fusion.weight_ref, bf16[4,45,16,128]{3,2,1,0:T(8,128)(2,1)S(1)} %collective-permute-done.4.low_ref, bf16[4,45,16,128]{3,2,1,0:T(8,128)(2,1)S(1)} %get-tuple-element.21.own_ref, ...), custom_call_target="tpu_custom_call" | custom-call | flops 1000 | bytes 1000 | tf_op jit(solution)/shard_map/collect/pallas_call | solution.py:227
  139.6 2.4 %collective-permute-start.10 = (f32[2,6,4,1440]{3,2,1,0:T(4,128)S(1)}, f32[2,6,4,1440]{3,2,1,0:T(4,128)S(1)}, u32[]{:S(2)}, u32[]{:S(2)}) collective-permute-start(f32[2,6,4,1440]{3,2,1,0:T(4,128)S(1)} %get-tuple-element.32), channel_id=1, source_target_pairs={{0,128},{128,0},{256,384},{384,256},{512,640},{640,512},{1,129},{1... | collective-permute-start | bytes 829448 | tf_op jit(solution)/shard_map/ppermute | solution.py:302
  142.0 1.2 collective-permute-done.10
  143.2 0.1 fusion.11
  143.3 5.0 %collective-permute-start.11 = (bf16[2,2,4,1440]{3,2,1,0:T(4,128)(2,1)S(1)}, bf16[2,2,4,1440]{3,2,1,0:T(4,128)(2,1)S(1)}, u32[]{:S(2)}, u32[]{:S(2)}) collective-permute-start(bf16[2,2,4,1440]{3,2,1,0:T(4,128)(2,1)S(1)} %get-tuple-element.35), channel_id=1, source_target_pairs={{0,256},{128,384},{256,512},{384,640},{512,0},{640,128},{1,257},{1... | collective-permute-start | bytes 138248 | tf_op jit(solution)/shard_map/ppermute | solution.py:303
  148.4 4.5 %collective-permute-start.12 = (bf16[2,2,4,1440]{3,2,1,0:T(4,128)(2,1)S(1)}, bf16[2,2,4,1440]{3,2,1,0:T(4,128)(2,1)S(1)}, u32[]{:S(2)}, u32[]{:S(2)}) collective-permute-start(bf16[2,2,4,1440]{3,2,1,0:T(4,128)(2,1)S(1)} %get-tuple-element.36), channel_id=1, source_target_pairs={{256,0},{384,128},{512,256},{640,384},{0,512},{128,640},{257,1},{3... | collective-permute-start | bytes 138248 | tf_op jit(solution)/shard_map/ppermute | solution.py:304
  152.8 0.0 collective-permute-done.11
  152.8 8.2 %collective-permute-done.12 = bf16[2,2,4,1440]{3,2,1,0:T(4,128)(2,1)S(1)} collective-permute-done((bf16[2,2,4,1440]{3,2,1,0:T(4,128)(2,1)S(1)}, bf16[2,2,4,1440]{3,2,1,0:T(4,128)(2,1)S(1)}, u32[]{:S(2)}, u32[]{:S(2)}) %collective-permute-start.12) | collective-permute-done | bytes 46112 | tf_op jit(solution)/shard_map/ppermute | solution.py:304
  161.0 0.7 fusion
  (6 shorter events, 0.1 us)
Async XLA Ops:
  0.0 31.5 %copy-start.5 = (s32[12]{0:T(128)S(1)}, s32[12]{0:T(128)}, u32[]{:S(2)}) copy-start(s32[12]{0:T(128)} %param.5) | copy-start | bytes 148
  0.0 31.8 %collective-permute-start = (f32[2,2,4,1440]{3,2,1,0:T(4,128)}, f32[2,2,4,1440]{3,2,1,0:T(4,128)S(1)}, u32[]{:S(2)}, u32[]{:S(2)}) collective-permute-start(f32[2,2,4,1440]{3,2,1,0:T(4,128)} %param.4), channel_id=1, source_target_pairs={{256,0},{384,128},{512,256},{640,384},{0,512},{128,640},{257,1},{3... | collective-permute-start | bytes 276488 | tf_op jit(solution)/shard_map/ppermute | solution.py:288
  14.4 17.4 %collective-permute-start.1 = (f32[2,2,4,1440]{3,2,1,0:T(4,128)}, f32[2,2,4,1440]{3,2,1,0:T(4,128)S(1)}, u32[]{:S(2)}, u32[]{:S(2)}) collective-permute-start(f32[2,2,4,1440]{3,2,1,0:T(4,128)} %param.4), channel_id=1, source_target_pairs={{0,256},{128,384},{256,512},{384,640},{512,0},{640,128},{1,257},{1... | collective-permute-start | bytes 276488 | tf_op jit(solution)/shard_map/ppermute | solution.py:289
  16.3 15.5 %collective-permute-start.2 = (f32[2,2,4,1440]{3,2,1,0:T(4,128)}, f32[2,2,4,1440]{3,2,1,0:T(4,128)S(1)}, u32[]{:S(2)}, u32[]{:S(2)}) collective-permute-start(f32[2,2,4,1440]{3,2,1,0:T(4,128)} %param.4), channel_id=1, source_target_pairs={{0,128},{128,0},{256,384},{384,256},{512,640},{640,512},{1,129},{1... | collective-permute-start | bytes 276488 | tf_op jit(solution)/shard_map/ppermute | solution.py:290
  23.5 15.8 %collective-permute-start.6 = (bf16[2,45,16,128]{3,2,1,0:T(8,128)(2,1)}, bf16[2,45,16,128]{3,2,1,0:T(8,128)(2,1)S(1)}, u32[]{:S(2)}, u32[]{:S(2)}) collective-permute-start(bf16[2,45,16,128]{3,2,1,0:T(8,128)(2,1)} %get-tuple-element.24.own_ref), channel_id=1, source_target_pairs={{0,1},{1,2},{2,3},{3,4},{4,5},{5,6},{6,7},{7,8},{8,9},{9,10},{10,1... | collective-permute-start | bytes 1105928 | tf_op jit(solution)/shard_map/ppermute | solution.py:280
  26.6 19.9 %collective-permute-start.8 = (bf16[2,45,16,128]{3,2,1,0:T(8,128)(2,1)}, bf16[2,45,16,128]{3,2,1,0:T(8,128)(2,1)S(1)}, u32[]{:S(2)}, u32[]{:S(2)}) collective-permute-start(bf16[2,45,16,128]{3,2,1,0:T(8,128)(2,1)} %get-tuple-element.24.own_ref), channel_id=1, source_target_pairs={{1,0},{2,1},{3,2},{4,3},{5,4},{6,5},{7,6},{8,7},{9,8},{10,9},{11,1... | collective-permute-start | bytes 1105928 | tf_op jit(solution)/shard_map/ppermute | solution.py:280
  31.9 2.3 %copy-start = (bf16[12,4,2,16,1440]{4,3,2,1,0:T(8,128)(2,1)S(1)}, bf16[12,4,2,16,1440]{4,3,2,1,0:T(8,128)(2,1)}, u32[]{:S(2)}) copy-start(bf16[12,4,2,16,1440]{4,3,2,1,0:T(8,128)(2,1)} %get-tuple-element.19.refs_0_) | copy-start | bytes 13271044
  34.2 2.3 %copy-start.3 = (bf16[16,2,12,4,1440]{4,3,2,1,0:T(4,128)(2,1)S(1)}, bf16[16,2,12,4,1440]{4,3,2,1,0:T(4,128)(2,1)}, u32[]{:S(2)}) copy-start(bf16[16,2,12,4,1440]{4,3,2,1,0:T(4,128)(2,1)} %pert_ref.5) | copy-start | bytes 13271044
  39.3 37.8 %collective-permute-start.7 = (bf16[6,45,16,128]{3,2,1,0:T(8,128)(2,1)S(1)}, bf16[6,45,16,128]{3,2,1,0:T(8,128)(2,1)S(1)}, u32[]{:S(2)}, u32[]{:S(2)}) collective-permute-start(bf16[6,45,16,128]{3,2,1,0:T(8,128)(2,1)S(1)} %get-tuple-element.26.own_ref), channel_id=1, source_target_pairs={{0,1},{1,2},{2,3},{3,4},{4,5},{5,6},{6,7},{7,8},{8,9},{9,10},{10,1... | collective-permute-start | bytes 3317768 | tf_op jit(solution)/shard_map/ppermute | solution.py:280
  46.5 52.8 %collective-permute-start.9 = (bf16[6,45,16,128]{3,2,1,0:T(8,128)(2,1)S(1)}, bf16[6,45,16,128]{3,2,1,0:T(8,128)(2,1)S(1)}, u32[]{:S(2)}, u32[]{:S(2)}) collective-permute-start(bf16[6,45,16,128]{3,2,1,0:T(8,128)(2,1)S(1)} %get-tuple-element.26.own_ref), channel_id=1, source_target_pairs={{1,0},{2,1},{3,2},{4,3},{5,4},{6,5},{7,6},{8,7},{9,8},{10,9},{11,1... | collective-permute-start | bytes 3317768 | tf_op jit(solution)/shard_map/ppermute | solution.py:280
  52.8 3.9 %collective-permute-start.3 = (f32[3,2,2,4,1440]{4,3,2,1,0:T(4,128)S(1)}, f32[3,2,2,4,1440]{4,3,2,1,0:T(4,128)S(1)}, u32[]{:S(2)}, u32[]{:S(2)}) collective-permute-start(f32[3,2,2,4,1440]{4,3,2,1,0:T(4,128)S(1)} %pad_maximum_fusion.grad_ref), channel_id=1, source_target_pairs={{0,128},{128,0},{256,384},{384,256},{512,640},{640,512},{1,129},{1... | collective-permute-start | bytes 829448 | tf_op jit(solution)/shard_map/ppermute | solution.py:293
  56.7 12.2 %copy-start.4 = (bf16[2,45,16,128]{3,2,1,0:T(8,128)(2,1)S(1)}, bf16[2,45,16,128]{3,2,1,0:T(8,128)(2,1)}, u32[]{:S(2)}) copy-start(bf16[2,45,16,128]{3,2,1,0:T(8,128)(2,1)} %get-tuple-element.24.own_ref) | copy-start | bytes 1105924
  58.7 2.1 %copy-start.1 = (bf16[12,4,2,16,1440]{4,3,2,1,0:T(8,128)(2,1)}, bf16[12,4,2,16,1440]{4,3,2,1,0:T(8,128)(2,1)S(1)}, u32[]{:S(2)}) copy-start(bf16[12,4,2,16,1440]{4,3,2,1,0:T(8,128)(2,1)S(1)} %get-tuple-element.22.pert_ref) | copy-start | bytes 13271044
  60.9 51.8 %collective-permute-start.4 = (bf16[4,45,16,128]{3,2,1,0:T(8,128)(2,1)S(1)}, bf16[4,45,16,128]{3,2,1,0:T(8,128)(2,1)S(1)}, u32[]{:S(2)}, u32[]{:S(2)}) collective-permute-start(bf16[4,45,16,128]{3,2,1,0:T(8,128)(2,1)S(1)} %get-tuple-element.21.own_ref), channel_id=1, source_target_pairs={{0,1},{1,2},{2,3},{3,4},{4,5},{5,6},{6,7},{7,8},{8,9},{9,10},{10,1... | collective-permute-start | bytes 2211848 | tf_op jit(solution)/shard_map/ppermute | solution.py:280
  62.8 67.3 %collective-permute-start.5 = (bf16[4,45,16,128]{3,2,1,0:T(8,128)(2,1)S(1)}, bf16[4,45,16,128]{3,2,1,0:T(8,128)(2,1)S(1)}, u32[]{:S(2)}, u32[]{:S(2)}) collective-permute-start(bf16[4,45,16,128]{3,2,1,0:T(8,128)(2,1)S(1)} %get-tuple-element.21.own_ref), channel_id=1, source_target_pairs={{1,0},{2,1},{3,2},{4,3},{5,4},{6,5},{7,6},{8,7},{9,8},{10,9},{11,1... | collective-permute-start | bytes 2211848 | tf_op jit(solution)/shard_map/ppermute | solution.py:280
  68.9 2.3 %copy-start.2 = (bf16[12,4,2,16,1440]{4,3,2,1,0:T(8,128)(2,1)S(1)}, bf16[12,4,2,16,1440]{4,3,2,1,0:T(8,128)(2,1)}, u32[]{:S(2)}) copy-start(bf16[12,4,2,16,1440]{4,3,2,1,0:T(8,128)(2,1)} %copy-done.1) | copy-start | bytes 13271044
  139.6 3.6 %collective-permute-start.10 = (f32[2,6,4,1440]{3,2,1,0:T(4,128)S(1)}, f32[2,6,4,1440]{3,2,1,0:T(4,128)S(1)}, u32[]{:S(2)}, u32[]{:S(2)}) collective-permute-start(f32[2,6,4,1440]{3,2,1,0:T(4,128)S(1)} %get-tuple-element.32), channel_id=1, source_target_pairs={{0,128},{128,0},{256,384},{384,256},{512,640},{640,512},{1,129},{1... | collective-permute-start | bytes 829448 | tf_op jit(solution)/shard_map/ppermute | solution.py:302
  143.3 9.5 %collective-permute-start.11 = (bf16[2,2,4,1440]{3,2,1,0:T(4,128)(2,1)S(1)}, bf16[2,2,4,1440]{3,2,1,0:T(4,128)(2,1)S(1)}, u32[]{:S(2)}, u32[]{:S(2)}) collective-permute-start(bf16[2,2,4,1440]{3,2,1,0:T(4,128)(2,1)S(1)} %get-tuple-element.35), channel_id=1, source_target_pairs={{0,256},{128,384},{256,512},{384,640},{512,0},{640,128},{1,257},{1... | collective-permute-start | bytes 138248 | tf_op jit(solution)/shard_map/ppermute | solution.py:303
  148.4 12.6 %collective-permute-start.12 = (bf16[2,2,4,1440]{3,2,1,0:T(4,128)(2,1)S(1)}, bf16[2,2,4,1440]{3,2,1,0:T(4,128)(2,1)S(1)}, u32[]{:S(2)}, u32[]{:S(2)}) collective-permute-start(bf16[2,2,4,1440]{3,2,1,0:T(4,128)(2,1)S(1)} %get-tuple-element.36), channel_id=1, source_target_pairs={{256,0},{384,128},{512,256},{640,384},{0,512},{128,640},{257,1},{3... | collective-permute-start | bytes 138248 | tf_op jit(solution)/shard_map/ppermute | solution.py:304

commit v2 on v1

--- a/solution.py
+++ b/solution.py
@@ -25,7 +25,7 @@
 LAT_W = weights_for(2.5)
 
 
-def prepare_kernel(levels_ref, pert_ref, grad_ref, *refs):
+def prepare_kernel(levels_ref, base_ref, pert_ref, grad_ref, *refs):
     turned_ref, packed_ref = refs[-2:]
     slots, rows, lon = grad_ref.shape[1], grad_ref.shape[3], grad_ref.shape[4]
     full = lon // LANES
@@ -50,21 +50,26 @@
     packed_ref[0, rows * full] = jnp.concatenate(tails, axis=1).astype(jnp.bfloat16)
 
 
-def prepare(first, size, levels, perturbations, gradient, turned=None, limit=VMEM_LIMIT):
+def prepare(
+    first, size, levels, base, perturbations, gradient, skip=0, turned=None
+):
     members, slots, count, rows, lon = perturbations.shape
     entries = rows * (lon // LANES) + 1
     inputs = [perturbations, gradient]
     in_specs = [
         pl.BlockSpec(
-            (members, slots, 1, rows, lon), lambda i, lev: (0, 0, lev[i], 0, 0)
-        ),
-        pl.BlockSpec((1, slots, 1, rows, lon), lambda i, lev: (i // 2, 0, i % 2, 0, 0)),
+            (members, slots, 1, rows, lon), lambda i, lev, b: (0, 0, lev[b[0] + i], 0, 0)
+        ),
+        pl.BlockSpec(
+            (1, slots, 1, rows, lon),
+            lambda i, lev, b: ((i + skip) // 2, 0, (i + skip) % 2, 0, 0),
+        ),
     ]
     aliases = {}
     if turned is not None:
         inputs.append(turned)
         in_specs.append(pl.BlockSpec(memory_space=pl.ANY))
-        aliases = {3: 0}
+        aliases = {4: 0}
     return pl.pallas_call(
         prepare_kernel,
         out_shape=(
@@ -72,22 +77,22 @@
             jax.ShapeDtypeStruct((size, entries, members, LANES), jnp.bfloat16),
         ),
         grid_spec=pltpu.PrefetchScalarGridSpec(
-            num_scalar_prefetch=1,
+            num_scalar_prefetch=2,
             grid=(size,),
             in_specs=in_specs,
             out_specs=(
                 pl.BlockSpec(
                     (1, rows, slots, members, lon),
-                    lambda i, lev: (2 * first + i, 0, 0, 0, 0),
+                    lambda i, lev, b: (first + i, 0, 0, 0, 0),
                 ),
-                pl.BlockSpec((1, entries, members, LANES), lambda i, lev: (i, 0, 0, 0)),
+                pl.BlockSpec((1, entries, members, LANES), lambda i, lev, b: (i, 0, 0, 0)),
             ),
         ),
         input_output_aliases=aliases,
         name="prepare",
         cost_estimate=COST,
-        compiler_params=pltpu.CompilerParams(vmem_limit_bytes=limit),
-    )(levels, *inputs)
+        compiler_params=pltpu.CompilerParams(vmem_limit_bytes=57 * 1024 * 1024),
+    )(levels, base, *inputs)
 
 
 def smooth_level(refs, out_ref, level, wide_ref, rows, lon):
@@ -150,7 +155,7 @@
     full = lon // LANES
     slots = out_ref.shape[0]
     weights = [
-        [weight_ref[2 * pair + i, 2 * first + source] for source in range(size)]
+        [weight_ref[2 * pair + i, first + source] for source in range(size)]
         for i in range(2)
     ]
     for tile in range(full + 1):
@@ -272,33 +277,44 @@
     for step in range(5):
         weights = jnp.where(apart == step, LEV_W[4 + step], weights)
 
-    def halos(control, after=None):
-        lower, upper = control, control
-        if after is not None:
-            lower, _ = lax.optimization_barrier((control, after[0]))
-            upper, _ = lax.optimization_barrier((control, after[1]))
-        return lax.ppermute(lower, "lat", forward), lax.ppermute(upper, "lat", backward)
-
-    held = lax.dynamic_slice_in_dim(block_owner.astype(jnp.int32), 2 * place, 2)
+    def halos(control):
+        return lax.ppermute(control, "lat", forward), lax.ppermute(control, "lat", backward)
+
     turned, own = prepare(
-        0, 2, held, perturbations, gradient_held[None], limit=57 * 1024 * 1024
+        0,
+        2,
+        block_owner.astype(jnp.int32),
+        (2 * place).astype(jnp.int32).reshape(1),
+        perturbations,
+        gradient_held[None],
     )
     own_low, own_high = halos(own)
-    near = [
-        lax.ppermute(gradient_held, "mem", down),
-        lax.ppermute(gradient_held, "mem", up),
-        lax.ppermute(gradient_held, "mem", swap),
-    ]
-    near = jnp.stack(near)
+    gradient_here, _ = lax.optimization_barrier((gradient_held, own))
+    above_held = lax.ppermute(gradient_here, "mem", down)
+    below_held = lax.ppermute(gradient_here, "mem", up)
+    other_held = lax.ppermute(gradient_here, "mem", swap)
+    above_held, below_held, other_held, own_low, own_high = lax.optimization_barrier(
+        (above_held, below_held, other_held, own_low, own_high)
+    )
+    near = jnp.stack([above_held, below_held, other_held])
     far = lax.ppermute(near, "mem", swap)
-    turned, mid = prepare(1, 6, order[2:8], perturbations, near, turned)
-    mid_low, mid_high = halos(mid, (own_low, own_high))
-    turned, last = prepare(4, 4, order[8:], perturbations, far, turned)
-    last_low, last_high = halos(last)
-
-    sums = collect(0, weights, own_low, own, own_high, turned, None)
-    sums = collect(1, weights, mid_low, mid, mid_high, turned, sums)
-    theirs, ours = collect(4, weights, last_low, last, last_high, turned, sums)
+
+    sums = None
+    groups = [(0, own, own_low, own_high)]
+    for first, size, gradient, skip in (
+        (2, 6, near, 0),
+        (8, 3, far, 0),
+        (11, 1, far, 3),
+    ):
+        start = jnp.full((1,), first, jnp.int32)
+        turned, control = prepare(
+            first, size, order, start, perturbations, gradient, skip, turned
+        )
+        low, upper = halos(control)
+        groups.append((first, control, low, upper))
+    for first, control, low, upper in groups:
+        sums = collect(first, weights, low, control, upper, turned, sums)
+    theirs, ours = sums
     kept = ours + lax.ppermute(theirs, "mem", swap)
     from_below = lax.ppermute(kept[:, 2:4].astype(jnp.bfloat16), "mem", up)
     from_above = lax.ppermute(kept[:, 4:6].astype(jnp.bfloat16), "mem", down)

time: 162 us -> 167 us (1.031)
  the two profiles are of different devices: /device:TPU:31 before, /device:TPU:32 now
where the time goes in v2:
time: 167 us
  starting transfers between devices  82 us (49%)
  Pallas kernels  47.7 us (29%)
  waiting for transfers between devices  31.1 us (19%)
  local copies, waits for them, and re-layouts  3.12 us (2%)
  other arithmetic  2.37 us (1%)
    ppermute x4, starting transfers between devices, halos(): lax.ppermute(control, 'lat', backward)  35.5 us
    pallas_call x4, Pallas kernels, collect(): pl.pallas_call(functools.partial(collect_kernel, first=first, lon=lon), o...  31.1 us
    pallas_call x4, Pallas kernels, prepare(): pl.pallas_call(prepare_kernel, out_shape=(jax.ShapeDtypeStruct((count, ro...  16.6 us
    ppermute x1, starting transfers between devices, local(): above_held = lax.ppermute(gradient_here, 'mem', down)  14.5 us
    ppermute x4, starting transfers between devices, halos(): lax.ppermute(control, 'lat', forward)  11.9 us
    ppermute x1, starting transfers between devices, local(): from_below = lax.ppermute(kept[:, 2:4].astype(jnp.bfloat16), 'mem', up)  10.4 us
    ppermute x1, waiting for transfers between devices, local(): from_above = lax.ppermute(kept[:, 4:6].astype(jnp.bfloat16), 'mem', down)  8.89 us
    ppermute x4, waiting for transfers between devices, halos(): lax.ppermute(control, 'lat', backward)  7.38 us
  transfers between devices with their start and end apart: 15, of which 9 were waited for; matrix products, arithmetic and copies ran while one was open for 0% of the time, Pallas kernels for 20%

profile of v2, /device:TPU:32, one launch (start us, length us, event | category | flops | bytes accessed | tf_op | source)
XLA Modules:
  0.0 166.6 jit_solution(3193705929069743074)
XLA Ops:
  0.0 3.2 %prepare.4 = (bf16[12,4,2,16,1440]{4,3,2,1,0:T(8,128)(2,1)}, bf16[2,45,16,128]{3,2,1,0:T(8,128)(2,1)}) custom-call(s32[12]{0:T(128)} %levels_ref.1, s32[1]{0:T(128)} %bitcast.base_ref, bf16[16,2,12,4,1440]{4,3,2,1,0:T(4,128)(2,1)} %pert_ref.7, f32[1,2,2,4,1440]{4,3,2,1,0:T(4,128)} %bitcast.8), custom_call_target="tpu_custom_call" | custom-call | flops 1000 | bytes 1000 | tf_op jit(solution)/shard_map/prepare/pallas_call | solution.py:73
  3.2 4.3 %collective-permute-start.3 = (bf16[2,45,16,128]{3,2,1,0:T(8,128)(2,1)}, bf16[2,45,16,128]{3,2,1,0:T(8,128)(2,1)S(1)}, u32[]{:S(2)}, u32[]{:S(2)}) collective-permute-start(bf16[2,45,16,128]{3,2,1,0:T(8,128)(2,1)} %get-tuple-element.27.own_ref), channel_id=1, source_target_pairs={{0,1},{1,2},{2,3},{3,4},{4,5},{5,6},{6,7},{7,8},{8,9},{9,10},{10,1... | collective-permute-start | bytes 1105928 | tf_op jit(solution)/shard_map/ppermute | solution.py:281
  7.5 7.6 %collective-permute-start.4 = (bf16[2,45,16,128]{3,2,1,0:T(8,128)(2,1)}, bf16[2,45,16,128]{3,2,1,0:T(8,128)(2,1)S(1)}, u32[]{:S(2)}, u32[]{:S(2)}) collective-permute-start(bf16[2,45,16,128]{3,2,1,0:T(8,128)(2,1)} %get-tuple-element.27.own_ref), channel_id=1, source_target_pairs={{1,0},{2,1},{3,2},{4,3},{5,4},{6,5},{7,6},{8,7},{9,8},{10,9},{11,1... | collective-permute-start | bytes 1105928 | tf_op jit(solution)/shard_map/ppermute | solution.py:281
  15.1 14.5 %collective-permute-start = (f32[2,2,4,1440]{3,2,1,0:T(4,128)S(1)}, f32[2,2,4,1440]{3,2,1,0:T(4,128)S(1)}, u32[]{:S(2)}, u32[]{:S(2)}) collective-permute-start(f32[2,2,4,1440]{3,2,1,0:T(4,128)S(1)} %copy-done.7), channel_id=1, source_target_pairs={{256,0},{384,128},{512,256},{640,384},{0,512},{128,640},{257,1},{3... | collective-permute-start | bytes 276488 | tf_op jit(solution)/shard_map/ppermute | solution.py:293
  29.7 1.9 %collective-permute-start.1 = (f32[2,2,4,1440]{3,2,1,0:T(4,128)S(1)}, f32[2,2,4,1440]{3,2,1,0:T(4,128)S(1)}, u32[]{:S(2)}, u32[]{:S(2)}) collective-permute-start(f32[2,2,4,1440]{3,2,1,0:T(4,128)S(1)} %copy-done.7), channel_id=1, source_target_pairs={{0,256},{128,384},{256,512},{384,640},{512,0},{640,128},{1,257},{1... | collective-permute-start | bytes 276488 | tf_op jit(solution)/shard_map/ppermute | solution.py:294
  31.6 1.9 %collective-permute-start.2 = (f32[2,2,4,1440]{3,2,1,0:T(4,128)S(1)}, f32[2,2,4,1440]{3,2,1,0:T(4,128)S(1)}, u32[]{:S(2)}, u32[]{:S(2)}) collective-permute-start(f32[2,2,4,1440]{3,2,1,0:T(4,128)S(1)} %copy-done.7), channel_id=1, source_target_pairs={{0,128},{128,0},{256,384},{384,256},{512,640},{640,512},{1,129},{1... | collective-permute-start | bytes 276488 | tf_op jit(solution)/shard_map/ppermute | solution.py:295
  33.6 0.0 copy-done.9
  33.6 0.7 select_reduce_fusion.levels_ref
  34.3 2.8 %collective-permute-done = f32[2,2,4,1440]{3,2,1,0:T(4,128)S(1)} collective-permute-done((f32[2,2,4,1440]{3,2,1,0:T(4,128)S(1)}, f32[2,2,4,1440]{3,2,1,0:T(4,128)S(1)}, u32[]{:S(2)}, u32[]{:S(2)}) %collective-permute-start) | collective-permute-done | bytes 92192 | tf_op jit(solution)/shard_map/ppermute | solution.py:293
  37.1 6.3 %collective-permute-done.1 = f32[2,2,4,1440]{3,2,1,0:T(4,128)S(1)} collective-permute-done((f32[2,2,4,1440]{3,2,1,0:T(4,128)S(1)}, f32[2,2,4,1440]{3,2,1,0:T(4,128)S(1)}, u32[]{:S(2)}, u32[]{:S(2)}) %collective-permute-start.1) | collective-permute-done | bytes 92192 | tf_op jit(solution)/shard_map/ppermute | solution.py:294
  43.4 0.0 collective-permute-done.2
  43.4 0.0 collective-permute-done.3.low_ref
  43.4 0.0 collective-permute-done.4.high_ref
  43.4 0.8 pad_maximum_fusion.grad_ref
  44.2 6.4 %prepare.5 = (bf16[12,4,2,16,1440]{4,3,2,1,0:T(8,128)(2,1)}, bf16[6,45,16,128]{3,2,1,0:T(8,128)(2,1)}) custom-call(s32[12]{0:T(128)} %select_reduce_fusion.levels_ref, s32[1]{0:T(128)} %constant.92.clone.1.base_ref, bf16[16,2,12,4,1440]{4,3,2,1,0:T(4,128)(2,1)} %pert_ref.7, ...), custom_call_target="tpu_custom_call", output_to_operand_aliasing={{0}: (4, {})} | custom-call | flops 1000 | bytes 1000 | tf_op jit(solution)/shard_map/prepare/pallas_call | solution.py:73
  50.6 3.9 %collective-permute-start.10 = (bf16[6,45,16,128]{3,2,1,0:T(8,128)(2,1)}, bf16[6,45,16,128]{3,2,1,0:T(8,128)(2,1)S(1)}, u32[]{:S(2)}, u32[]{:S(2)}) collective-permute-start(bf16[6,45,16,128]{3,2,1,0:T(8,128)(2,1)} %get-tuple-element.38.own_ref), channel_id=1, source_target_pairs={{0,1},{1,2},{2,3},{3,4},{4,5},{5,6},{6,7},{7,8},{8,9},{9,10},{10,1... | collective-permute-start | bytes 3317768 | tf_op jit(solution)/shard_map/ppermute | solution.py:281
  54.5 8.0 %collective-permute-start.11 = (bf16[6,45,16,128]{3,2,1,0:T(8,128)(2,1)}, bf16[6,45,16,128]{3,2,1,0:T(8,128)(2,1)S(1)}, u32[]{:S(2)}, u32[]{:S(2)}) collective-permute-start(bf16[6,45,16,128]{3,2,1,0:T(8,128)(2,1)} %get-tuple-element.38.own_ref), channel_id=1, source_target_pairs={{1,0},{2,1},{3,2},{4,3},{5,4},{6,5},{7,6},{8,7},{9,8},{10,9},{11,1... | collective-permute-start | bytes 3317768 | tf_op jit(solution)/shard_map/ppermute | solution.py:281
  62.5 1.9 %collective-permute-start.5 = (f32[3,2,2,4,1440]{4,3,2,1,0:T(4,128)S(1)}, f32[3,2,2,4,1440]{4,3,2,1,0:T(4,128)S(1)}, u32[]{:S(2)}, u32[]{:S(2)}) collective-permute-start(f32[3,2,2,4,1440]{4,3,2,1,0:T(4,128)S(1)} %copy-done.6), channel_id=1, source_target_pairs={{0,128},{128,0},{256,384},{384,256},{512,640},{640,512},{1,129},{1... | collective-permute-start | bytes 829448 | tf_op jit(solution)/shard_map/ppermute | solution.py:300
  64.4 1.5 collective-permute-done.5.grad_ref
  66.0 0.7 copy-done.5
  66.7 4.2 %prepare.6 = (bf16[12,4,2,16,1440]{4,3,2,1,0:T(8,128)(2,1)}, bf16[3,45,16,128]{3,2,1,0:T(8,128)(2,1)}) custom-call(s32[12]{0:T(128)} %select_reduce_fusion.levels_ref, s32[1]{0:T(128)} %constant.91.clone.1.base_ref, bf16[16,2,12,4,1440]{4,3,2,1,0:T(4,128)(2,1)} %pert_ref.7, f32[3,2,2,4,1440]{4,3,2,1,0:T(4,128)} %copy-done.5, ...), custom_call_target="tpu_custom_call", output_to_operand_aliasing={{0}: (4, {})} | custom-call | flops 1000 | bytes 1000 | tf_op jit(solution)/shard_map/prepare/pallas_call | solution.py:73
  70.8 1.9 %collective-permute-start.8 = (bf16[3,45,16,128]{3,2,1,0:T(8,128)(2,1)}, bf16[3,45,16,128]{3,2,1,0:T(8,128)(2,1)S(1)}, u32[]{:S(2)}, u32[]{:S(2)}) collective-permute-start(bf16[3,45,16,128]{3,2,1,0:T(8,128)(2,1)} %get-tuple-element.37.own_ref), channel_id=1, source_target_pairs={{0,1},{1,2},{2,3},{3,4},{4,5},{5,6},{6,7},{7,8},{8,9},{9,10},{10,1... | collective-permute-start | bytes 1658888 | tf_op jit(solution)/shard_map/ppermute | solution.py:281
  72.8 9.9 %collective-permute-start.9 = (bf16[3,45,16,128]{3,2,1,0:T(8,128)(2,1)}, bf16[3,45,16,128]{3,2,1,0:T(8,128)(2,1)S(1)}, u32[]{:S(2)}, u32[]{:S(2)}) collective-permute-start(bf16[3,45,16,128]{3,2,1,0:T(8,128)(2,1)} %get-tuple-element.37.own_ref), channel_id=1, source_target_pairs={{1,0},{2,1},{3,2},{4,3},{5,4},{6,5},{7,6},{8,7},{9,8},{10,9},{11,1... | collective-permute-start | bytes 1658888 | tf_op jit(solution)/shard_map/ppermute | solution.py:281
  82.7 0.0 copy-start.8
  82.7 2.9 %prepare.7 = (bf16[12,4,2,16,1440]{4,3,2,1,0:T(8,128)(2,1)}, bf16[1,45,16,128]{3,2,1,0:T(8,128)(2,1)}) custom-call(s32[12]{0:T(128)} %select_reduce_fusion.levels_ref, s32[1]{0:T(128)} %constant.90.clone.1.base_ref, bf16[16,2,12,4,1440]{4,3,2,1,0:T(4,128)(2,1)} %pert_ref.7, f32[3,2,2,4,1440]{4,3,2,1,0:T(4,128)} %copy-done.5, ...), custom_call_target="tpu_custom_call", output_to_operand_aliasing={{0}: (4, {})} | custom-call | flops 1000 | bytes 1000 | tf_op jit(solution)/shard_map/prepare/pallas_call | solution.py:73
  85.6 1.9 %collective-permute-start.6 = (bf16[1,45,16,128]{3,2,1,0:T(8,128)(2,1)}, bf16[1,45,16,128]{3,2,1,0:T(8,128)(2,1)S(1)}, u32[]{:S(2)}, u32[]{:S(2)}) collective-permute-start(bf16[1,45,16,128]{3,2,1,0:T(8,128)(2,1)} %get-tuple-element.35.own_ref), channel_id=1, source_target_pairs={{0,1},{1,2},{2,3},{3,4},{4,5},{5,6},{6,7},{7,8},{8,9},{9,10},{10,1... | collective-permute-start | bytes 552968 | tf_op jit(solution)/shard_map/ppermute | solution.py:281
  87.5 0.0 collective-permute-done.10.low_ref
  87.5 9.9 %collective-permute-start.7 = (bf16[1,45,16,128]{3,2,1,0:T(8,128)(2,1)}, bf16[1,45,16,128]{3,2,1,0:T(8,128)(2,1)S(1)}, u32[]{:S(2)}, u32[]{:S(2)}) collective-permute-start(bf16[1,45,16,128]{3,2,1,0:T(8,128)(2,1)} %get-tuple-element.35.own_ref), channel_id=1, source_target_pairs={{1,0},{2,1},{3,2},{4,3},{5,4},{6,5},{7,6},{8,7},{9,8},{10,9},{11,1... | collective-permute-start | bytes 552968 | tf_op jit(solution)/shard_map/ppermute | solution.py:281
  97.5 0.1 select_select_fusion.weight_ref
  97.6 0.0 copy-done.3
  97.6 2.3 %copy-done = bf16[12,4,2,16,1440]{4,3,2,1,0:T(8,128)(2,1)S(1)} copy-done((bf16[12,4,2,16,1440]{4,3,2,1,0:T(8,128)(2,1)S(1)}, bf16[12,4,2,16,1440]{4,3,2,1,0:T(8,128)(2,1)}, u32[]{:S(2)}) %copy-start) | copy-done | bytes 4423704
  99.9 5.8 %collect.4 = (f32[2,6,4,1440]{3,2,1,0:T(4,128)S(1)}, f32[2,6,4,1440]{3,2,1,0:T(4,128)S(1)}) custom-call(f32[12,12]{1,0:T(8,128)S(1)} %select_select_fusion.weight_ref, bf16[2,45,16,128]{3,2,1,0:T(8,128)(2,1)S(1)} %collective-permute-done.3.low_ref, bf16[2,45,16,128]{3,2,1,0:T(8,128)(2,1)S(1)} %copy-done.3, ...), custom_call_target="tpu_custom_call" | custom-call | flops 1000 | bytes 1000 | tf_op jit(solution)/shard_map/collect/pallas_call | solution.py:232
  105.7 0.3 collective-permute-done.11.high_ref
  106.0 13.3 %collect.5 = (f32[2,6,4,1440]{3,2,1,0:T(4,128)S(1)}, f32[2,6,4,1440]{3,2,1,0:T(4,128)S(1)}) custom-call(f32[12,12]{1,0:T(8,128)S(1)} %select_select_fusion.weight_ref, bf16[6,45,16,128]{3,2,1,0:T(8,128)(2,1)S(1)} %collective-permute-done.10.low_ref, bf16[6,45,16,128]{3,2,1,0:T(8,128)(2,1)S(1)} %copy-done.1, ...), custom_call_target="tpu_custom_call" | custom-call | flops 1000 | bytes 1000 | tf_op jit(solution)/shard_map/collect/pallas_call | solution.py:232
  119.3 2.4 %collective-permute-done.8.low_ref = bf16[3,45,16,128]{3,2,1,0:T(8,128)(2,1)S(1)} collective-permute-done((bf16[3,45,16,128]{3,2,1,0:T(8,128)(2,1)}, bf16[3,45,16,128]{3,2,1,0:T(8,128)(2,1)S(1)}, u32[]{:S(2)}, u32[]{:S(2)}) %collective-permute-start.8) | collective-permute-done | bytes 552992 | tf_op jit(solution)/shard_map/ppermute | solution.py:281
  121.7 7.1 %collective-permute-done.9.high_ref = bf16[3,45,16,128]{3,2,1,0:T(8,128)(2,1)S(1)} collective-permute-done((bf16[3,45,16,128]{3,2,1,0:T(8,128)(2,1)}, bf16[3,45,16,128]{3,2,1,0:T(8,128)(2,1)S(1)}, u32[]{:S(2)}, u32[]{:S(2)}) %collective-permute-start.9) | collective-permute-done | bytes 552992 | tf_op jit(solution)/shard_map/ppermute | solution.py:281
  128.8 7.8 %collect.6 = (f32[2,6,4,1440]{3,2,1,0:T(4,128)S(1)}, f32[2,6,4,1440]{3,2,1,0:T(4,128)S(1)}) custom-call(f32[12,12]{1,0:T(8,128)S(1)} %select_select_fusion.weight_ref, bf16[3,45,16,128]{3,2,1,0:T(8,128)(2,1)S(1)} %collective-permute-done.8.low_ref, bf16[3,45,16,128]{3,2,1,0:T(8,128)(2,1)S(1)} %copy-done.2, ...), custom_call_target="tpu_custom_call" | custom-call | flops 1000 | bytes 1000 | tf_op jit(solution)/shard_map/collect/pallas_call | solution.py:232
  136.6 0.3 collective-permute-done.6.low_ref
  136.8 0.0 collective-permute-done.7.high_ref
  136.8 4.2 %collect.7 = (f32[2,6,4,1440]{3,2,1,0:T(4,128)S(1)}, f32[2,6,4,1440]{3,2,1,0:T(4,128)S(1)}) custom-call(f32[12,12]{1,0:T(8,128)S(1)} %select_select_fusion.weight_ref, bf16[1,45,16,128]{3,2,1,0:T(8,128)(2,1)S(1)} %collective-permute-done.6.low_ref, bf16[1,45,16,128]{3,2,1,0:T(8,128)(2,1)S(1)} %copy-done.4, ...), custom_call_target="tpu_custom_call" | custom-call | flops 1000 | bytes 1000 | tf_op jit(solution)/shard_map/collect/pallas_call | solution.py:232
  141.0 1.9 %collective-permute-start.12 = (f32[2,6,4,1440]{3,2,1,0:T(4,128)S(1)}, f32[2,6,4,1440]{3,2,1,0:T(4,128)S(1)}, u32[]{:S(2)}, u32[]{:S(2)}) collective-permute-start(f32[2,6,4,1440]{3,2,1,0:T(4,128)S(1)} %get-tuple-element.48), channel_id=1, source_target_pairs={{0,128},{128,0},{256,384},{384,256},{512,640},{640,512},{1,129},{1... | collective-permute-start | bytes 829448 | tf_op jit(solution)/shard_map/ppermute | solution.py:318
  143.0 1.5 collective-permute-done.12
  144.5 0.1 fusion.11
  144.7 10.4 %collective-permute-start.13 = (bf16[2,2,4,1440]{3,2,1,0:T(4,128)(2,1)S(1)}, bf16[2,2,4,1440]{3,2,1,0:T(4,128)(2,1)S(1)}, u32[]{:S(2)}, u32[]{:S(2)}) collective-permute-start(bf16[2,2,4,1440]{3,2,1,0:T(4,128)(2,1)S(1)} %get-tuple-element.51), channel_id=1, source_target_pairs={{0,256},{128,384},{256,512},{384,640},{512,0},{640,128},{1,257},{1... | collective-permute-start | bytes 138248 | tf_op jit(solution)/shard_map/ppermute | solution.py:319
  155.1 1.9 %collective-permute-start.14 = (bf16[2,2,4,1440]{3,2,1,0:T(4,128)(2,1)S(1)}, bf16[2,2,4,1440]{3,2,1,0:T(4,128)(2,1)S(1)}, u32[]{:S(2)}, u32[]{:S(2)}) collective-permute-start(bf16[2,2,4,1440]{3,2,1,0:T(4,128)(2,1)S(1)} %get-tuple-element.52), channel_id=1, source_target_pairs={{256,0},{384,128},{512,256},{640,384},{0,512},{128,640},{257,1},{3... | collective-permute-start | bytes 138248 | tf_op jit(solution)/shard_map/ppermute | solution.py:320
  157.0 0.0 collective-permute-done.13
  157.0 8.9 %collective-permute-done.14 = bf16[2,2,4,1440]{3,2,1,0:T(4,128)(2,1)S(1)} collective-permute-done((bf16[2,2,4,1440]{3,2,1,0:T(4,128)(2,1)S(1)}, bf16[2,2,4,1440]{3,2,1,0:T(4,128)(2,1)S(1)}, u32[]{:S(2)}, u32[]{:S(2)}) %collective-permute-start.14) | collective-permute-done | bytes 46112 | tf_op jit(solution)/shard_map/ppermute | solution.py:320
  165.9 0.7 fusion
  (17 shorter events, 0.1 us)
Async XLA Ops:
  0.0 15.1 %copy-start.7 = (f32[2,2,4,1440]{3,2,1,0:T(4,128)S(1)}, f32[2,2,4,1440]{3,2,1,0:T(4,128)}, u32[]{:S(2)}) copy-start(f32[2,2,4,1440]{3,2,1,0:T(4,128)} %param.4) | copy-start | bytes 276484
  0.0 33.6 %copy-start.9 = (s32[12]{0:T(128)S(1)}, s32[12]{0:T(128)}, u32[]{:S(2)}) copy-start(s32[12]{0:T(128)} %levels_ref.1) | copy-start | bytes 148
  3.2 40.2 %collective-permute-start.3 = (bf16[2,45,16,128]{3,2,1,0:T(8,128)(2,1)}, bf16[2,45,16,128]{3,2,1,0:T(8,128)(2,1)S(1)}, u32[]{:S(2)}, u32[]{:S(2)}) collective-permute-start(bf16[2,45,16,128]{3,2,1,0:T(8,128)(2,1)} %get-tuple-element.27.own_ref), channel_id=1, source_target_pairs={{0,1},{1,2},{2,3},{3,4},{4,5},{5,6},{6,7},{7,8},{8,9},{9,10},{10,1... | collective-permute-start | bytes 1105928 | tf_op jit(solution)/shard_map/ppermute | solution.py:281
  7.5 35.9 %collective-permute-start.4 = (bf16[2,45,16,128]{3,2,1,0:T(8,128)(2,1)}, bf16[2,45,16,128]{3,2,1,0:T(8,128)(2,1)S(1)}, u32[]{:S(2)}, u32[]{:S(2)}) collective-permute-start(bf16[2,45,16,128]{3,2,1,0:T(8,128)(2,1)} %get-tuple-element.27.own_ref), channel_id=1, source_target_pairs={{1,0},{2,1},{3,2},{4,3},{5,4},{6,5},{7,6},{8,7},{9,8},{10,9},{11,1... | collective-permute-start | bytes 1105928 | tf_op jit(solution)/shard_map/ppermute | solution.py:281
  15.1 22.0 %collective-permute-start = (f32[2,2,4,1440]{3,2,1,0:T(4,128)S(1)}, f32[2,2,4,1440]{3,2,1,0:T(4,128)S(1)}, u32[]{:S(2)}, u32[]{:S(2)}) collective-permute-start(f32[2,2,4,1440]{3,2,1,0:T(4,128)S(1)} %copy-done.7), channel_id=1, source_target_pairs={{256,0},{384,128},{512,256},{640,384},{0,512},{128,640},{257,1},{3... | collective-permute-start | bytes 276488 | tf_op jit(solution)/shard_map/ppermute | solution.py:293
  29.7 13.7 %collective-permute-start.1 = (f32[2,2,4,1440]{3,2,1,0:T(4,128)S(1)}, f32[2,2,4,1440]{3,2,1,0:T(4,128)S(1)}, u32[]{:S(2)}, u32[]{:S(2)}) collective-permute-start(f32[2,2,4,1440]{3,2,1,0:T(4,128)S(1)} %copy-done.7), channel_id=1, source_target_pairs={{0,256},{128,384},{256,512},{384,640},{512,0},{640,128},{1,257},{1... | collective-permute-start | bytes 276488 | tf_op jit(solution)/shard_map/ppermute | solution.py:294
  31.6 11.8 %collective-permute-start.2 = (f32[2,2,4,1440]{3,2,1,0:T(4,128)S(1)}, f32[2,2,4,1440]{3,2,1,0:T(4,128)S(1)}, u32[]{:S(2)}, u32[]{:S(2)}) collective-permute-start(f32[2,2,4,1440]{3,2,1,0:T(4,128)S(1)} %copy-done.7), channel_id=1, source_target_pairs={{0,128},{128,0},{256,384},{384,256},{512,640},{640,512},{1,129},{1... | collective-permute-start | bytes 276488 | tf_op jit(solution)/shard_map/ppermute | solution.py:295
  44.2 18.3 %copy-start.6 = (f32[3,2,2,4,1440]{4,3,2,1,0:T(4,128)S(1)}, f32[3,2,2,4,1440]{4,3,2,1,0:T(4,128)}, u32[]{:S(2)}) copy-start(f32[3,2,2,4,1440]{4,3,2,1,0:T(4,128)} %pad_maximum_fusion.grad_ref) | copy-start | bytes 829444
  50.6 36.9 %collective-permute-start.10 = (bf16[6,45,16,128]{3,2,1,0:T(8,128)(2,1)}, bf16[6,45,16,128]{3,2,1,0:T(8,128)(2,1)S(1)}, u32[]{:S(2)}, u32[]{:S(2)}) collective-permute-start(bf16[6,45,16,128]{3,2,1,0:T(8,128)(2,1)} %get-tuple-element.38.own_ref), channel_id=1, source_target_pairs={{0,1},{1,2},{2,3},{3,4},{4,5},{5,6},{6,7},{7,8},{8,9},{9,10},{10,1... | collective-permute-start | bytes 3317768 | tf_op jit(solution)/shard_map/ppermute | solution.py:281
  54.5 51.5 %collective-permute-start.11 = (bf16[6,45,16,128]{3,2,1,0:T(8,128)(2,1)}, bf16[6,45,16,128]{3,2,1,0:T(8,128)(2,1)S(1)}, u32[]{:S(2)}, u32[]{:S(2)}) collective-permute-start(bf16[6,45,16,128]{3,2,1,0:T(8,128)(2,1)} %get-tuple-element.38.own_ref), channel_id=1, source_target_pairs={{1,0},{2,1},{3,2},{4,3},{5,4},{6,5},{7,6},{8,7},{9,8},{10,9},{11,1... | collective-permute-start | bytes 3317768 | tf_op jit(solution)/shard_map/ppermute | solution.py:281
  62.5 3.5 %collective-permute-start.5 = (f32[3,2,2,4,1440]{4,3,2,1,0:T(4,128)S(1)}, f32[3,2,2,4,1440]{4,3,2,1,0:T(4,128)S(1)}, u32[]{:S(2)}, u32[]{:S(2)}) collective-permute-start(f32[3,2,2,4,1440]{4,3,2,1,0:T(4,128)S(1)} %copy-done.6), channel_id=1, source_target_pairs={{0,128},{128,0},{256,384},{384,256},{512,640},{640,512},{1,129},{1... | collective-permute-start | bytes 829448 | tf_op jit(solution)/shard_map/ppermute | solution.py:300
  66.0 0.7 copy-start.5
  70.8 50.8 %collective-permute-start.8 = (bf16[3,45,16,128]{3,2,1,0:T(8,128)(2,1)}, bf16[3,45,16,128]{3,2,1,0:T(8,128)(2,1)S(1)}, u32[]{:S(2)}, u32[]{:S(2)}) collective-permute-start(bf16[3,45,16,128]{3,2,1,0:T(8,128)(2,1)} %get-tuple-element.37.own_ref), channel_id=1, source_target_pairs={{0,1},{1,2},{2,3},{3,4},{4,5},{5,6},{6,7},{7,8},{8,9},{9,10},{10,1... | collective-permute-start | bytes 1658888 | tf_op jit(solution)/shard_map/ppermute | solution.py:281
  72.8 56.0 %collective-permute-start.9 = (bf16[3,45,16,128]{3,2,1,0:T(8,128)(2,1)}, bf16[3,45,16,128]{3,2,1,0:T(8,128)(2,1)S(1)}, u32[]{:S(2)}, u32[]{:S(2)}) collective-permute-start(bf16[3,45,16,128]{3,2,1,0:T(8,128)(2,1)} %get-tuple-element.37.own_ref), channel_id=1, source_target_pairs={{1,0},{2,1},{3,2},{4,3},{5,4},{6,5},{7,6},{8,7},{9,8},{10,9},{11,1... | collective-permute-start | bytes 1658888 | tf_op jit(solution)/shard_map/ppermute | solution.py:281
  82.7 14.8 %copy-start.8 = (s32[12]{0:T(128)S(1)}, s32[12]{0:T(128)}, u32[]{:S(2)}) copy-start(s32[12]{0:T(128)} %select_reduce_fusion.levels_ref) | copy-start | bytes 148
  82.7 14.8 %copy-start.3 = (bf16[2,45,16,128]{3,2,1,0:T(8,128)(2,1)S(1)}, bf16[2,45,16,128]{3,2,1,0:T(8,128)(2,1)}, u32[]{:S(2)}) copy-start(bf16[2,45,16,128]{3,2,1,0:T(8,128)(2,1)} %get-tuple-element.27.own_ref) | copy-start | bytes 1105924
  82.7 23.2 %copy-start.1 = (bf16[6,45,16,128]{3,2,1,0:T(8,128)(2,1)S(1)}, bf16[6,45,16,128]{3,2,1,0:T(8,128)(2,1)}, u32[]{:S(2)}) copy-start(bf16[6,45,16,128]{3,2,1,0:T(8,128)(2,1)} %get-tuple-element.38.own_ref) | copy-start | bytes 3317764
  85.6 51.2 %collective-permute-start.6 = (bf16[1,45,16,128]{3,2,1,0:T(8,128)(2,1)}, bf16[1,45,16,128]{3,2,1,0:T(8,128)(2,1)S(1)}, u32[]{:S(2)}, u32[]{:S(2)}) collective-permute-start(bf16[1,45,16,128]{3,2,1,0:T(8,128)(2,1)} %get-tuple-element.35.own_ref), channel_id=1, source_target_pairs={{0,1},{1,2},{2,3},{3,4},{4,5},{5,6},{6,7},{7,8},{8,9},{9,10},{10,1... | collective-permute-start | bytes 552968 | tf_op jit(solution)/shard_map/ppermute | solution.py:281
  87.5 49.3 %collective-permute-start.7 = (bf16[1,45,16,128]{3,2,1,0:T(8,128)(2,1)}, bf16[1,45,16,128]{3,2,1,0:T(8,128)(2,1)S(1)}, u32[]{:S(2)}, u32[]{:S(2)}) collective-permute-start(bf16[1,45,16,128]{3,2,1,0:T(8,128)(2,1)} %get-tuple-element.35.own_ref), channel_id=1, source_target_pairs={{1,0},{2,1},{3,2},{4,3},{5,4},{6,5},{7,6},{8,7},{9,8},{10,9},{11,1... | collective-permute-start | bytes 552968 | tf_op jit(solution)/shard_map/ppermute | solution.py:281
  97.6 2.3 %copy-start = (bf16[12,4,2,16,1440]{4,3,2,1,0:T(8,128)(2,1)S(1)}, bf16[12,4,2,16,1440]{4,3,2,1,0:T(8,128)(2,1)}, u32[]{:S(2)}) copy-start(bf16[12,4,2,16,1440]{4,3,2,1,0:T(8,128)(2,1)} %get-tuple-element.36.pert_ref) | copy-start | bytes 13271044
  105.7 23.1 %copy-start.2 = (bf16[3,45,16,128]{3,2,1,0:T(8,128)(2,1)S(1)}, bf16[3,45,16,128]{3,2,1,0:T(8,128)(2,1)}, u32[]{:S(2)}) copy-start(bf16[3,45,16,128]{3,2,1,0:T(8,128)(2,1)} %get-tuple-element.37.own_ref) | copy-start | bytes 1658884
  119.3 17.5 %copy-start.4 = (bf16[1,45,16,128]{3,2,1,0:T(8,128)(2,1)S(1)}, bf16[1,45,16,128]{3,2,1,0:T(8,128)(2,1)}, u32[]{:S(2)}) copy-start(bf16[1,45,16,128]{3,2,1,0:T(8,128)(2,1)} %get-tuple-element.35.own_ref) | copy-start | bytes 552964
  141.0 3.5 %collective-permute-start.12 = (f32[2,6,4,1440]{3,2,1,0:T(4,128)S(1)}, f32[2,6,4,1440]{3,2,1,0:T(4,128)S(1)}, u32[]{:S(2)}, u32[]{:S(2)}) collective-permute-start(f32[2,6,4,1440]{3,2,1,0:T(4,128)S(1)} %get-tuple-element.48), channel_id=1, source_target_pairs={{0,128},{128,0},{256,384},{384,256},{512,640},{640,512},{1,129},{1... | collective-permute-start | bytes 829448 | tf_op jit(solution)/shard_map/ppermute | solution.py:318
  144.7 12.4 %collective-permute-start.13 = (bf16[2,2,4,1440]{3,2,1,0:T(4,128)(2,1)S(1)}, bf16[2,2,4,1440]{3,2,1,0:T(4,128)(2,1)S(1)}, u32[]{:S(2)}, u32[]{:S(2)}) collective-permute-start(bf16[2,2,4,1440]{3,2,1,0:T(4,128)(2,1)S(1)} %get-tuple-element.51), channel_id=1, source_target_pairs={{0,256},{128,384},{256,512},{384,640},{512,0},{640,128},{1,257},{1... | collective-permute-start | bytes 138248 | tf_op jit(solution)/shard_map/ppermute | solution.py:319
  155.1 10.8 %collective-permute-start.14 = (bf16[2,2,4,1440]{3,2,1,0:T(4,128)(2,1)S(1)}, bf16[2,2,4,1440]{3,2,1,0:T(4,128)(2,1)S(1)}, u32[]{:S(2)}, u32[]{:S(2)}) collective-permute-start(bf16[2,2,4,1440]{3,2,1,0:T(4,128)(2,1)S(1)} %get-tuple-element.52), channel_id=1, source_target_pairs={{256,0},{384,128},{512,256},{640,384},{0,512},{128,640},{257,1},{3... | collective-permute-start | bytes 138248 | tf_op jit(solution)/shard_map/ppermute | solution.py:320

commit v3 on v1

--- a/solution.py
+++ b/solution.py
@@ -10,6 +10,7 @@
 
 LANES = 128
 VMEM_LIMIT = 24 * 1024 * 1024
+WIDE_LIMIT = 57 * 1024 * 1024
 COST = pl.CostEstimate(flops=1000, bytes_accessed=1000, transcendentals=0)
 
 
@@ -25,13 +26,15 @@
 LAT_W = weights_for(2.5)
 
 
-def prepare_kernel(levels_ref, pert_ref, grad_ref, *refs):
-    turned_ref, packed_ref = refs[-2:]
+def turn_level(pert_ref, turned_ref):
+    for slot in range(pert_ref.shape[1]):
+        turned = jnp.transpose(pert_ref[:, slot, 0].astype(jnp.float32), (1, 0, 2))
+        turned_ref[0, :, slot] = turned.astype(jnp.bfloat16)
+
+
+def control_level(turned_ref, grad_ref, pair, level, packed_ref):
     slots, rows, lon = grad_ref.shape[1], grad_ref.shape[3], grad_ref.shape[4]
     full = lon // LANES
-    for slot in range(slots):
-        turned = jnp.transpose(pert_ref[:, slot, 0].astype(jnp.float32), (1, 0, 2))
-        turned_ref[0, :, slot] = turned.astype(jnp.bfloat16)
     tails = []
     for row in range(rows):
         for tile in range(full + 1):
@@ -40,7 +43,7 @@
             for slot in range(slots):
                 term = (
                     turned_ref[0, row, slot, :, lanes].astype(jnp.float32)
-                    * grad_ref[0, slot, 0, row : row + 1, lanes]
+                    * grad_ref[pair, slot, level, row : row + 1, lanes]
                 )
                 value = term if value is None else value + term
             if tile < full:
@@ -50,44 +53,99 @@
     packed_ref[0, rows * full] = jnp.concatenate(tails, axis=1).astype(jnp.bfloat16)
 
 
-def prepare(first, size, levels, perturbations, gradient, turned=None, limit=VMEM_LIMIT):
+def prepare_kernel(levels_ref, base_ref, pert_ref, grad_ref, turned_ref, packed_ref):
+    turn_level(pert_ref, turned_ref)
+    control_level(turned_ref, grad_ref, 0, pl.program_id(0), packed_ref)
+
+
+def prepare(levels, base, perturbations, gradient):
     members, slots, count, rows, lon = perturbations.shape
     entries = rows * (lon // LANES) + 1
-    inputs = [perturbations, gradient]
-    in_specs = [
-        pl.BlockSpec(
-            (members, slots, 1, rows, lon), lambda i, lev: (0, 0, lev[i], 0, 0)
-        ),
-        pl.BlockSpec((1, slots, 1, rows, lon), lambda i, lev: (i // 2, 0, i % 2, 0, 0)),
-    ]
-    aliases = {}
-    if turned is not None:
-        inputs.append(turned)
-        in_specs.append(pl.BlockSpec(memory_space=pl.ANY))
-        aliases = {3: 0}
     return pl.pallas_call(
         prepare_kernel,
         out_shape=(
             jax.ShapeDtypeStruct((count, rows, slots, members, lon), jnp.bfloat16),
-            jax.ShapeDtypeStruct((size, entries, members, LANES), jnp.bfloat16),
-        ),
+            jax.ShapeDtypeStruct((2, entries, members, LANES), jnp.bfloat16),
+        ),
+        grid_spec=pltpu.PrefetchScalarGridSpec(
+            num_scalar_prefetch=2,
+            grid=(2,),
+            in_specs=[
+                pl.BlockSpec(
+                    (members, slots, 1, rows, lon), lambda i, lev, b: (0, 0, lev[b[0] + i], 0, 0)
+                ),
+                pl.BlockSpec(gradient.shape, lambda i, lev, b: (0, 0, 0, 0, 0)),
+            ],
+            out_specs=(
+                pl.BlockSpec((1, rows, slots, members, lon), lambda i, lev, b: (i, 0, 0, 0, 0)),
+                pl.BlockSpec((1, entries, members, LANES), lambda i, lev, b: (i, 0, 0, 0)),
+            ),
+        ),
+        name="prepare",
+        cost_estimate=COST,
+        compiler_params=pltpu.CompilerParams(vmem_limit_bytes=WIDE_LIMIT),
+    )(levels, base, perturbations, gradient)
+
+
+def turn_kernel(levels_ref, pert_ref, turned_in_ref, turned_ref):
+    turn_level(pert_ref, turned_ref)
+
+
+def turn_rest(levels, perturbations, turned):
+    members, slots, count, rows, lon = perturbations.shape
+    return pl.pallas_call(
+        turn_kernel,
+        out_shape=jax.ShapeDtypeStruct(turned.shape, turned.dtype),
         grid_spec=pltpu.PrefetchScalarGridSpec(
             num_scalar_prefetch=1,
-            grid=(size,),
-            in_specs=in_specs,
-            out_specs=(
+            grid=(count - 2,),
+            in_specs=[
                 pl.BlockSpec(
-                    (1, rows, slots, members, lon),
-                    lambda i, lev: (2 * first + i, 0, 0, 0, 0),
+                    (members, slots, 1, rows, lon), lambda i, lev: (0, 0, lev[2 + i], 0, 0)
                 ),
-                pl.BlockSpec((1, entries, members, LANES), lambda i, lev: (i, 0, 0, 0)),
+                pl.BlockSpec(memory_space=pl.ANY),
+            ],
+            out_specs=pl.BlockSpec(
+                (1, rows, slots, members, lon), lambda i, lev: (2 + i, 0, 0, 0, 0)
             ),
         ),
-        input_output_aliases=aliases,
-        name="prepare",
+        input_output_aliases={2: 0},
+        name="turn",
         cost_estimate=COST,
-        compiler_params=pltpu.CompilerParams(vmem_limit_bytes=limit),
-    )(levels, *inputs)
+        compiler_params=pltpu.CompilerParams(vmem_limit_bytes=WIDE_LIMIT),
+    )(levels, perturbations, turned)
+
+
+def control_kernel(turned_ref, *refs):
+    packed_ref = refs[-1]
+    step = pl.program_id(0)
+    for pair, grad_ref in enumerate(refs[:-1]):
+
+        @pl.when(step // 2 == pair)
+        def _():
+            control_level(turned_ref, grad_ref, 0, step % 2, packed_ref)
+
+
+def control_of(first, turned, gradients):
+    count, rows, slots, members, lon = turned.shape
+    entries = rows * (lon // LANES) + 1
+    size = 2 * len(gradients)
+    return pl.pallas_call(
+        control_kernel,
+        out_shape=jax.ShapeDtypeStruct((size, entries, members, LANES), jnp.bfloat16),
+        grid=(size,),
+        in_specs=[
+            pl.BlockSpec((1, rows, slots, members, lon), lambda i: (first + i, 0, 0, 0, 0))
+        ]
+        + [
+            pl.BlockSpec((1,) + gradient.shape[1:], lambda i: (0, 0, 0, 0, 0))
+            for gradient in gradients
+        ],
+        out_specs=pl.BlockSpec((1, entries, members, LANES), lambda i: (i, 0, 0, 0)),
+        name="control",
+        cost_estimate=COST,
+        compiler_params=pltpu.CompilerParams(vmem_limit_bytes=56320 * 1024),
+    )(turned, *gradients)
 
 
 def smooth_level(refs, out_ref, level, wide_ref, rows, lon):
@@ -121,18 +179,34 @@
             before = pltpu.roll(tiles[full], LANES - rest, 1)
             tiles[full] = jnp.where(lane < rest, tiles[full], pltpu.roll(tiles[0], rest, 1))
             tiles = [before] + tiles
-            totals = [LON_W[4] * tile for tile in tiles[1:]]
-            for step in range(1, 5):
-                right = [pltpu.roll(tile, step, 1) for tile in tiles]
-                left = [pltpu.roll(tile, LANES - step, 1) for tile in tiles[1:]]
-                left.append(left[-1])
-                for tile in range(full + 1):
-                    both = jnp.where(lane < step, right[tile], right[tile + 1]) + jnp.where(
-                        lane < LANES - step, left[tile], left[tile + 1]
-                    )
-                    totals[tile] = totals[tile] + LON_W[4 + step] * both
+
+            def moved(arrays, step):
+                rolled = [pltpu.roll(array, -step % LANES, 1) for array in arrays]
+                if step > 0:
+                    return [
+                        jnp.where(lane < LANES - step, here, after)
+                        for here, after in zip(rolled, rolled[1:] + rolled[-1:])
+                    ]
+                return [
+                    jnp.where(lane < -step, former, here)
+                    for former, here in zip(rolled[:1] + rolled[:-1], rolled)
+                ]
+
+            last, following = moved(tiles, -1), moved(tiles, 1)
+            inner = [LON_W[1] * tile for tile in tiles]
+            lower = [
+                LON_W[0] * a + b + LON_W[2] * c for a, b, c in zip(last, inner, following)
+            ]
+            upper = [
+                LON_W[2] * a + b + LON_W[0] * c for a, b, c in zip(last, inner, following)
+            ]
+            lower, upper = moved(lower, -3), moved(upper, 3)
             for tile in range(full + 1):
-                out_ref[level, row, some, tile * LANES : (tile + 1) * LANES] = totals[tile]
+                k = tile + 1
+                total = LON_W[4] * tiles[k] + LON_W[3] * (last[k] + following[k])
+                out_ref[level, row, some, tile * LANES : (tile + 1) * LANES] = (
+                    total + lower[k] + upper[k]
+                )
 
 
 def sums_of(arrays, sub):
@@ -150,7 +224,7 @@
     full = lon // LANES
     slots = out_ref.shape[0]
     weights = [
-        [weight_ref[2 * pair + i, 2 * first + source] for source in range(size)]
+        [weight_ref[2 * pair + i, first + source] for source in range(size)]
         for i in range(2)
     ]
     for tile in range(full + 1):
@@ -165,7 +239,7 @@
                 for source in range(1, size):
                     total = total + weights[i][source] * values[source]
                 for slot in range(slots):
-                    product = total * pert_ref[i, row, slot, :, lanes].astype(jnp.float32)
+                    product = total * pert_ref[2 * pair + i, row, slot, :, lanes].astype(jnp.float32)
                     product = product.reshape(members // 8, 8, across)
                     part = product[0]
                     for other in range(1, members // 8):
@@ -219,10 +293,7 @@
     ours = pl.BlockSpec(
         (slots, 2, rows, lon), lambda i, w: (0, jnp.clip(i - size - half, 0, half - 1), 0, 0)
     )
-    pert = pl.BlockSpec(
-        (2, rows, slots, members, lon),
-        lambda i, w: ((jnp.maximum(i - size, 0) + half) % pairs, 0, 0, 0, 0),
-    )
+    pert = pl.BlockSpec(memory_space=pltpu.VMEM)
     result = jax.ShapeDtypeStruct((slots, count // 2, rows, lon), jnp.float32)
     return pl.pallas_call(
         functools.partial(collect_kernel, first=first, lon=lon),
@@ -272,33 +343,37 @@
     for step in range(5):
         weights = jnp.where(apart == step, LEV_W[4 + step], weights)
 
-    def halos(control, after=None):
-        lower, upper = control, control
-        if after is not None:
-            lower, _ = lax.optimization_barrier((control, after[0]))
-            upper, _ = lax.optimization_barrier((control, after[1]))
-        return lax.ppermute(lower, "lat", forward), lax.ppermute(upper, "lat", backward)
-
-    held = lax.dynamic_slice_in_dim(block_owner.astype(jnp.int32), 2 * place, 2)
+    def halos(control):
+        return lax.ppermute(control, "lat", forward), lax.ppermute(control, "lat", backward)
+
+    base = (2 * place).astype(jnp.int32).reshape(1)
     turned, own = prepare(
-        0, 2, held, perturbations, gradient_held[None], limit=57 * 1024 * 1024
+        block_owner.astype(jnp.int32), base, perturbations, gradient_held[None]
     )
     own_low, own_high = halos(own)
+    gradient_here, _ = lax.optimization_barrier((gradient_held, own))
     near = [
-        lax.ppermute(gradient_held, "mem", down),
-        lax.ppermute(gradient_held, "mem", up),
-        lax.ppermute(gradient_held, "mem", swap),
+        lax.ppermute(gradient_here, "mem", down),
+        lax.ppermute(gradient_here, "mem", up),
+        lax.ppermute(gradient_here, "mem", swap),
     ]
-    near = jnp.stack(near)
-    far = lax.ppermute(near, "mem", swap)
-    turned, mid = prepare(1, 6, order[2:8], perturbations, near, turned)
-    mid_low, mid_high = halos(mid, (own_low, own_high))
-    turned, last = prepare(4, 4, order[8:], perturbations, far, turned)
+    turned = turn_rest(order, perturbations, turned)
+    *near, own_low, own_high = lax.optimization_barrier((*near, own_low, own_high))
+    mid = control_of(2, turned, [gradient[None] for gradient in near])
+    mid_low, mid_high = halos(mid)
+    far = [lax.ppermute(gradient, "mem", swap) for gradient in near[:2]]
+    last = control_of(8, turned, [gradient[None] for gradient in far])
     last_low, last_high = halos(last)
 
-    sums = collect(0, weights, own_low, own, own_high, turned, None)
-    sums = collect(1, weights, mid_low, mid, mid_high, turned, sums)
-    theirs, ours = collect(4, weights, last_low, last, last_high, turned, sums)
+    sums = None
+    groups = (
+        (0, own, own_low, own_high),
+        (2, mid, mid_low, mid_high),
+        (8, last, last_low, last_high),
+    )
+    for first, control, low, upper in groups:
+        sums = collect(first, weights, low, control, upper, turned, sums)
+    theirs, ours = sums
     kept = ours + lax.ppermute(theirs, "mem", swap)
     from_below = lax.ppermute(kept[:, 2:4].astype(jnp.bfloat16), "mem", up)
     from_above = lax.ppermute(kept[:, 4:6].astype(jnp.bfloat16), "mem", down)

time: 162 us -> 166 us (1.025)
  the two profiles are of different devices: /device:TPU:31 before, /device:TPU:32 now
where the time goes in v3:
time: 166 us; the launch traced here: 165 us
  starting transfers between devices  64.4 us (39%)
  waiting for transfers between devices  49.8 us (30%)
  Pallas kernels  47.9 us (29%)
    ppermute x3, waiting for transfers between devices, halos(): lax.ppermute(control, 'lat', forward)  27.8 us
    pallas_call x3, Pallas kernels, collect(): pl.pallas_call(functools.partial(collect_kernel, first=first, lon=lon), o...  26.9 us
    ppermute x3, starting transfers between devices, halos(): lax.ppermute(control, 'lat', backward)  17.5 us
    ppermute x1, starting transfers between devices, local(): lax.ppermute(gradient_here, 'mem', down)  14.5 us
    ppermute x3, starting transfers between devices, halos(): lax.ppermute(control, 'lat', forward)  12.1 us
    ppermute x3, waiting for transfers between devices, halos(): lax.ppermute(control, 'lat', backward)  10.5 us
    pallas_call x2, Pallas kernels, control_of(): pl.pallas_call(control_kernel, out_shape=jax.ShapeDtypeStruct((size, entr...  9.05 us
    pallas_call x1, Pallas kernels, turn_rest(): pl.pallas_call(turn_kernel, out_shape=jax.ShapeDtypeStruct(turned.shape,...  8.73 us
  transfers between devices with their start and end apart: 14, of which 8 were waited for; matrix products, arithmetic and copies ran while one was open for 0% of the time, Pallas kernels for 18%

profile of v3, /device:TPU:32, one launch (start us, length us, event | category | flops | bytes accessed | tf_op | source)
XLA Modules:
  0.0 165.3 jit_solution(12012829277324924180)
XLA Ops:
  0.0 3.2 %prepare.1 = (bf16[12,4,2,16,1440]{4,3,2,1,0:T(8,128)(2,1)}, bf16[2,45,16,128]{3,2,1,0:T(8,128)(2,1)}) custom-call(s32[12]{0:T(128)} %levels_ref.1, s32[1]{0:T(128)} %bitcast.base_ref, bf16[16,2,12,4,1440]{4,3,2,1,0:T(4,128)(2,1)} %pert_ref.3, f32[1,2,2,4,1440]{4,3,2,1,0:T(4,128)} %bitcast.14), custom_call_target="tpu_custom_call" | custom-call | flops 1000 | bytes 1000 | tf_op jit(solution)/shard_map/prepare/pallas_call | solution.py:64
  3.2 4.3 %collective-permute-start.3 = (bf16[2,45,16,128]{3,2,1,0:T(8,128)(2,1)}, bf16[2,45,16,128]{3,2,1,0:T(8,128)(2,1)S(1)}, u32[]{:S(2)}, u32[]{:S(2)}) collective-permute-start(bf16[2,45,16,128]{3,2,1,0:T(8,128)(2,1)} %get-tuple-element.20.own_ref), channel_id=1, source_target_pairs={{0,1},{1,2},{2,3},{3,4},{4,5},{5,6},{6,7},{7,8},{8,9},{9,10},{10,1... | collective-permute-start | bytes 1105928 | tf_op jit(solution)/shard_map/ppermute | solution.py:347
  7.5 7.6 %collective-permute-start.4 = (bf16[2,45,16,128]{3,2,1,0:T(8,128)(2,1)}, bf16[2,45,16,128]{3,2,1,0:T(8,128)(2,1)S(1)}, u32[]{:S(2)}, u32[]{:S(2)}) collective-permute-start(bf16[2,45,16,128]{3,2,1,0:T(8,128)(2,1)} %get-tuple-element.20.own_ref), channel_id=1, source_target_pairs={{1,0},{2,1},{3,2},{4,3},{5,4},{6,5},{7,6},{8,7},{9,8},{10,9},{11,1... | collective-permute-start | bytes 1105928 | tf_op jit(solution)/shard_map/ppermute | solution.py:347
  15.1 0.0 copy-done.8
  15.1 14.5 %collective-permute-start = (f32[2,2,4,1440]{3,2,1,0:T(4,128)S(1)}, f32[2,2,4,1440]{3,2,1,0:T(4,128)S(1)}, u32[]{:S(2)}, u32[]{:S(2)}) collective-permute-start(f32[2,2,4,1440]{3,2,1,0:T(4,128)S(1)} %copy-done.8), channel_id=1, source_target_pairs={{256,0},{384,128},{512,256},{640,384},{0,512},{128,640},{257,1},{3... | collective-permute-start | bytes 276488 | tf_op jit(solution)/shard_map/ppermute | solution.py:356
  29.6 1.9 %collective-permute-start.1 = (f32[2,2,4,1440]{3,2,1,0:T(4,128)S(1)}, f32[2,2,4,1440]{3,2,1,0:T(4,128)S(1)}, u32[]{:S(2)}, u32[]{:S(2)}) collective-permute-start(f32[2,2,4,1440]{3,2,1,0:T(4,128)S(1)} %copy-done.8), channel_id=1, source_target_pairs={{0,256},{128,384},{256,512},{384,640},{512,0},{640,128},{1,257},{1... | collective-permute-start | bytes 276488 | tf_op jit(solution)/shard_map/ppermute | solution.py:357
  31.6 1.9 %collective-permute-start.2 = (f32[2,2,4,1440]{3,2,1,0:T(4,128)S(1)}, f32[2,2,4,1440]{3,2,1,0:T(4,128)S(1)}, u32[]{:S(2)}, u32[]{:S(2)}) collective-permute-start(f32[2,2,4,1440]{3,2,1,0:T(4,128)S(1)} %copy-done.8), channel_id=1, source_target_pairs={{0,128},{128,0},{256,384},{384,256},{512,640},{640,512},{1,129},{1... | collective-permute-start | bytes 276488 | tf_op jit(solution)/shard_map/ppermute | solution.py:358
  33.5 0.7 select_reduce_fusion.levels_ref
  34.2 8.7 %turn.1.turned_ref.pert_ref = bf16[12,4,2,16,1440]{4,3,2,1,0:T(8,128)(2,1)} custom-call(s32[12]{0:T(128)} %select_reduce_fusion.levels_ref, bf16[16,2,12,4,1440]{4,3,2,1,0:T(4,128)(2,1)} %pert_ref.3, bf16[12,4,2,16,1440]{4,3,2,1,0:T(8,128)(2,1)} %get-tuple-element.19.turned_in_ref), custom_call_target="tpu_custom_call", output_to_operand_aliasing={{}: (2, {})} | custom-call | flops 1000 | bytes 1000 | tf_op jit(solution)/shard_map/turn/pallas_call | solution.py:96
  42.9 0.0 collective-permute-done
  43.0 0.4 collective-permute-done.1
  43.4 0.0 collective-permute-done.2
  43.4 0.0 collective-permute-done.3.low_ref
  43.4 0.0 collective-permute-done.4.high_ref
  43.4 0.0 slice-start
  43.4 0.2 copy-done.3
  43.6 0.4 copy-done.4
  44.0 0.0 copy-done.5
  44.1 5.3 %control.3.own_ref = bf16[6,45,16,128]{3,2,1,0:T(8,128)(2,1)} custom-call(bf16[12,4,2,16,1440]{4,3,2,1,0:T(8,128)(2,1)} %turn.1.turned_ref.pert_ref, f32[1,2,2,4,1440]{4,3,2,1,0:T(4,128)} %bitcast.9, f32[1,2,2,4,1440]{4,3,2,1,0:T(4,128)} %bitcast.10, f32[1,2,2,4,1440]{4,3,2,1,0:T(4,128)} %bitcast.11), custom_call_target="tpu_custom_call" | custom-call | flops 1000 | bytes 1000 | tf_op jit(solution)/shard_map/control/pallas_call | solution.py:133
  49.4 1.9 %collective-permute-start.10 = (bf16[6,45,16,128]{3,2,1,0:T(8,128)(2,1)}, bf16[6,45,16,128]{3,2,1,0:T(8,128)(2,1)S(1)}, u32[]{:S(2)}, u32[]{:S(2)}) collective-permute-start(bf16[6,45,16,128]{3,2,1,0:T(8,128)(2,1)} %control.3.own_ref), channel_id=1, source_target_pairs={{1,0},{2,1},{3,2},{4,3},{5,4},{6,5},{7,6},{8,7},{9,8},{10,9},{11,1... | collective-permute-start | bytes 3317768 | tf_op jit(solution)/shard_map/ppermute | solution.py:347
  51.3 3.9 %collective-permute-start.9 = (bf16[6,45,16,128]{3,2,1,0:T(8,128)(2,1)}, bf16[6,45,16,128]{3,2,1,0:T(8,128)(2,1)S(1)}, u32[]{:S(2)}, u32[]{:S(2)}) collective-permute-start(bf16[6,45,16,128]{3,2,1,0:T(8,128)(2,1)} %control.3.own_ref), channel_id=1, source_target_pairs={{0,1},{1,2},{2,3},{3,4},{4,5},{5,6},{6,7},{7,8},{8,9},{9,10},{10,1... | collective-permute-start | bytes 3317768 | tf_op jit(solution)/shard_map/ppermute | solution.py:347
  55.2 1.9 %collective-permute-start.5 = (f32[2,2,4,1440]{3,2,1,0:T(4,128)}, f32[2,2,4,1440]{3,2,1,0:T(4,128)S(1)}, u32[]{:S(2)}, u32[]{:S(2)}) collective-permute-start(f32[2,2,4,1440]{3,2,1,0:T(4,128)} %copy-done.3), channel_id=1, source_target_pairs={{0,128},{128,0},{256,384},{384,256},{512,640},{640,512},{1,129},{1... | collective-permute-start | bytes 276488 | tf_op jit(solution)/shard_map/ppermute | solution.py:364
  57.2 2.4 %collective-permute-start.6 = (f32[2,2,4,1440]{3,2,1,0:T(4,128)}, f32[2,2,4,1440]{3,2,1,0:T(4,128)S(1)}, u32[]{:S(2)}, u32[]{:S(2)}) collective-permute-start(f32[2,2,4,1440]{3,2,1,0:T(4,128)} %copy-done.4), channel_id=1, source_target_pairs={{0,128},{128,0},{256,384},{384,256},{512,640},{640,512},{1,129},{1... | collective-permute-start | bytes 276488 | tf_op jit(solution)/shard_map/ppermute | solution.py:364
  59.6 0.0 collective-permute-done.5
  59.6 0.0 copy-start.6
  59.6 1.1 collective-permute-done.6
  60.7 0.6 copy-done.7
  61.3 3.7 %control.2.own_ref = bf16[4,45,16,128]{3,2,1,0:T(8,128)(2,1)} custom-call(bf16[12,4,2,16,1440]{4,3,2,1,0:T(8,128)(2,1)} %turn.1.turned_ref.pert_ref, f32[1,2,2,4,1440]{4,3,2,1,0:T(4,128)} %bitcast.12, f32[1,2,2,4,1440]{4,3,2,1,0:T(4,128)} %bitcast.13), custom_call_target="tpu_custom_call" | custom-call | flops 1000 | bytes 1000 | tf_op jit(solution)/shard_map/control/pallas_call | solution.py:133
  65.1 3.9 %collective-permute-start.7 = (bf16[4,45,16,128]{3,2,1,0:T(8,128)(2,1)}, bf16[4,45,16,128]{3,2,1,0:T(8,128)(2,1)S(1)}, u32[]{:S(2)}, u32[]{:S(2)}) collective-permute-start(bf16[4,45,16,128]{3,2,1,0:T(8,128)(2,1)} %control.2.own_ref), channel_id=1, source_target_pairs={{0,1},{1,2},{2,3},{3,4},{4,5},{5,6},{6,7},{7,8},{8,9},{9,10},{10,1... | collective-permute-start | bytes 2211848 | tf_op jit(solution)/shard_map/ppermute | solution.py:347
  69.0 8.0 %collective-permute-start.8 = (bf16[4,45,16,128]{3,2,1,0:T(8,128)(2,1)}, bf16[4,45,16,128]{3,2,1,0:T(8,128)(2,1)S(1)}, u32[]{:S(2)}, u32[]{:S(2)}) collective-permute-start(bf16[4,45,16,128]{3,2,1,0:T(8,128)(2,1)} %control.2.own_ref), channel_id=1, source_target_pairs={{1,0},{2,1},{3,2},{4,3},{5,4},{6,5},{7,6},{8,7},{9,8},{10,9},{11,1... | collective-permute-start | bytes 2211848 | tf_op jit(solution)/shard_map/ppermute | solution.py:347
  77.0 0.1 select_select_fusion.weight_ref
  77.0 0.0 slice-done
  77.1 5.5 %collect.3 = (f32[2,6,4,1440]{3,2,1,0:T(4,128)S(1)}, f32[2,6,4,1440]{3,2,1,0:T(4,128)S(1)}) custom-call(f32[12,12]{1,0:T(8,128)S(1)} %select_select_fusion.weight_ref, bf16[2,45,16,128]{3,2,1,0:T(8,128)(2,1)S(1)} %collective-permute-done.3.low_ref, bf16[2,45,16,128]{3,2,1,0:T(8,128)(2,1)S(1)} %copy-done.2, ...), custom_call_target="tpu_custom_call" | custom-call | flops 1000 | bytes 1000 | tf_op jit(solution)/shard_map/collect/pallas_call | solution.py:298
  82.6 0.0 copy-start.1
  82.6 0.0 collective-permute-done.10.high_ref
  82.6 24.6 %collective-permute-done.9.low_ref = bf16[6,45,16,128]{3,2,1,0:T(8,128)(2,1)S(1)} collective-permute-done((bf16[6,45,16,128]{3,2,1,0:T(8,128)(2,1)}, bf16[6,45,16,128]{3,2,1,0:T(8,128)(2,1)S(1)}, u32[]{:S(2)}, u32[]{:S(2)}) %collective-permute-start.9) | collective-permute-done | bytes 1105952 | tf_op jit(solution)/shard_map/ppermute | solution.py:347
  107.2 12.5 %collect.4 = (f32[2,6,4,1440]{3,2,1,0:T(4,128)S(1)}, f32[2,6,4,1440]{3,2,1,0:T(4,128)S(1)}) custom-call(f32[12,12]{1,0:T(8,128)S(1)} %select_select_fusion.weight_ref, bf16[6,45,16,128]{3,2,1,0:T(8,128)(2,1)S(1)} %collective-permute-done.9.low_ref, bf16[6,45,16,128]{3,2,1,0:T(8,128)(2,1)S(1)} %copy-done, ...), custom_call_target="tpu_custom_call" | custom-call | flops 1000 | bytes 1000 | tf_op jit(solution)/shard_map/collect/pallas_call | solution.py:298
  119.7 3.2 %collective-permute-done.7.low_ref = bf16[4,45,16,128]{3,2,1,0:T(8,128)(2,1)S(1)} collective-permute-done((bf16[4,45,16,128]{3,2,1,0:T(8,128)(2,1)}, bf16[4,45,16,128]{3,2,1,0:T(8,128)(2,1)S(1)}, u32[]{:S(2)}, u32[]{:S(2)}) %collective-permute-start.7) | collective-permute-done | bytes 737312 | tf_op jit(solution)/shard_map/ppermute | solution.py:347
  122.9 10.5 %collective-permute-done.8.high_ref = bf16[4,45,16,128]{3,2,1,0:T(8,128)(2,1)S(1)} collective-permute-done((bf16[4,45,16,128]{3,2,1,0:T(8,128)(2,1)}, bf16[4,45,16,128]{3,2,1,0:T(8,128)(2,1)S(1)}, u32[]{:S(2)}, u32[]{:S(2)}) %collective-permute-start.8) | collective-permute-done | bytes 737312 | tf_op jit(solution)/shard_map/ppermute | solution.py:347
  133.3 9.0 %collect.5 = (f32[2,6,4,1440]{3,2,1,0:T(4,128)S(1)}, f32[2,6,4,1440]{3,2,1,0:T(4,128)S(1)}) custom-call(f32[12,12]{1,0:T(8,128)S(1)} %select_select_fusion.weight_ref, bf16[4,45,16,128]{3,2,1,0:T(8,128)(2,1)S(1)} %collective-permute-done.7.low_ref, bf16[4,45,16,128]{3,2,1,0:T(8,128)(2,1)S(1)} %copy-done.1, ...), custom_call_target="tpu_custom_call" | custom-call | flops 1000 | bytes 1000 | tf_op jit(solution)/shard_map/collect/pallas_call | solution.py:298
  142.3 1.9 %collective-permute-start.11 = (f32[2,6,4,1440]{3,2,1,0:T(4,128)S(1)}, f32[2,6,4,1440]{3,2,1,0:T(4,128)S(1)}, u32[]{:S(2)}, u32[]{:S(2)}) collective-permute-start(f32[2,6,4,1440]{3,2,1,0:T(4,128)S(1)} %get-tuple-element.32), channel_id=1, source_target_pairs={{0,128},{128,0},{256,384},{384,256},{512,640},{640,512},{1,129},{1... | collective-permute-start | bytes 829448 | tf_op jit(solution)/shard_map/ppermute | solution.py:377
  144.2 1.5 collective-permute-done.11
  145.8 0.1 fusion.11
  145.9 8.3 %collective-permute-start.12 = (bf16[2,2,4,1440]{3,2,1,0:T(4,128)(2,1)S(1)}, bf16[2,2,4,1440]{3,2,1,0:T(4,128)(2,1)S(1)}, u32[]{:S(2)}, u32[]{:S(2)}) collective-permute-start(bf16[2,2,4,1440]{3,2,1,0:T(4,128)(2,1)S(1)} %get-tuple-element.35), channel_id=1, source_target_pairs={{0,256},{128,384},{256,512},{384,640},{512,0},{640,128},{1,257},{1... | collective-permute-start | bytes 138248 | tf_op jit(solution)/shard_map/ppermute | solution.py:378
  154.2 1.9 %collective-permute-start.13 = (bf16[2,2,4,1440]{3,2,1,0:T(4,128)(2,1)S(1)}, bf16[2,2,4,1440]{3,2,1,0:T(4,128)(2,1)S(1)}, u32[]{:S(2)}, u32[]{:S(2)}) collective-permute-start(bf16[2,2,4,1440]{3,2,1,0:T(4,128)(2,1)S(1)} %get-tuple-element.36), channel_id=1, source_target_pairs={{256,0},{384,128},{512,256},{640,384},{0,512},{128,640},{257,1},{3... | collective-permute-start | bytes 138248 | tf_op jit(solution)/shard_map/ppermute | solution.py:379
  156.2 1.1 collective-permute-done.12
  157.3 7.4 %collective-permute-done.13 = bf16[2,2,4,1440]{3,2,1,0:T(4,128)(2,1)S(1)} collective-permute-done((bf16[2,2,4,1440]{3,2,1,0:T(4,128)(2,1)S(1)}, bf16[2,2,4,1440]{3,2,1,0:T(4,128)(2,1)S(1)}, u32[]{:S(2)}, u32[]{:S(2)}) %collective-permute-start.13) | collective-permute-done | bytes 46112 | tf_op jit(solution)/shard_map/ppermute | solution.py:379
  164.7 0.7 fusion
  (20 shorter events, 0.1 us)
Async XLA Ops:
  0.0 33.5 %copy-start.10 = (s32[12]{0:T(128)S(1)}, s32[12]{0:T(128)}, u32[]{:S(2)}) copy-start(s32[12]{0:T(128)} %levels_ref.1) | copy-start | bytes 148
  0.0 15.1 %copy-start.8 = (f32[2,2,4,1440]{3,2,1,0:T(4,128)S(1)}, f32[2,2,4,1440]{3,2,1,0:T(4,128)}, u32[]{:S(2)}) copy-start(f32[2,2,4,1440]{3,2,1,0:T(4,128)} %param.4) | copy-start | bytes 276484
  3.2 40.2 %collective-permute-start.3 = (bf16[2,45,16,128]{3,2,1,0:T(8,128)(2,1)}, bf16[2,45,16,128]{3,2,1,0:T(8,128)(2,1)S(1)}, u32[]{:S(2)}, u32[]{:S(2)}) collective-permute-start(bf16[2,45,16,128]{3,2,1,0:T(8,128)(2,1)} %get-tuple-element.20.own_ref), channel_id=1, source_target_pairs={{0,1},{1,2},{2,3},{3,4},{4,5},{5,6},{6,7},{7,8},{8,9},{9,10},{10,1... | collective-permute-start | bytes 1105928 | tf_op jit(solution)/shard_map/ppermute | solution.py:347
  7.5 35.9 %collective-permute-start.4 = (bf16[2,45,16,128]{3,2,1,0:T(8,128)(2,1)}, bf16[2,45,16,128]{3,2,1,0:T(8,128)(2,1)S(1)}, u32[]{:S(2)}, u32[]{:S(2)}) collective-permute-start(bf16[2,45,16,128]{3,2,1,0:T(8,128)(2,1)} %get-tuple-element.20.own_ref), channel_id=1, source_target_pairs={{1,0},{2,1},{3,2},{4,3},{5,4},{6,5},{7,6},{8,7},{9,8},{10,9},{11,1... | collective-permute-start | bytes 1105928 | tf_op jit(solution)/shard_map/ppermute | solution.py:347
  15.1 27.8 %collective-permute-start = (f32[2,2,4,1440]{3,2,1,0:T(4,128)S(1)}, f32[2,2,4,1440]{3,2,1,0:T(4,128)S(1)}, u32[]{:S(2)}, u32[]{:S(2)}) collective-permute-start(f32[2,2,4,1440]{3,2,1,0:T(4,128)S(1)} %copy-done.8), channel_id=1, source_target_pairs={{256,0},{384,128},{512,256},{640,384},{0,512},{128,640},{257,1},{3... | collective-permute-start | bytes 276488 | tf_op jit(solution)/shard_map/ppermute | solution.py:356
  29.6 13.7 %collective-permute-start.1 = (f32[2,2,4,1440]{3,2,1,0:T(4,128)S(1)}, f32[2,2,4,1440]{3,2,1,0:T(4,128)S(1)}, u32[]{:S(2)}, u32[]{:S(2)}) collective-permute-start(f32[2,2,4,1440]{3,2,1,0:T(4,128)S(1)} %copy-done.8), channel_id=1, source_target_pairs={{0,256},{128,384},{256,512},{384,640},{512,0},{640,128},{1,257},{1... | collective-permute-start | bytes 276488 | tf_op jit(solution)/shard_map/ppermute | solution.py:357
  31.6 11.8 %collective-permute-start.2 = (f32[2,2,4,1440]{3,2,1,0:T(4,128)S(1)}, f32[2,2,4,1440]{3,2,1,0:T(4,128)S(1)}, u32[]{:S(2)}, u32[]{:S(2)}) collective-permute-start(f32[2,2,4,1440]{3,2,1,0:T(4,128)S(1)} %copy-done.8), channel_id=1, source_target_pairs={{0,128},{128,0},{256,384},{384,256},{512,640},{640,512},{1,129},{1... | collective-permute-start | bytes 276488 | tf_op jit(solution)/shard_map/ppermute | solution.py:358
  43.0 0.6 copy-start.3
  43.4 0.7 copy-start.4
  43.4 0.7 copy-start.5
  43.4 33.6 %slice-start = ((s8[4718592]{0:T(1024)(128)(4,1)}), s8[4194304]{0:T(1024)(128)(4,1)S(1)}, s32[]{:S(2)}) async-start(s8[4718592]{0:T(1024)(128)(4,1)} %bitcast.7), calls=%async_computation | async-start | bytes 8388608
  44.1 32.9 %copy-start.9 = (s32[12]{0:T(128)S(1)}, s32[12]{0:T(128)}, u32[]{:S(2)}) copy-start(s32[12]{0:T(128)} %select_reduce_fusion.levels_ref) | copy-start | bytes 148
  44.1 33.0 %slice-start.1 = ((s8[4718592]{0:T(1024)(128)(4,1)}), s8[524288]{0:T(1024)(128)(4,1)S(1)}, s32[]{:S(2)}) async-start(s8[4718592]{0:T(1024)(128)(4,1)} %bitcast.7), calls=%async_computation.1 | async-start | bytes 1048576
  44.1 33.0 %copy-start.2 = (bf16[2,45,16,128]{3,2,1,0:T(8,128)(2,1)S(1)}, bf16[2,45,16,128]{3,2,1,0:T(8,128)(2,1)}, u32[]{:S(2)}) copy-start(bf16[2,45,16,128]{3,2,1,0:T(8,128)(2,1)} %get-tuple-element.20.own_ref) | copy-start | bytes 1105924
  49.4 33.2 %collective-permute-start.10 = (bf16[6,45,16,128]{3,2,1,0:T(8,128)(2,1)}, bf16[6,45,16,128]{3,2,1,0:T(8,128)(2,1)S(1)}, u32[]{:S(2)}, u32[]{:S(2)}) collective-permute-start(bf16[6,45,16,128]{3,2,1,0:T(8,128)(2,1)} %control.3.own_ref), channel_id=1, source_target_pairs={{1,0},{2,1},{3,2},{4,3},{5,4},{6,5},{7,6},{8,7},{9,8},{10,9},{11,1... | collective-permute-start | bytes 3317768 | tf_op jit(solution)/shard_map/ppermute | solution.py:347
  51.3 55.9 %collective-permute-start.9 = (bf16[6,45,16,128]{3,2,1,0:T(8,128)(2,1)}, bf16[6,45,16,128]{3,2,1,0:T(8,128)(2,1)S(1)}, u32[]{:S(2)}, u32[]{:S(2)}) collective-permute-start(bf16[6,45,16,128]{3,2,1,0:T(8,128)(2,1)} %control.3.own_ref), channel_id=1, source_target_pairs={{0,1},{1,2},{2,3},{3,4},{4,5},{5,6},{6,7},{7,8},{8,9},{9,10},{10,1... | collective-permute-start | bytes 3317768 | tf_op jit(solution)/shard_map/ppermute | solution.py:347
  55.2 4.3 %collective-permute-start.5 = (f32[2,2,4,1440]{3,2,1,0:T(4,128)}, f32[2,2,4,1440]{3,2,1,0:T(4,128)S(1)}, u32[]{:S(2)}, u32[]{:S(2)}) collective-permute-start(f32[2,2,4,1440]{3,2,1,0:T(4,128)} %copy-done.3), channel_id=1, source_target_pairs={{0,128},{128,0},{256,384},{384,256},{512,640},{640,512},{1,129},{1... | collective-permute-start | bytes 276488 | tf_op jit(solution)/shard_map/ppermute | solution.py:364
  57.2 3.5 %collective-permute-start.6 = (f32[2,2,4,1440]{3,2,1,0:T(4,128)}, f32[2,2,4,1440]{3,2,1,0:T(4,128)S(1)}, u32[]{:S(2)}, u32[]{:S(2)}) collective-permute-start(f32[2,2,4,1440]{3,2,1,0:T(4,128)} %copy-done.4), channel_id=1, source_target_pairs={{0,128},{128,0},{256,384},{384,256},{512,640},{640,512},{1,129},{1... | collective-permute-start | bytes 276488 | tf_op jit(solution)/shard_map/ppermute | solution.py:364
  59.6 1.1 copy-start.6
  60.7 0.6 copy-start.7
  61.3 45.8 %copy-start = (bf16[6,45,16,128]{3,2,1,0:T(8,128)(2,1)S(1)}, bf16[6,45,16,128]{3,2,1,0:T(8,128)(2,1)}, u32[]{:S(2)}) copy-start(bf16[6,45,16,128]{3,2,1,0:T(8,128)(2,1)} %control.3.own_ref) | copy-start | bytes 3317764
  65.1 57.8 %collective-permute-start.7 = (bf16[4,45,16,128]{3,2,1,0:T(8,128)(2,1)}, bf16[4,45,16,128]{3,2,1,0:T(8,128)(2,1)S(1)}, u32[]{:S(2)}, u32[]{:S(2)}) collective-permute-start(bf16[4,45,16,128]{3,2,1,0:T(8,128)(2,1)} %control.2.own_ref), channel_id=1, source_target_pairs={{0,1},{1,2},{2,3},{3,4},{4,5},{5,6},{6,7},{7,8},{8,9},{9,10},{10,1... | collective-permute-start | bytes 2211848 | tf_op jit(solution)/shard_map/ppermute | solution.py:347
  69.0 64.4 %collective-permute-start.8 = (bf16[4,45,16,128]{3,2,1,0:T(8,128)(2,1)}, bf16[4,45,16,128]{3,2,1,0:T(8,128)(2,1)S(1)}, u32[]{:S(2)}, u32[]{:S(2)}) collective-permute-start(bf16[4,45,16,128]{3,2,1,0:T(8,128)(2,1)} %control.2.own_ref), channel_id=1, source_target_pairs={{1,0},{2,1},{3,2},{4,3},{5,4},{6,5},{7,6},{8,7},{9,8},{10,9},{11,1... | collective-permute-start | bytes 2211848 | tf_op jit(solution)/shard_map/ppermute | solution.py:347
  82.6 50.8 %copy-start.1 = (bf16[4,45,16,128]{3,2,1,0:T(8,128)(2,1)S(1)}, bf16[4,45,16,128]{3,2,1,0:T(8,128)(2,1)}, u32[]{:S(2)}) copy-start(bf16[4,45,16,128]{3,2,1,0:T(8,128)(2,1)} %control.2.own_ref) | copy-start | bytes 2211844
  142.3 3.5 %collective-permute-start.11 = (f32[2,6,4,1440]{3,2,1,0:T(4,128)S(1)}, f32[2,6,4,1440]{3,2,1,0:T(4,128)S(1)}, u32[]{:S(2)}, u32[]{:S(2)}) collective-permute-start(f32[2,6,4,1440]{3,2,1,0:T(4,128)S(1)} %get-tuple-element.32), channel_id=1, source_target_pairs={{0,128},{128,0},{256,384},{384,256},{512,640},{640,512},{1,129},{1... | collective-permute-start | bytes 829448 | tf_op jit(solution)/shard_map/ppermute | solution.py:377
  145.9 11.3 %collective-permute-start.12 = (bf16[2,2,4,1440]{3,2,1,0:T(4,128)(2,1)S(1)}, bf16[2,2,4,1440]{3,2,1,0:T(4,128)(2,1)S(1)}, u32[]{:S(2)}, u32[]{:S(2)}) collective-permute-start(bf16[2,2,4,1440]{3,2,1,0:T(4,128)(2,1)S(1)} %get-tuple-element.35), channel_id=1, source_target_pairs={{0,256},{128,384},{256,512},{384,640},{512,0},{640,128},{1,257},{1... | collective-permute-start | bytes 138248 | tf_op jit(solution)/shard_map/ppermute | solution.py:378
  154.2 10.4 %collective-permute-start.13 = (bf16[2,2,4,1440]{3,2,1,0:T(4,128)(2,1)S(1)}, bf16[2,2,4,1440]{3,2,1,0:T(4,128)(2,1)S(1)}, u32[]{:S(2)}, u32[]{:S(2)}) collective-permute-start(bf16[2,2,4,1440]{3,2,1,0:T(4,128)(2,1)S(1)} %get-tuple-element.36), channel_id=1, source_target_pairs={{256,0},{384,128},{512,256},{640,384},{0,512},{128,640},{257,1},{3... | collective-permute-start | bytes 138248 | tf_op jit(solution)/shard_map/ppermute | solution.py:379

commit v4 on v2

--- a/solution.py
+++ b/solution.py
@@ -51,7 +51,7 @@
 
 
 def prepare(
-    first, size, levels, base, perturbations, gradient, skip=0, turned=None
+    first, size, levels, base, perturbations, gradient, skip=0, turned=None, limit=VMEM_LIMIT
 ):
     members, slots, count, rows, lon = perturbations.shape
     entries = rows * (lon // LANES) + 1
@@ -91,7 +91,7 @@
         input_output_aliases=aliases,
         name="prepare",
         cost_estimate=COST,
-        compiler_params=pltpu.CompilerParams(vmem_limit_bytes=57 * 1024 * 1024),
+        compiler_params=pltpu.CompilerParams(vmem_limit_bytes=limit),
     )(levels, base, *inputs)
 
 
@@ -126,18 +126,34 @@
             before = pltpu.roll(tiles[full], LANES - rest, 1)
             tiles[full] = jnp.where(lane < rest, tiles[full], pltpu.roll(tiles[0], rest, 1))
             tiles = [before] + tiles
-            totals = [LON_W[4] * tile for tile in tiles[1:]]
-            for step in range(1, 5):
-                right = [pltpu.roll(tile, step, 1) for tile in tiles]
-                left = [pltpu.roll(tile, LANES - step, 1) for tile in tiles[1:]]
-                left.append(left[-1])
-                for tile in range(full + 1):
-                    both = jnp.where(lane < step, right[tile], right[tile + 1]) + jnp.where(
-                        lane < LANES - step, left[tile], left[tile + 1]
-                    )
-                    totals[tile] = totals[tile] + LON_W[4 + step] * both
+
+            def moved(arrays, step):
+                rolled = [pltpu.roll(array, -step % LANES, 1) for array in arrays]
+                if step > 0:
+                    return [
+                        jnp.where(lane < LANES - step, here, after)
+                        for here, after in zip(rolled, rolled[1:] + rolled[-1:])
+                    ]
+                return [
+                    jnp.where(lane < -step, former, here)
+                    for former, here in zip(rolled[:1] + rolled[:-1], rolled)
+                ]
+
+            last, following = moved(tiles, -1), moved(tiles, 1)
+            inner = [LON_W[1] * tile for tile in tiles]
+            lower = [
+                LON_W[0] * a + b + LON_W[2] * c for a, b, c in zip(last, inner, following)
+            ]
+            upper = [
+                LON_W[2] * a + b + LON_W[0] * c for a, b, c in zip(last, inner, following)
+            ]
+            lower, upper = moved(lower, -3), moved(upper, 3)
             for tile in range(full + 1):
-                out_ref[level, row, some, tile * LANES : (tile + 1) * LANES] = totals[tile]
+                k = tile + 1
+                total = LON_W[4] * tiles[k] + LON_W[3] * (last[k] + following[k])
+                out_ref[level, row, some, tile * LANES : (tile + 1) * LANES] = (
+                    total + lower[k] + upper[k]
+                )
 
 
 def sums_of(arrays, sub):
@@ -170,7 +186,7 @@
                 for source in range(1, size):
                     total = total + weights[i][source] * values[source]
                 for slot in range(slots):
-                    product = total * pert_ref[i, row, slot, :, lanes].astype(jnp.float32)
+                    product = total * pert_ref[2 * pair + i, row, slot, :, lanes].astype(jnp.float32)
                     product = product.reshape(members // 8, 8, across)
                     part = product[0]
                     for other in range(1, members // 8):
@@ -224,10 +240,7 @@
     ours = pl.BlockSpec(
         (slots, 2, rows, lon), lambda i, w: (0, jnp.clip(i - size - half, 0, half - 1), 0, 0)
     )
-    pert = pl.BlockSpec(
-        (2, rows, slots, members, lon),
-        lambda i, w: ((jnp.maximum(i - size, 0) + half) % pairs, 0, 0, 0, 0),
-    )
+    pert = pl.BlockSpec(memory_space=pltpu.VMEM)
     result = jax.ShapeDtypeStruct((slots, count // 2, rows, lon), jnp.float32)
     return pl.pallas_call(
         functools.partial(collect_kernel, first=first, lon=lon),
@@ -248,6 +261,73 @@
     )(weights, low, own, high, turned, *(() if before is None else before))
 
 
+def first_kernel(weight_ref, low_ref, own_ref, high_ref, pert_ref, *refs, first, lon):
+    before_ref, theirs_ref, fields_ref, wide_ref = refs
+    size, rows = fields_ref.shape[:2]
+    step = pl.program_id(0)
+
+    @pl.when(step < size)
+    def _():
+        smooth_level((low_ref, own_ref, high_ref), fields_ref, step, wide_ref, rows, lon)
+
+    @pl.when(step >= size)
+    def _():
+        pair = step - size + pl.num_programs(0) - size
+        collect_pair(
+            pair, first, fields_ref, weight_ref, pert_ref, before_ref, theirs_ref, lon
+        )
+
+
+def second_kernel(weight_ref, fields_ref, pert_ref, before_ref, ours_ref, *, first, lon):
+    pair = pl.program_id(0)
+    collect_pair(pair, first, fields_ref, weight_ref, pert_ref, before_ref, ours_ref, lon)
+
+
+def collect_last(first, weights, low, own, high, turned, before):
+    count, rows, slots, members, lon = turned.shape
+    size, entries = own.shape[:2]
+    half = count // 4
+    width = (lon // LANES + 1) * LANES
+    level = pl.BlockSpec(
+        (1, entries, members, LANES), lambda i, w: (jnp.minimum(i, size - 1), 0, 0, 0)
+    )
+    moved = pl.BlockSpec((slots, 2, rows, lon), lambda i, w: (0, jnp.maximum(i - size, 0), 0, 0))
+    still = pl.BlockSpec((slots, 2, rows, lon), lambda i, w: (0, i, 0, 0))
+    resident = pl.BlockSpec(memory_space=pltpu.VMEM)
+    result = jax.ShapeDtypeStruct((slots, count // 2, rows, lon), jnp.float32)
+    theirs, fields = pl.pallas_call(
+        functools.partial(first_kernel, first=first, lon=lon),
+        out_shape=(
+            result,
+            jax.ShapeDtypeStruct((size, rows, members, width), jnp.float32),
+        ),
+        grid_spec=pltpu.PrefetchScalarGridSpec(
+            num_scalar_prefetch=1,
+            grid=(size + half,),
+            in_specs=[level] * 3 + [resident, moved],
+            out_specs=(moved, resident),
+            scratch_shapes=[pltpu.VMEM((rows, members, width), jnp.float32)],
+        ),
+        name="collect_theirs",
+        cost_estimate=COST,
+        compiler_params=pltpu.CompilerParams(vmem_limit_bytes=VMEM_LIMIT),
+    )(weights, low, own, high, turned, before[0])
+    ours = pl.pallas_call(
+        functools.partial(second_kernel, first=first, lon=lon),
+        out_shape=result,
+        grid_spec=pltpu.PrefetchScalarGridSpec(
+            num_scalar_prefetch=1,
+            grid=(half,),
+            in_specs=[resident, resident, still],
+            out_specs=still,
+        ),
+        name="collect_ours",
+        cost_estimate=COST,
+        compiler_params=pltpu.CompilerParams(vmem_limit_bytes=VMEM_LIMIT),
+    )(weights, fields, turned, before[1])
+    return theirs, ours
+
+
 def local(perturbations, gradient_held, block_owner):
     members, slots, levels, rows, lon = perturbations.shape
     across = lax.axis_size("mem") // 2
@@ -277,8 +357,12 @@
     for step in range(5):
         weights = jnp.where(apart == step, LEV_W[4 + step], weights)
 
-    def halos(control):
-        return lax.ppermute(control, "lat", forward), lax.ppermute(control, "lat", backward)
+    def halos(control, after=None):
+        lower, upper = control, control
+        if after is not None:
+            lower, _ = lax.optimization_barrier((control, after[0]))
+            upper, _ = lax.optimization_barrier((control, after[1]))
+        return lax.ppermute(lower, "lat", forward), lax.ppermute(upper, "lat", backward)
 
     turned, own = prepare(
         0,
@@ -287,34 +371,31 @@
         (2 * place).astype(jnp.int32).reshape(1),
         perturbations,
         gradient_held[None],
+        limit=57 * 1024 * 1024,
     )
     own_low, own_high = halos(own)
     gradient_here, _ = lax.optimization_barrier((gradient_held, own))
-    above_held = lax.ppermute(gradient_here, "mem", down)
-    below_held = lax.ppermute(gradient_here, "mem", up)
-    other_held = lax.ppermute(gradient_here, "mem", swap)
-    above_held, below_held, other_held, own_low, own_high = lax.optimization_barrier(
-        (above_held, below_held, other_held, own_low, own_high)
-    )
-    near = jnp.stack([above_held, below_held, other_held])
+    near = [
+        lax.ppermute(gradient_here, "mem", down),
+        lax.ppermute(gradient_here, "mem", up),
+        lax.ppermute(gradient_here, "mem", swap),
+    ]
+    near = jnp.stack(near)
     far = lax.ppermute(near, "mem", swap)
 
     sums = None
     groups = [(0, own, own_low, own_high)]
-    for first, size, gradient, skip in (
-        (2, 6, near, 0),
-        (8, 3, far, 0),
-        (11, 1, far, 3),
-    ):
+    for first, size, gradient, skip in ((2, 6, near, 0), (8, 4, far, 0)):
         start = jnp.full((1,), first, jnp.int32)
         turned, control = prepare(
             first, size, order, start, perturbations, gradient, skip, turned
         )
-        low, upper = halos(control)
+        low, upper = halos(control, (own_low, own_high) if first == 2 else None)
         groups.append((first, control, low, upper))
-    for first, control, low, upper in groups:
+    for first, control, low, upper in groups[:-1]:
         sums = collect(first, weights, low, control, upper, turned, sums)
-    theirs, ours = sums
+    first, control, low, upper = groups[-1]
+    theirs, ours = collect_last(first, weights, low, control, upper, turned, sums)
     kept = ours + lax.ppermute(theirs, "mem", swap)
     from_below = lax.ppermute(kept[:, 2:4].astype(jnp.bfloat16), "mem", up)
     from_above = lax.ppermute(kept[:, 4:6].astype(jnp.bfloat16), "mem", down)

time: 167 us -> 160 us (0.958)
  the two profiles are of different devices: /device:TPU:32 before, /device:TPU:31 now
where the time goes in v4:
time: 160 us; the launch traced here: 159 us
  starting transfers between devices  60.8 us (38%)
  waiting for transfers between devices  52.3 us (33%)
  Pallas kernels  35.4 us (22%)
  local copies, waits for them, and re-layouts  9.19 us (6%)
    ppermute x3, waiting for transfers between devices, halos(): lax.ppermute(upper, 'lat', backward)  41.3 us
    pallas_call x2, Pallas kernels, collect(): pl.pallas_call(functools.partial(collect_kernel, first=first, lon=lon), o...  18 us
    ppermute x3, starting transfers between devices, halos(): lax.ppermute(upper, 'lat', backward)  17.6 us
    ppermute x1, starting transfers between devices, local(): lax.ppermute(gradient_here, 'mem', down)  14.3 us
    unnamed x14, local copies, waits for them, and re-layouts  9.15 us
    ppermute x3, starting transfers between devices, halos(): lax.ppermute(lower, 'lat', forward)  9 us
    ppermute x1, waiting for transfers between devices, local(): from_above = lax.ppermute(kept[:, 4:6].astype(jnp.bfloat16), 'mem', down)  8.01 us
    pallas_call x3, Pallas kernels, prepare(): pl.pallas_call(prepare_kernel, out_shape=(jax.ShapeDtypeStruct((count, ro...  7.94 us
  transfers between devices with their start and end apart: 13, of which 6 were waited for; matrix products, arithmetic and copies ran while one was open for 0% of the time, Pallas kernels for 16%

profile of v4, /device:TPU:31, one launch (start us, length us, event | category | flops | bytes accessed | tf_op | source)
XLA Modules:
  0.0 159.1 jit_solution(921015320395512964)
XLA Ops:
  0.0 3.2 %prepare.3 = (bf16[12,4,2,16,1440]{4,3,2,1,0:T(8,128)(2,1)}, bf16[2,45,16,128]{3,2,1,0:T(8,128)(2,1)}) custom-call(s32[12]{0:T(128)} %levels_ref.1, s32[1]{0:T(128)} %bitcast.base_ref, bf16[16,2,12,4,1440]{4,3,2,1,0:T(4,128)(2,1)} %pert_ref.5, f32[1,2,2,4,1440]{4,3,2,1,0:T(4,128)} %bitcast.8), custom_call_target="tpu_custom_call" | custom-call | flops 1000 | bytes 1000 | tf_op jit(solution)/shard_map/prepare/pallas_call | solution.py:73
  3.2 0.0 copy-done.5
  3.2 14.3 %collective-permute-start = (f32[2,2,4,1440]{3,2,1,0:T(4,128)S(1)}, f32[2,2,4,1440]{3,2,1,0:T(4,128)S(1)}, u32[]{:S(2)}, u32[]{:S(2)}) collective-permute-start(f32[2,2,4,1440]{3,2,1,0:T(4,128)S(1)} %copy-done.5), channel_id=1, source_target_pairs={{256,0},{384,128},{512,256},{640,384},{0,512},{128,640},{257,1},{3... | collective-permute-start | bytes 276488 | tf_op jit(solution)/shard_map/ppermute | solution.py:379
  17.5 1.9 %collective-permute-start.1 = (f32[2,2,4,1440]{3,2,1,0:T(4,128)S(1)}, f32[2,2,4,1440]{3,2,1,0:T(4,128)S(1)}, u32[]{:S(2)}, u32[]{:S(2)}) collective-permute-start(f32[2,2,4,1440]{3,2,1,0:T(4,128)S(1)} %copy-done.5), channel_id=1, source_target_pairs={{0,256},{128,384},{256,512},{384,640},{512,0},{640,128},{1,257},{1... | collective-permute-start | bytes 276488 | tf_op jit(solution)/shard_map/ppermute | solution.py:380
  19.4 2.9 %collective-permute-start.2 = (f32[2,2,4,1440]{3,2,1,0:T(4,128)S(1)}, f32[2,2,4,1440]{3,2,1,0:T(4,128)S(1)}, u32[]{:S(2)}, u32[]{:S(2)}) collective-permute-start(f32[2,2,4,1440]{3,2,1,0:T(4,128)S(1)} %copy-done.5), channel_id=1, source_target_pairs={{0,128},{128,0},{256,384},{384,256},{512,640},{640,512},{1,129},{1... | collective-permute-start | bytes 276488 | tf_op jit(solution)/shard_map/ppermute | solution.py:381
  22.3 3.1 %collective-permute-start.6 = (bf16[2,45,16,128]{3,2,1,0:T(8,128)(2,1)}, bf16[2,45,16,128]{3,2,1,0:T(8,128)(2,1)S(1)}, u32[]{:S(2)}, u32[]{:S(2)}) collective-permute-start(bf16[2,45,16,128]{3,2,1,0:T(8,128)(2,1)} %get-tuple-element.20.own_ref), channel_id=1, source_target_pairs={{0,1},{1,2},{2,3},{3,4},{4,5},{5,6},{6,7},{7,8},{8,9},{9,10},{10,1... | collective-permute-start | bytes 1105928 | tf_op jit(solution)/shard_map/ppermute | solution.py:365
  25.4 4.9 %collective-permute-start.8 = (bf16[2,45,16,128]{3,2,1,0:T(8,128)(2,1)}, bf16[2,45,16,128]{3,2,1,0:T(8,128)(2,1)S(1)}, u32[]{:S(2)}, u32[]{:S(2)}) collective-permute-start(bf16[2,45,16,128]{3,2,1,0:T(8,128)(2,1)} %get-tuple-element.20.own_ref), channel_id=1, source_target_pairs={{1,0},{2,1},{3,2},{4,3},{5,4},{6,5},{7,6},{8,7},{9,8},{10,9},{11,1... | collective-permute-start | bytes 1105928 | tf_op jit(solution)/shard_map/ppermute | solution.py:365
  30.3 0.0 copy-done.6
  30.3 0.2 select_reduce_fusion.levels_ref
  30.5 0.0 collective-permute-done
  30.5 0.0 collective-permute-done.1
  30.5 0.0 collective-permute-done.2
  30.5 0.1 pad_maximum_fusion.grad_ref
  30.6 0.0 copy-start
  30.6 2.3 %copy-done = bf16[12,4,2,16,1440]{4,3,2,1,0:T(8,128)(2,1)S(1)} copy-done((bf16[12,4,2,16,1440]{4,3,2,1,0:T(8,128)(2,1)S(1)}, bf16[12,4,2,16,1440]{4,3,2,1,0:T(8,128)(2,1)}, u32[]{:S(2)}) %copy-start) | copy-done | bytes 4423704
  32.9 2.3 %copy-done.3 = bf16[16,2,12,4,1440]{4,3,2,1,0:T(4,128)(2,1)S(1)} copy-done((bf16[16,2,12,4,1440]{4,3,2,1,0:T(4,128)(2,1)S(1)}, bf16[16,2,12,4,1440]{4,3,2,1,0:T(4,128)(2,1)}, u32[]{:S(2)}) %copy-start.3) | copy-done | bytes 4423704
  35.3 2.7 %prepare.4 = (bf16[12,4,2,16,1440]{4,3,2,1,0:T(8,128)(2,1)S(1)}, bf16[6,45,16,128]{3,2,1,0:T(8,128)(2,1)S(1)}) custom-call(s32[12]{0:T(128)S(1)} %select_reduce_fusion.levels_ref, s32[1]{0:T(128)} %constant.90.clone.1.base_ref, bf16[16,2,12,4,1440]{4,3,2,1,0:T(4,128)(2,1)S(1)} %copy-done.3, ...), custom_call_target="tpu_custom_call", output_to_operand_aliasing={{0}: (4, {})} | custom-call | flops 1000 | bytes 1000 | tf_op jit(solution)/shard_map/prepare/pallas_call | solution.py:73
  38.0 1.7 %collective-permute-done.6.low_ref = bf16[2,45,16,128]{3,2,1,0:T(8,128)(2,1)S(1)} collective-permute-done((bf16[2,45,16,128]{3,2,1,0:T(8,128)(2,1)}, bf16[2,45,16,128]{3,2,1,0:T(8,128)(2,1)S(1)}, u32[]{:S(2)}, u32[]{:S(2)}) %collective-permute-start.6) | collective-permute-done | bytes 368672 | tf_op jit(solution)/shard_map/ppermute | solution.py:365
  39.8 4.0 %collective-permute-start.7 = (bf16[6,45,16,128]{3,2,1,0:T(8,128)(2,1)S(1)}, bf16[6,45,16,128]{3,2,1,0:T(8,128)(2,1)S(1)}, u32[]{:S(2)}, u32[]{:S(2)}) collective-permute-start(bf16[6,45,16,128]{3,2,1,0:T(8,128)(2,1)S(1)} %get-tuple-element.28.own_ref), channel_id=1, source_target_pairs={{0,1},{1,2},{2,3},{3,4},{4,5},{5,6},{6,7},{7,8},{8,9},{9,10},{10,1... | collective-permute-start | bytes 3317768 | tf_op jit(solution)/shard_map/ppermute | solution.py:365
  43.8 3.9 %collective-permute-done.8.high_ref = bf16[2,45,16,128]{3,2,1,0:T(8,128)(2,1)S(1)} collective-permute-done((bf16[2,45,16,128]{3,2,1,0:T(8,128)(2,1)}, bf16[2,45,16,128]{3,2,1,0:T(8,128)(2,1)S(1)}, u32[]{:S(2)}, u32[]{:S(2)}) %collective-permute-start.8) | collective-permute-done | bytes 368672 | tf_op jit(solution)/shard_map/ppermute | solution.py:365
  47.7 6.7 %collective-permute-start.9 = (bf16[6,45,16,128]{3,2,1,0:T(8,128)(2,1)S(1)}, bf16[6,45,16,128]{3,2,1,0:T(8,128)(2,1)S(1)}, u32[]{:S(2)}, u32[]{:S(2)}) collective-permute-start(bf16[6,45,16,128]{3,2,1,0:T(8,128)(2,1)S(1)} %get-tuple-element.28.own_ref), channel_id=1, source_target_pairs={{1,0},{2,1},{3,2},{4,3},{5,4},{6,5},{7,6},{8,7},{9,8},{10,9},{11,1... | collective-permute-start | bytes 3317768 | tf_op jit(solution)/shard_map/ppermute | solution.py:365
  54.4 3.3 %collective-permute-start.3 = (f32[3,2,2,4,1440]{4,3,2,1,0:T(4,128)S(1)}, f32[3,2,2,4,1440]{4,3,2,1,0:T(4,128)S(1)}, u32[]{:S(2)}, u32[]{:S(2)}) collective-permute-start(f32[3,2,2,4,1440]{4,3,2,1,0:T(4,128)S(1)} %pad_maximum_fusion.grad_ref), channel_id=1, source_target_pairs={{0,128},{128,0},{256,384},{384,256},{512,640},{640,512},{1,129},{1... | collective-permute-start | bytes 829448 | tf_op jit(solution)/shard_map/ppermute | solution.py:384
  57.7 1.2 collective-permute-done.3.grad_ref
  58.9 2.0 %prepare.5 = (bf16[12,4,2,16,1440]{4,3,2,1,0:T(8,128)(2,1)S(1)}, bf16[4,45,16,128]{3,2,1,0:T(8,128)(2,1)S(1)}) custom-call(s32[12]{0:T(128)S(1)} %select_reduce_fusion.levels_ref, s32[1]{0:T(128)} %constant.89.clone.1.base_ref, bf16[16,2,12,4,1440]{4,3,2,1,0:T(4,128)(2,1)S(1)} %copy-done.3, ...), custom_call_target="tpu_custom_call", output_to_operand_aliasing={{0}: (4, {})} | custom-call | flops 1000 | bytes 1000 | tf_op jit(solution)/shard_map/prepare/pallas_call | solution.py:73
  60.9 0.0 copy-start.1
  60.9 2.1 %copy-done.1 = bf16[12,4,2,16,1440]{4,3,2,1,0:T(8,128)(2,1)} copy-done((bf16[12,4,2,16,1440]{4,3,2,1,0:T(8,128)(2,1)}, bf16[12,4,2,16,1440]{4,3,2,1,0:T(8,128)(2,1)S(1)}, u32[]{:S(2)}) %copy-start.1) | copy-done | bytes 4423704
  63.0 1.9 %collective-permute-start.4 = (bf16[4,45,16,128]{3,2,1,0:T(8,128)(2,1)S(1)}, bf16[4,45,16,128]{3,2,1,0:T(8,128)(2,1)S(1)}, u32[]{:S(2)}, u32[]{:S(2)}) collective-permute-start(bf16[4,45,16,128]{3,2,1,0:T(8,128)(2,1)S(1)} %get-tuple-element.24.own_ref), channel_id=1, source_target_pairs={{0,1},{1,2},{2,3},{3,4},{4,5},{5,6},{6,7},{7,8},{8,9},{9,10},{10,1... | collective-permute-start | bytes 2211848 | tf_op jit(solution)/shard_map/ppermute | solution.py:365
  65.0 6.1 %collective-permute-start.5 = (bf16[4,45,16,128]{3,2,1,0:T(8,128)(2,1)S(1)}, bf16[4,45,16,128]{3,2,1,0:T(8,128)(2,1)S(1)}, u32[]{:S(2)}, u32[]{:S(2)}) collective-permute-start(bf16[4,45,16,128]{3,2,1,0:T(8,128)(2,1)S(1)} %get-tuple-element.24.own_ref), channel_id=1, source_target_pairs={{1,0},{2,1},{3,2},{4,3},{5,4},{6,5},{7,6},{8,7},{9,8},{10,9},{11,1... | collective-permute-start | bytes 2211848 | tf_op jit(solution)/shard_map/ppermute | solution.py:365
  71.0 0.1 select_select_fusion.weight_ref
  71.1 0.0 copy-done.4
  71.1 0.0 copy-start.2
  71.1 2.3 %copy-done.2 = bf16[12,4,2,16,1440]{4,3,2,1,0:T(8,128)(2,1)S(1)} copy-done((bf16[12,4,2,16,1440]{4,3,2,1,0:T(8,128)(2,1)S(1)}, bf16[12,4,2,16,1440]{4,3,2,1,0:T(8,128)(2,1)}, u32[]{:S(2)}) %copy-start.2) | copy-done | bytes 4423704
  73.4 5.5 %collect.2 = (f32[2,6,4,1440]{3,2,1,0:T(4,128)S(1)}, f32[2,6,4,1440]{3,2,1,0:T(4,128)S(1)}) custom-call(f32[12,12]{1,0:T(8,128)S(1)} %select_select_fusion.weight_ref, bf16[2,45,16,128]{3,2,1,0:T(8,128)(2,1)S(1)} %collective-permute-done.6.low_ref, bf16[2,45,16,128]{3,2,1,0:T(8,128)(2,1)S(1)} %copy-done.4, ...), custom_call_target="tpu_custom_call" | custom-call | flops 1000 | bytes 1000 | tf_op jit(solution)/shard_map/collect/pallas_call | solution.py:245
  78.9 0.0 collective-permute-done.7.low_ref
  78.9 20.2 %collective-permute-done.9.high_ref = bf16[6,45,16,128]{3,2,1,0:T(8,128)(2,1)S(1)} collective-permute-done((bf16[6,45,16,128]{3,2,1,0:T(8,128)(2,1)S(1)}, bf16[6,45,16,128]{3,2,1,0:T(8,128)(2,1)S(1)}, u32[]{:S(2)}, u32[]{:S(2)}) %collective-permute-start.9) | collective-permute-done | bytes 1105952 | tf_op jit(solution)/shard_map/ppermute | solution.py:365
  99.2 12.5 %collect.3 = (f32[2,6,4,1440]{3,2,1,0:T(4,128)S(1)}, f32[2,6,4,1440]{3,2,1,0:T(4,128)S(1)}) custom-call(f32[12,12]{1,0:T(8,128)S(1)} %select_select_fusion.weight_ref, bf16[6,45,16,128]{3,2,1,0:T(8,128)(2,1)S(1)} %collective-permute-done.7.low_ref, bf16[6,45,16,128]{3,2,1,0:T(8,128)(2,1)S(1)} %get-tuple-element.28.own_ref, ...), custom_call_target="tpu_custom_call" | custom-call | flops 1000 | bytes 1000 | tf_op jit(solution)/shard_map/collect/pallas_call | solution.py:245
  111.7 0.0 collective-permute-done.4.low_ref
  111.7 17.2 %collective-permute-done.5.high_ref = bf16[4,45,16,128]{3,2,1,0:T(8,128)(2,1)S(1)} collective-permute-done((bf16[4,45,16,128]{3,2,1,0:T(8,128)(2,1)S(1)}, bf16[4,45,16,128]{3,2,1,0:T(8,128)(2,1)S(1)}, u32[]{:S(2)}, u32[]{:S(2)}) %collective-permute-start.5) | collective-permute-done | bytes 737312 | tf_op jit(solution)/shard_map/ppermute | solution.py:365
  128.9 7.4 %collect_theirs.1 = (f32[2,6,4,1440]{3,2,1,0:T(4,128)S(1)}, f32[4,4,16,1536]{3,2,1,0:T(8,128)S(1)}) custom-call(f32[12,12]{1,0:T(8,128)S(1)} %select_select_fusion.weight_ref, bf16[4,45,16,128]{3,2,1,0:T(8,128)(2,1)S(1)} %collective-permute-done.4.low_ref, bf16[4,45,16,128]{3,2,1,0:T(8,128)(2,1)S(1)} %get-tuple-element.24.own_ref, ...), custom_call_target="tpu_custom_call" | custom-call | flops 1000 | bytes 1000 | tf_op jit(solution)/shard_map/collect_theirs/pallas_call | solution.py:298
  136.3 2.4 %collective-permute-start.10 = (f32[2,6,4,1440]{3,2,1,0:T(4,128)S(1)}, f32[2,6,4,1440]{3,2,1,0:T(4,128)S(1)}, u32[]{:S(2)}, u32[]{:S(2)}) collective-permute-start(f32[2,6,4,1440]{3,2,1,0:T(4,128)S(1)} %get-tuple-element.34), channel_id=1, source_target_pairs={{0,128},{128,0},{256,384},{384,256},{512,640},{640,512},{1,129},{1... | collective-permute-start | bytes 829448 | tf_op jit(solution)/shard_map/ppermute | solution.py:399
  138.7 2.1 %collect_ours.1 = f32[2,6,4,1440]{3,2,1,0:T(4,128)S(1)} custom-call(f32[12,12]{1,0:T(8,128)S(1)} %select_select_fusion.weight_ref, f32[4,4,16,1536]{3,2,1,0:T(8,128)S(1)} %get-tuple-element.32.fields_ref, bf16[12,4,2,16,1440]{4,3,2,1,0:T(8,128)(2,1)S(1)} %copy-done.2, f32[2,6,4,1440]{3,2,1,0:T(4,128)S(1)} %get-tuple-element.33.before_ref), custom_call_target="tpu_custom_call" | custom-call | flops 1000 | bytes 1000 | tf_op jit(solution)/shard_map/collect_ours/pallas_call | solution.py:315
  140.8 0.0 collective-permute-done.10
  140.8 0.1 fusion.11
  141.0 4.5 %collective-permute-start.11 = (bf16[2,2,4,1440]{3,2,1,0:T(4,128)(2,1)S(1)}, bf16[2,2,4,1440]{3,2,1,0:T(4,128)(2,1)S(1)}, u32[]{:S(2)}, u32[]{:S(2)}) collective-permute-start(bf16[2,2,4,1440]{3,2,1,0:T(4,128)(2,1)S(1)} %get-tuple-element.37), channel_id=1, source_target_pairs={{0,256},{128,384},{256,512},{384,640},{512,0},{640,128},{1,257},{1... | collective-permute-start | bytes 138248 | tf_op jit(solution)/shard_map/ppermute | solution.py:400
  145.5 4.9 %collective-permute-start.12 = (bf16[2,2,4,1440]{3,2,1,0:T(4,128)(2,1)S(1)}, bf16[2,2,4,1440]{3,2,1,0:T(4,128)(2,1)S(1)}, u32[]{:S(2)}, u32[]{:S(2)}) collective-permute-start(bf16[2,2,4,1440]{3,2,1,0:T(4,128)(2,1)S(1)} %get-tuple-element.38), channel_id=1, source_target_pairs={{256,0},{384,128},{512,256},{640,384},{0,512},{128,640},{257,1},{3... | collective-permute-start | bytes 138248 | tf_op jit(solution)/shard_map/ppermute | solution.py:401
  150.4 0.0 collective-permute-done.11
  150.4 8.0 %collective-permute-done.12 = bf16[2,2,4,1440]{3,2,1,0:T(4,128)(2,1)S(1)} collective-permute-done((bf16[2,2,4,1440]{3,2,1,0:T(4,128)(2,1)S(1)}, bf16[2,2,4,1440]{3,2,1,0:T(4,128)(2,1)S(1)}, u32[]{:S(2)}, u32[]{:S(2)}) %collective-permute-start.12) | collective-permute-done | bytes 46112 | tf_op jit(solution)/shard_map/ppermute | solution.py:401
  158.4 0.7 fusion
  (6 shorter events, 0.1 us)
Async XLA Ops:
  0.0 30.3 %copy-start.6 = (s32[12]{0:T(128)S(1)}, s32[12]{0:T(128)}, u32[]{:S(2)}) copy-start(s32[12]{0:T(128)} %levels_ref.1) | copy-start | bytes 148
  0.0 3.2 %copy-start.5 = (f32[2,2,4,1440]{3,2,1,0:T(4,128)S(1)}, f32[2,2,4,1440]{3,2,1,0:T(4,128)}, u32[]{:S(2)}) copy-start(f32[2,2,4,1440]{3,2,1,0:T(4,128)} %param.4) | copy-start | bytes 276484
  3.2 27.3 %collective-permute-start = (f32[2,2,4,1440]{3,2,1,0:T(4,128)S(1)}, f32[2,2,4,1440]{3,2,1,0:T(4,128)S(1)}, u32[]{:S(2)}, u32[]{:S(2)}) collective-permute-start(f32[2,2,4,1440]{3,2,1,0:T(4,128)S(1)} %copy-done.5), channel_id=1, source_target_pairs={{256,0},{384,128},{512,256},{640,384},{0,512},{128,640},{257,1},{3... | collective-permute-start | bytes 276488 | tf_op jit(solution)/shard_map/ppermute | solution.py:379
  17.5 13.0 %collective-permute-start.1 = (f32[2,2,4,1440]{3,2,1,0:T(4,128)S(1)}, f32[2,2,4,1440]{3,2,1,0:T(4,128)S(1)}, u32[]{:S(2)}, u32[]{:S(2)}) collective-permute-start(f32[2,2,4,1440]{3,2,1,0:T(4,128)S(1)} %copy-done.5), channel_id=1, source_target_pairs={{0,256},{128,384},{256,512},{384,640},{512,0},{640,128},{1,257},{1... | collective-permute-start | bytes 276488 | tf_op jit(solution)/shard_map/ppermute | solution.py:380
  19.4 11.1 %collective-permute-start.2 = (f32[2,2,4,1440]{3,2,1,0:T(4,128)S(1)}, f32[2,2,4,1440]{3,2,1,0:T(4,128)S(1)}, u32[]{:S(2)}, u32[]{:S(2)}) collective-permute-start(f32[2,2,4,1440]{3,2,1,0:T(4,128)S(1)} %copy-done.5), channel_id=1, source_target_pairs={{0,128},{128,0},{256,384},{384,256},{512,640},{640,512},{1,129},{1... | collective-permute-start | bytes 276488 | tf_op jit(solution)/shard_map/ppermute | solution.py:381
  22.3 17.5 %collective-permute-start.6 = (bf16[2,45,16,128]{3,2,1,0:T(8,128)(2,1)}, bf16[2,45,16,128]{3,2,1,0:T(8,128)(2,1)S(1)}, u32[]{:S(2)}, u32[]{:S(2)}) collective-permute-start(bf16[2,45,16,128]{3,2,1,0:T(8,128)(2,1)} %get-tuple-element.20.own_ref), channel_id=1, source_target_pairs={{0,1},{1,2},{2,3},{3,4},{4,5},{5,6},{6,7},{7,8},{8,9},{9,10},{10,1... | collective-permute-start | bytes 1105928 | tf_op jit(solution)/shard_map/ppermute | solution.py:365
  25.4 22.3 %collective-permute-start.8 = (bf16[2,45,16,128]{3,2,1,0:T(8,128)(2,1)}, bf16[2,45,16,128]{3,2,1,0:T(8,128)(2,1)S(1)}, u32[]{:S(2)}, u32[]{:S(2)}) collective-permute-start(bf16[2,45,16,128]{3,2,1,0:T(8,128)(2,1)} %get-tuple-element.20.own_ref), channel_id=1, source_target_pairs={{1,0},{2,1},{3,2},{4,3},{5,4},{6,5},{7,6},{8,7},{9,8},{10,9},{11,1... | collective-permute-start | bytes 1105928 | tf_op jit(solution)/shard_map/ppermute | solution.py:365
  30.6 2.3 %copy-start = (bf16[12,4,2,16,1440]{4,3,2,1,0:T(8,128)(2,1)S(1)}, bf16[12,4,2,16,1440]{4,3,2,1,0:T(8,128)(2,1)}, u32[]{:S(2)}) copy-start(bf16[12,4,2,16,1440]{4,3,2,1,0:T(8,128)(2,1)} %get-tuple-element.22.refs_0_) | copy-start | bytes 13271044
  32.9 2.3 %copy-start.3 = (bf16[16,2,12,4,1440]{4,3,2,1,0:T(4,128)(2,1)S(1)}, bf16[16,2,12,4,1440]{4,3,2,1,0:T(4,128)(2,1)}, u32[]{:S(2)}) copy-start(bf16[16,2,12,4,1440]{4,3,2,1,0:T(4,128)(2,1)} %pert_ref.5) | copy-start | bytes 13271044
  39.8 39.2 %collective-permute-start.7 = (bf16[6,45,16,128]{3,2,1,0:T(8,128)(2,1)S(1)}, bf16[6,45,16,128]{3,2,1,0:T(8,128)(2,1)S(1)}, u32[]{:S(2)}, u32[]{:S(2)}) collective-permute-start(bf16[6,45,16,128]{3,2,1,0:T(8,128)(2,1)S(1)} %get-tuple-element.28.own_ref), channel_id=1, source_target_pairs={{0,1},{1,2},{2,3},{3,4},{4,5},{5,6},{6,7},{7,8},{8,9},{9,10},{10,1... | collective-permute-start | bytes 3317768 | tf_op jit(solution)/shard_map/ppermute | solution.py:365
  47.7 51.5 %collective-permute-start.9 = (bf16[6,45,16,128]{3,2,1,0:T(8,128)(2,1)S(1)}, bf16[6,45,16,128]{3,2,1,0:T(8,128)(2,1)S(1)}, u32[]{:S(2)}, u32[]{:S(2)}) collective-permute-start(bf16[6,45,16,128]{3,2,1,0:T(8,128)(2,1)S(1)} %get-tuple-element.28.own_ref), channel_id=1, source_target_pairs={{1,0},{2,1},{3,2},{4,3},{5,4},{6,5},{7,6},{8,7},{9,8},{10,9},{11,1... | collective-permute-start | bytes 3317768 | tf_op jit(solution)/shard_map/ppermute | solution.py:365
  54.4 4.5 %collective-permute-start.3 = (f32[3,2,2,4,1440]{4,3,2,1,0:T(4,128)S(1)}, f32[3,2,2,4,1440]{4,3,2,1,0:T(4,128)S(1)}, u32[]{:S(2)}, u32[]{:S(2)}) collective-permute-start(f32[3,2,2,4,1440]{4,3,2,1,0:T(4,128)S(1)} %pad_maximum_fusion.grad_ref), channel_id=1, source_target_pairs={{0,128},{128,0},{256,384},{384,256},{512,640},{640,512},{1,129},{1... | collective-permute-start | bytes 829448 | tf_op jit(solution)/shard_map/ppermute | solution.py:384
  58.9 12.2 %copy-start.4 = (bf16[2,45,16,128]{3,2,1,0:T(8,128)(2,1)S(1)}, bf16[2,45,16,128]{3,2,1,0:T(8,128)(2,1)}, u32[]{:S(2)}) copy-start(bf16[2,45,16,128]{3,2,1,0:T(8,128)(2,1)} %get-tuple-element.20.own_ref) | copy-start | bytes 1105924
  60.9 2.1 %copy-start.1 = (bf16[12,4,2,16,1440]{4,3,2,1,0:T(8,128)(2,1)}, bf16[12,4,2,16,1440]{4,3,2,1,0:T(8,128)(2,1)S(1)}, u32[]{:S(2)}) copy-start(bf16[12,4,2,16,1440]{4,3,2,1,0:T(8,128)(2,1)S(1)} %get-tuple-element.25.pert_ref) | copy-start | bytes 13271044
  63.0 48.7 %collective-permute-start.4 = (bf16[4,45,16,128]{3,2,1,0:T(8,128)(2,1)S(1)}, bf16[4,45,16,128]{3,2,1,0:T(8,128)(2,1)S(1)}, u32[]{:S(2)}, u32[]{:S(2)}) collective-permute-start(bf16[4,45,16,128]{3,2,1,0:T(8,128)(2,1)S(1)} %get-tuple-element.24.own_ref), channel_id=1, source_target_pairs={{0,1},{1,2},{2,3},{3,4},{4,5},{5,6},{6,7},{7,8},{8,9},{9,10},{10,1... | collective-permute-start | bytes 2211848 | tf_op jit(solution)/shard_map/ppermute | solution.py:365
  65.0 63.9 %collective-permute-start.5 = (bf16[4,45,16,128]{3,2,1,0:T(8,128)(2,1)S(1)}, bf16[4,45,16,128]{3,2,1,0:T(8,128)(2,1)S(1)}, u32[]{:S(2)}, u32[]{:S(2)}) collective-permute-start(bf16[4,45,16,128]{3,2,1,0:T(8,128)(2,1)S(1)} %get-tuple-element.24.own_ref), channel_id=1, source_target_pairs={{1,0},{2,1},{3,2},{4,3},{5,4},{6,5},{7,6},{8,7},{9,8},{10,9},{11,1... | collective-permute-start | bytes 2211848 | tf_op jit(solution)/shard_map/ppermute | solution.py:365
  71.1 2.3 %copy-start.2 = (bf16[12,4,2,16,1440]{4,3,2,1,0:T(8,128)(2,1)S(1)}, bf16[12,4,2,16,1440]{4,3,2,1,0:T(8,128)(2,1)}, u32[]{:S(2)}) copy-start(bf16[12,4,2,16,1440]{4,3,2,1,0:T(8,128)(2,1)} %copy-done.1) | copy-start | bytes 13271044
  136.3 4.5 %collective-permute-start.10 = (f32[2,6,4,1440]{3,2,1,0:T(4,128)S(1)}, f32[2,6,4,1440]{3,2,1,0:T(4,128)S(1)}, u32[]{:S(2)}, u32[]{:S(2)}) collective-permute-start(f32[2,6,4,1440]{3,2,1,0:T(4,128)S(1)} %get-tuple-element.34), channel_id=1, source_target_pairs={{0,128},{128,0},{256,384},{384,256},{512,640},{640,512},{1,129},{1... | collective-permute-start | bytes 829448 | tf_op jit(solution)/shard_map/ppermute | solution.py:399
  141.0 9.5 %collective-permute-start.11 = (bf16[2,2,4,1440]{3,2,1,0:T(4,128)(2,1)S(1)}, bf16[2,2,4,1440]{3,2,1,0:T(4,128)(2,1)S(1)}, u32[]{:S(2)}, u32[]{:S(2)}) collective-permute-start(bf16[2,2,4,1440]{3,2,1,0:T(4,128)(2,1)S(1)} %get-tuple-element.37), channel_id=1, source_target_pairs={{0,256},{128,384},{256,512},{384,640},{512,0},{640,128},{1,257},{1... | collective-permute-start | bytes 138248 | tf_op jit(solution)/shard_map/ppermute | solution.py:400
  145.5 13.0 %collective-permute-start.12 = (bf16[2,2,4,1440]{3,2,1,0:T(4,128)(2,1)S(1)}, bf16[2,2,4,1440]{3,2,1,0:T(4,128)(2,1)S(1)}, u32[]{:S(2)}, u32[]{:S(2)}) collective-permute-start(bf16[2,2,4,1440]{3,2,1,0:T(4,128)(2,1)S(1)} %get-tuple-element.38), channel_id=1, source_target_pairs={{256,0},{384,128},{512,256},{640,384},{0,512},{128,640},{257,1},{3... | collective-permute-start | bytes 138248 | tf_op jit(solution)/shard_map/ppermute | solution.py:401

commit v5 on v4

--- a/solution.py
+++ b/solution.py
@@ -360,8 +360,8 @@
     def halos(control, after=None):
         lower, upper = control, control
         if after is not None:
-            lower, _ = lax.optimization_barrier((control, after[0]))
-            upper, _ = lax.optimization_barrier((control, after[1]))
+            lower = lax.optimization_barrier((control, after[0], *after[2:]))[0]
+            upper = lax.optimization_barrier((control, after[1], *after[2:]))[0]
         return lax.ppermute(lower, "lat", forward), lax.ppermute(upper, "lat", backward)
 
     turned, own = prepare(
@@ -385,14 +385,18 @@
 
     sums = None
     groups = [(0, own, own_low, own_high)]
-    for first, size, gradient, skip in ((2, 6, near, 0), (8, 4, far, 0)):
+    for first, size, gradient, skip in ((2, 6, near, 0), (8, 2, far, 0), (10, 2, far, 2)):
         start = jnp.full((1,), first, jnp.int32)
         turned, control = prepare(
             first, size, order, start, perturbations, gradient, skip, turned
         )
-        low, upper = halos(control, (own_low, own_high) if first == 2 else None)
+        after = groups[0][2:] if first == 2 else None
+        if first == 10:
+            sums = collect(0, weights, own_low, own, own_high, turned, None)
+            after = (*groups[1][2:], sums[0])
+        low, upper = halos(control, after)
         groups.append((first, control, low, upper))
-    for first, control, low, upper in groups[:-1]:
+    for first, control, low, upper in groups[1:-1]:
         sums = collect(first, weights, low, control, upper, turned, sums)
     first, control, low, upper = groups[-1]
     theirs, ours = collect_last(first, weights, low, control, upper, turned, sums)

time: 160 us -> 163 us (1.019)
  the two profiles are of different devices: /device:TPU:31 before, /device:TPU:32 now
where the time goes in v5:
time: 163 us; the launch traced here: 162 us
  starting transfers between devices  76.9 us (47%)
  Pallas kernels  38.3 us (23%)
  waiting for transfers between devices  36.1 us (22%)
  local copies, waits for them, and re-layouts  9.19 us (6%)
    ppermute x4, starting transfers between devices, halos(): lax.ppermute(upper, 'lat', backward)  33.9 us
    pallas_call x3, Pallas kernels, collect(): pl.pallas_call(functools.partial(collect_kernel, first=first, lon=lon), o...  23.6 us
    ppermute x4, waiting for transfers between devices, halos(): lax.ppermute(lower, 'lat', forward)  21.3 us
    ppermute x1, starting transfers between devices, local(): lax.ppermute(gradient_here, 'mem', down)  14.5 us
    ppermute x4, starting transfers between devices, halos(): lax.ppermute(lower, 'lat', forward)  11 us
    unnamed x14, local copies, waits for them, and re-layouts  9.15 us
    pallas_call x4, Pallas kernels, prepare(): pl.pallas_call(prepare_kernel, out_shape=(jax.ShapeDtypeStruct((count, ro...  8.53 us
    ppermute x4, waiting for transfers between devices, halos(): lax.ppermute(upper, 'lat', backward)  6.78 us
  transfers between devices with their start and end apart: 15, of which 8 were waited for; matrix products, arithmetic and copies ran while one was open for 0% of the time, Pallas kernels for 19%

profile of v5, /device:TPU:32, one launch (start us, length us, event | category | flops | bytes accessed | tf_op | source)
XLA Modules:
  0.0 161.9 jit_solution(16488304894616360738)
XLA Ops:
  0.0 3.2 %prepare.4 = (bf16[12,4,2,16,1440]{4,3,2,1,0:T(8,128)(2,1)}, bf16[2,45,16,128]{3,2,1,0:T(8,128)(2,1)}) custom-call(s32[12]{0:T(128)} %levels_ref.1, s32[1]{0:T(128)} %bitcast.base_ref, bf16[16,2,12,4,1440]{4,3,2,1,0:T(4,128)(2,1)} %pert_ref.7, f32[1,2,2,4,1440]{4,3,2,1,0:T(4,128)} %bitcast.8), custom_call_target="tpu_custom_call" | custom-call | flops 1000 | bytes 1000 | tf_op jit(solution)/shard_map/prepare/pallas_call | solution.py:73
  3.2 14.5 %collective-permute-start = (f32[2,2,4,1440]{3,2,1,0:T(4,128)S(1)}, f32[2,2,4,1440]{3,2,1,0:T(4,128)S(1)}, u32[]{:S(2)}, u32[]{:S(2)}) collective-permute-start(f32[2,2,4,1440]{3,2,1,0:T(4,128)S(1)} %copy-done.5), channel_id=1, source_target_pairs={{256,0},{384,128},{512,256},{640,384},{0,512},{128,640},{257,1},{3... | collective-permute-start | bytes 276488 | tf_op jit(solution)/shard_map/ppermute | solution.py:379
  17.7 1.9 %collective-permute-start.1 = (f32[2,2,4,1440]{3,2,1,0:T(4,128)S(1)}, f32[2,2,4,1440]{3,2,1,0:T(4,128)S(1)}, u32[]{:S(2)}, u32[]{:S(2)}) collective-permute-start(f32[2,2,4,1440]{3,2,1,0:T(4,128)S(1)} %copy-done.5), channel_id=1, source_target_pairs={{0,256},{128,384},{256,512},{384,640},{512,0},{640,128},{1,257},{1... | collective-permute-start | bytes 276488 | tf_op jit(solution)/shard_map/ppermute | solution.py:380
  19.7 1.9 %collective-permute-start.2 = (f32[2,2,4,1440]{3,2,1,0:T(4,128)S(1)}, f32[2,2,4,1440]{3,2,1,0:T(4,128)S(1)}, u32[]{:S(2)}, u32[]{:S(2)}) collective-permute-start(f32[2,2,4,1440]{3,2,1,0:T(4,128)S(1)} %copy-done.5), channel_id=1, source_target_pairs={{0,128},{128,0},{256,384},{384,256},{512,640},{640,512},{1,129},{1... | collective-permute-start | bytes 276488 | tf_op jit(solution)/shard_map/ppermute | solution.py:381
  21.6 3.4 %collective-permute-start.4 = (bf16[2,45,16,128]{3,2,1,0:T(8,128)(2,1)}, bf16[2,45,16,128]{3,2,1,0:T(8,128)(2,1)S(1)}, u32[]{:S(2)}, u32[]{:S(2)}) collective-permute-start(bf16[2,45,16,128]{3,2,1,0:T(8,128)(2,1)} %get-tuple-element.26.own_ref), channel_id=1, source_target_pairs={{0,1},{1,2},{2,3},{3,4},{4,5},{5,6},{6,7},{7,8},{8,9},{9,10},{10,1... | collective-permute-start | bytes 1105928 | tf_op jit(solution)/shard_map/ppermute | solution.py:365
  25.0 8.5 %collective-permute-start.6 = (bf16[2,45,16,128]{3,2,1,0:T(8,128)(2,1)}, bf16[2,45,16,128]{3,2,1,0:T(8,128)(2,1)S(1)}, u32[]{:S(2)}, u32[]{:S(2)}) collective-permute-start(bf16[2,45,16,128]{3,2,1,0:T(8,128)(2,1)} %get-tuple-element.26.own_ref), channel_id=1, source_target_pairs={{1,0},{2,1},{3,2},{4,3},{5,4},{6,5},{7,6},{8,7},{9,8},{10,9},{11,1... | collective-permute-start | bytes 1105928 | tf_op jit(solution)/shard_map/ppermute | solution.py:365
  33.5 0.2 select_reduce_fusion.levels_ref
  33.7 0.0 collective-permute-done
  33.7 0.9 collective-permute-done.1
  34.6 0.0 collective-permute-done.2
  34.6 0.1 pad_maximum_fusion.grad_ref
  34.7 2.3 %copy-done = bf16[12,4,2,16,1440]{4,3,2,1,0:T(8,128)(2,1)S(1)} copy-done((bf16[12,4,2,16,1440]{4,3,2,1,0:T(8,128)(2,1)S(1)}, bf16[12,4,2,16,1440]{4,3,2,1,0:T(8,128)(2,1)}, u32[]{:S(2)}) %copy-start) | copy-done | bytes 4423704
  37.0 2.3 %copy-done.3 = bf16[16,2,12,4,1440]{4,3,2,1,0:T(4,128)(2,1)S(1)} copy-done((bf16[16,2,12,4,1440]{4,3,2,1,0:T(4,128)(2,1)S(1)}, bf16[16,2,12,4,1440]{4,3,2,1,0:T(4,128)(2,1)}, u32[]{:S(2)}) %copy-start.3) | copy-done | bytes 4423704
  39.4 2.7 %prepare.5 = (bf16[12,4,2,16,1440]{4,3,2,1,0:T(8,128)(2,1)S(1)}, bf16[6,45,16,128]{3,2,1,0:T(8,128)(2,1)S(1)}) custom-call(s32[12]{0:T(128)S(1)} %select_reduce_fusion.levels_ref, s32[1]{0:T(128)} %constant.92.clone.1.base_ref, bf16[16,2,12,4,1440]{4,3,2,1,0:T(4,128)(2,1)S(1)} %copy-done.3, ...), custom_call_target="tpu_custom_call", output_to_operand_aliasing={{0}: (4, {})} | custom-call | flops 1000 | bytes 1000 | tf_op jit(solution)/shard_map/prepare/pallas_call | solution.py:73
  42.1 5.6 %collective-permute-done.6.high_ref = bf16[2,45,16,128]{3,2,1,0:T(8,128)(2,1)S(1)} collective-permute-done((bf16[2,45,16,128]{3,2,1,0:T(8,128)(2,1)}, bf16[2,45,16,128]{3,2,1,0:T(8,128)(2,1)S(1)}, u32[]{:S(2)}, u32[]{:S(2)}) %collective-permute-start.6) | collective-permute-done | bytes 368672 | tf_op jit(solution)/shard_map/ppermute | solution.py:365
  47.7 10.3 %collective-permute-start.8 = (bf16[6,45,16,128]{3,2,1,0:T(8,128)(2,1)S(1)}, bf16[6,45,16,128]{3,2,1,0:T(8,128)(2,1)S(1)}, u32[]{:S(2)}, u32[]{:S(2)}) collective-permute-start(bf16[6,45,16,128]{3,2,1,0:T(8,128)(2,1)S(1)} %get-tuple-element.37.own_ref), channel_id=1, source_target_pairs={{1,0},{2,1},{3,2},{4,3},{5,4},{6,5},{7,6},{8,7},{9,8},{10,9},{11,1... | collective-permute-start | bytes 3317768 | tf_op jit(solution)/shard_map/ppermute | solution.py:365
  58.0 0.0 collective-permute-done.4.low_ref
  58.0 1.9 %collective-permute-start.5 = (bf16[6,45,16,128]{3,2,1,0:T(8,128)(2,1)S(1)}, bf16[6,45,16,128]{3,2,1,0:T(8,128)(2,1)S(1)}, u32[]{:S(2)}, u32[]{:S(2)}) collective-permute-start(bf16[6,45,16,128]{3,2,1,0:T(8,128)(2,1)S(1)} %get-tuple-element.37.own_ref), channel_id=1, source_target_pairs={{0,1},{1,2},{2,3},{3,4},{4,5},{5,6},{6,7},{7,8},{8,9},{9,10},{10,1... | collective-permute-start | bytes 3317768 | tf_op jit(solution)/shard_map/ppermute | solution.py:365
  59.9 1.9 %collective-permute-start.3 = (f32[3,2,2,4,1440]{4,3,2,1,0:T(4,128)S(1)}, f32[3,2,2,4,1440]{4,3,2,1,0:T(4,128)S(1)}, u32[]{:S(2)}, u32[]{:S(2)}) collective-permute-start(f32[3,2,2,4,1440]{4,3,2,1,0:T(4,128)S(1)} %pad_maximum_fusion.grad_ref), channel_id=1, source_target_pairs={{0,128},{128,0},{256,384},{384,256},{512,640},{640,512},{1,129},{1... | collective-permute-start | bytes 829448 | tf_op jit(solution)/shard_map/ppermute | solution.py:384
  61.9 0.1 select_select_fusion.weight_ref
  61.9 1.5 collective-permute-done.3.grad_ref
  63.4 1.3 prepare.6
  64.7 1.9 %collective-permute-start.10 = (bf16[2,45,16,128]{3,2,1,0:T(8,128)(2,1)S(1)}, bf16[2,45,16,128]{3,2,1,0:T(8,128)(2,1)S(1)}, u32[]{:S(2)}, u32[]{:S(2)}) collective-permute-start(bf16[2,45,16,128]{3,2,1,0:T(8,128)(2,1)S(1)} %get-tuple-element.39.own_ref), channel_id=1, source_target_pairs={{0,1},{1,2},{2,3},{3,4},{4,5},{5,6},{6,7},{7,8},{8,9},{9,10},{10,1... | collective-permute-start | bytes 1105928 | tf_op jit(solution)/shard_map/ppermute | solution.py:365
  66.7 9.9 %collective-permute-start.11 = (bf16[2,45,16,128]{3,2,1,0:T(8,128)(2,1)S(1)}, bf16[2,45,16,128]{3,2,1,0:T(8,128)(2,1)S(1)}, u32[]{:S(2)}, u32[]{:S(2)}) collective-permute-start(bf16[2,45,16,128]{3,2,1,0:T(8,128)(2,1)S(1)} %get-tuple-element.39.own_ref), channel_id=1, source_target_pairs={{1,0},{2,1},{3,2},{4,3},{5,4},{6,5},{7,6},{8,7},{9,8},{10,9},{11,1... | collective-permute-start | bytes 1105928 | tf_op jit(solution)/shard_map/ppermute | solution.py:365
  76.6 1.3 prepare.7
  77.9 2.1 %copy-done.1 = bf16[12,4,2,16,1440]{4,3,2,1,0:T(8,128)(2,1)} copy-done((bf16[12,4,2,16,1440]{4,3,2,1,0:T(8,128)(2,1)}, bf16[12,4,2,16,1440]{4,3,2,1,0:T(8,128)(2,1)S(1)}, u32[]{:S(2)}) %copy-start.1) | copy-done | bytes 4423704
  80.1 2.3 %copy-done.2 = bf16[12,4,2,16,1440]{4,3,2,1,0:T(8,128)(2,1)S(1)} copy-done((bf16[12,4,2,16,1440]{4,3,2,1,0:T(8,128)(2,1)S(1)}, bf16[12,4,2,16,1440]{4,3,2,1,0:T(8,128)(2,1)}, u32[]{:S(2)}) %copy-start.2) | copy-done | bytes 4423704
  82.4 5.5 %collect.3 = (f32[2,6,4,1440]{3,2,1,0:T(4,128)S(1)}, f32[2,6,4,1440]{3,2,1,0:T(4,128)S(1)}) custom-call(f32[12,12]{1,0:T(8,128)S(1)} %select_select_fusion.weight_ref, bf16[2,45,16,128]{3,2,1,0:T(8,128)(2,1)S(1)} %collective-permute-done.4.low_ref, bf16[2,45,16,128]{3,2,1,0:T(8,128)(2,1)S(1)} %copy-done.4, ...), custom_call_target="tpu_custom_call" | custom-call | flops 1000 | bytes 1000 | tf_op jit(solution)/shard_map/collect/pallas_call | solution.py:245
  87.9 0.0 collective-permute-done.8.high_ref
  87.9 5.2 %collective-permute-start.9 = (bf16[2,45,16,128]{3,2,1,0:T(8,128)(2,1)S(1)}, bf16[2,45,16,128]{3,2,1,0:T(8,128)(2,1)S(1)}, u32[]{:S(2)}, u32[]{:S(2)}) collective-permute-start(bf16[2,45,16,128]{3,2,1,0:T(8,128)(2,1)S(1)} %get-tuple-element.38.own_ref), channel_id=1, source_target_pairs={{1,0},{2,1},{3,2},{4,3},{5,4},{6,5},{7,6},{8,7},{9,8},{10,9},{11,1... | collective-permute-start | bytes 1105928 | tf_op jit(solution)/shard_map/ppermute | solution.py:365
  93.2 13.9 %collective-permute-done.5.low_ref = bf16[6,45,16,128]{3,2,1,0:T(8,128)(2,1)S(1)} collective-permute-done((bf16[6,45,16,128]{3,2,1,0:T(8,128)(2,1)S(1)}, bf16[6,45,16,128]{3,2,1,0:T(8,128)(2,1)S(1)}, u32[]{:S(2)}, u32[]{:S(2)}) %collective-permute-start.5) | collective-permute-done | bytes 1105952 | tf_op jit(solution)/shard_map/ppermute | solution.py:365
  107.1 3.8 %collective-permute-start.7 = (bf16[2,45,16,128]{3,2,1,0:T(8,128)(2,1)S(1)}, bf16[2,45,16,128]{3,2,1,0:T(8,128)(2,1)S(1)}, u32[]{:S(2)}, u32[]{:S(2)}) collective-permute-start(bf16[2,45,16,128]{3,2,1,0:T(8,128)(2,1)S(1)} %get-tuple-element.38.own_ref), channel_id=1, source_target_pairs={{0,1},{1,2},{2,3},{3,4},{4,5},{5,6},{6,7},{7,8},{8,9},{9,10},{10,1... | collective-permute-start | bytes 1105928 | tf_op jit(solution)/shard_map/ppermute | solution.py:365
  110.9 12.5 %collect.4 = (f32[2,6,4,1440]{3,2,1,0:T(4,128)S(1)}, f32[2,6,4,1440]{3,2,1,0:T(4,128)S(1)}) custom-call(f32[12,12]{1,0:T(8,128)S(1)} %select_select_fusion.weight_ref, bf16[6,45,16,128]{3,2,1,0:T(8,128)(2,1)S(1)} %collective-permute-done.5.low_ref, bf16[6,45,16,128]{3,2,1,0:T(8,128)(2,1)S(1)} %get-tuple-element.37.own_ref, ...), custom_call_target="tpu_custom_call" | custom-call | flops 1000 | bytes 1000 | tf_op jit(solution)/shard_map/collect/pallas_call | solution.py:245
  123.4 0.0 collective-permute-done.10.low_ref
  123.4 0.0 collective-permute-done.11.high_ref
  123.4 5.6 %collect.5 = (f32[2,6,4,1440]{3,2,1,0:T(4,128)S(1)}, f32[2,6,4,1440]{3,2,1,0:T(4,128)S(1)}) custom-call(f32[12,12]{1,0:T(8,128)S(1)} %select_select_fusion.weight_ref, bf16[2,45,16,128]{3,2,1,0:T(8,128)(2,1)S(1)} %collective-permute-done.10.low_ref, bf16[2,45,16,128]{3,2,1,0:T(8,128)(2,1)S(1)} %get-tuple-element.39.own_ref, ...), custom_call_target="tpu_custom_call" | custom-call | flops 1000 | bytes 1000 | tf_op jit(solution)/shard_map/collect/pallas_call | solution.py:245
  129.1 1.2 collective-permute-done.9.high_ref
  130.2 7.4 %collective-permute-done.7.low_ref = bf16[2,45,16,128]{3,2,1,0:T(8,128)(2,1)S(1)} collective-permute-done((bf16[2,45,16,128]{3,2,1,0:T(8,128)(2,1)S(1)}, bf16[2,45,16,128]{3,2,1,0:T(8,128)(2,1)S(1)}, u32[]{:S(2)}, u32[]{:S(2)}) %collective-permute-start.7) | collective-permute-done | bytes 368672 | tf_op jit(solution)/shard_map/ppermute | solution.py:365
  137.7 4.4 %collect_theirs.1 = (f32[2,6,4,1440]{3,2,1,0:T(4,128)S(1)}, f32[2,4,16,1536]{3,2,1,0:T(8,128)S(1)}) custom-call(f32[12,12]{1,0:T(8,128)S(1)} %select_select_fusion.weight_ref, bf16[2,45,16,128]{3,2,1,0:T(8,128)(2,1)S(1)} %collective-permute-done.7.low_ref, bf16[2,45,16,128]{3,2,1,0:T(8,128)(2,1)S(1)} %get-tuple-element.38.own_ref, ...), custom_call_target="tpu_custom_call" | custom-call | flops 1000 | bytes 1000 | tf_op jit(solution)/shard_map/collect_theirs/pallas_call | solution.py:298
  142.1 1.9 %collective-permute-start.12 = (f32[2,6,4,1440]{3,2,1,0:T(4,128)S(1)}, f32[2,6,4,1440]{3,2,1,0:T(4,128)S(1)}, u32[]{:S(2)}, u32[]{:S(2)}) collective-permute-start(f32[2,6,4,1440]{3,2,1,0:T(4,128)S(1)} %get-tuple-element.46), channel_id=1, source_target_pairs={{0,128},{128,0},{256,384},{384,256},{512,640},{640,512},{1,129},{1... | collective-permute-start | bytes 829448 | tf_op jit(solution)/shard_map/ppermute | solution.py:403
  144.0 1.7 %collect_ours.1 = f32[2,6,4,1440]{3,2,1,0:T(4,128)S(1)} custom-call(f32[12,12]{1,0:T(8,128)S(1)} %select_select_fusion.weight_ref, f32[2,4,16,1536]{3,2,1,0:T(8,128)S(1)} %get-tuple-element.44.fields_ref, bf16[12,4,2,16,1440]{4,3,2,1,0:T(8,128)(2,1)S(1)} %copy-done.2, f32[2,6,4,1440]{3,2,1,0:T(4,128)S(1)} %get-tuple-element.45.before_ref), custom_call_target="tpu_custom_call" | custom-call | flops 1000 | bytes 1000 | tf_op jit(solution)/shard_map/collect_ours/pallas_call | solution.py:315
  145.7 0.0 collective-permute-done.12
  145.7 0.1 fusion.11
  145.9 3.8 %collective-permute-start.13 = (bf16[2,2,4,1440]{3,2,1,0:T(4,128)(2,1)S(1)}, bf16[2,2,4,1440]{3,2,1,0:T(4,128)(2,1)S(1)}, u32[]{:S(2)}, u32[]{:S(2)}) collective-permute-start(bf16[2,2,4,1440]{3,2,1,0:T(4,128)(2,1)S(1)} %get-tuple-element.49), channel_id=1, source_target_pairs={{0,256},{128,384},{256,512},{384,640},{512,0},{640,128},{1,257},{1... | collective-permute-start | bytes 138248 | tf_op jit(solution)/shard_map/ppermute | solution.py:404
  149.7 5.9 %collective-permute-start.14 = (bf16[2,2,4,1440]{3,2,1,0:T(4,128)(2,1)S(1)}, bf16[2,2,4,1440]{3,2,1,0:T(4,128)(2,1)S(1)}, u32[]{:S(2)}, u32[]{:S(2)}) collective-permute-start(bf16[2,2,4,1440]{3,2,1,0:T(4,128)(2,1)S(1)} %get-tuple-element.50), channel_id=1, source_target_pairs={{256,0},{384,128},{512,256},{640,384},{0,512},{128,640},{257,1},{3... | collective-permute-start | bytes 138248 | tf_op jit(solution)/shard_map/ppermute | solution.py:405
  155.7 0.3 collective-permute-done.13
  155.9 5.4 %collective-permute-done.14 = bf16[2,2,4,1440]{3,2,1,0:T(4,128)(2,1)S(1)} collective-permute-done((bf16[2,2,4,1440]{3,2,1,0:T(4,128)(2,1)S(1)}, bf16[2,2,4,1440]{3,2,1,0:T(4,128)(2,1)S(1)}, u32[]{:S(2)}, u32[]{:S(2)}) %collective-permute-start.14) | collective-permute-done | bytes 46112 | tf_op jit(solution)/shard_map/ppermute | solution.py:405
  161.3 0.7 fusion
  (12 shorter events, 0.1 us)
Async XLA Ops:
  0.0 33.5 %copy-start.6 = (s32[12]{0:T(128)S(1)}, s32[12]{0:T(128)}, u32[]{:S(2)}) copy-start(s32[12]{0:T(128)} %levels_ref.1) | copy-start | bytes 148
  0.0 3.2 %copy-start.5 = (f32[2,2,4,1440]{3,2,1,0:T(4,128)S(1)}, f32[2,2,4,1440]{3,2,1,0:T(4,128)}, u32[]{:S(2)}) copy-start(f32[2,2,4,1440]{3,2,1,0:T(4,128)} %param.4) | copy-start | bytes 276484
  3.2 30.5 %collective-permute-start = (f32[2,2,4,1440]{3,2,1,0:T(4,128)S(1)}, f32[2,2,4,1440]{3,2,1,0:T(4,128)S(1)}, u32[]{:S(2)}, u32[]{:S(2)}) collective-permute-start(f32[2,2,4,1440]{3,2,1,0:T(4,128)S(1)} %copy-done.5), channel_id=1, source_target_pairs={{256,0},{384,128},{512,256},{640,384},{0,512},{128,640},{257,1},{3... | collective-permute-start | bytes 276488 | tf_op jit(solution)/shard_map/ppermute | solution.py:379
  17.7 16.9 %collective-permute-start.1 = (f32[2,2,4,1440]{3,2,1,0:T(4,128)S(1)}, f32[2,2,4,1440]{3,2,1,0:T(4,128)S(1)}, u32[]{:S(2)}, u32[]{:S(2)}) collective-permute-start(f32[2,2,4,1440]{3,2,1,0:T(4,128)S(1)} %copy-done.5), channel_id=1, source_target_pairs={{0,256},{128,384},{256,512},{384,640},{512,0},{640,128},{1,257},{1... | collective-permute-start | bytes 276488 | tf_op jit(solution)/shard_map/ppermute | solution.py:380
  19.7 14.9 %collective-permute-start.2 = (f32[2,2,4,1440]{3,2,1,0:T(4,128)S(1)}, f32[2,2,4,1440]{3,2,1,0:T(4,128)S(1)}, u32[]{:S(2)}, u32[]{:S(2)}) collective-permute-start(f32[2,2,4,1440]{3,2,1,0:T(4,128)S(1)} %copy-done.5), channel_id=1, source_target_pairs={{0,128},{128,0},{256,384},{384,256},{512,640},{640,512},{1,129},{1... | collective-permute-start | bytes 276488 | tf_op jit(solution)/shard_map/ppermute | solution.py:381
  21.6 36.4 %collective-permute-start.4 = (bf16[2,45,16,128]{3,2,1,0:T(8,128)(2,1)}, bf16[2,45,16,128]{3,2,1,0:T(8,128)(2,1)S(1)}, u32[]{:S(2)}, u32[]{:S(2)}) collective-permute-start(bf16[2,45,16,128]{3,2,1,0:T(8,128)(2,1)} %get-tuple-element.26.own_ref), channel_id=1, source_target_pairs={{0,1},{1,2},{2,3},{3,4},{4,5},{5,6},{6,7},{7,8},{8,9},{9,10},{10,1... | collective-permute-start | bytes 1105928 | tf_op jit(solution)/shard_map/ppermute | solution.py:365
  25.0 22.7 %collective-permute-start.6 = (bf16[2,45,16,128]{3,2,1,0:T(8,128)(2,1)}, bf16[2,45,16,128]{3,2,1,0:T(8,128)(2,1)S(1)}, u32[]{:S(2)}, u32[]{:S(2)}) collective-permute-start(bf16[2,45,16,128]{3,2,1,0:T(8,128)(2,1)} %get-tuple-element.26.own_ref), channel_id=1, source_target_pairs={{1,0},{2,1},{3,2},{4,3},{5,4},{6,5},{7,6},{8,7},{9,8},{10,9},{11,1... | collective-permute-start | bytes 1105928 | tf_op jit(solution)/shard_map/ppermute | solution.py:365
  34.7 2.3 %copy-start = (bf16[12,4,2,16,1440]{4,3,2,1,0:T(8,128)(2,1)S(1)}, bf16[12,4,2,16,1440]{4,3,2,1,0:T(8,128)(2,1)}, u32[]{:S(2)}) copy-start(bf16[12,4,2,16,1440]{4,3,2,1,0:T(8,128)(2,1)} %get-tuple-element.28.refs_0_) | copy-start | bytes 13271044
  37.0 2.3 %copy-start.3 = (bf16[16,2,12,4,1440]{4,3,2,1,0:T(4,128)(2,1)S(1)}, bf16[16,2,12,4,1440]{4,3,2,1,0:T(4,128)(2,1)}, u32[]{:S(2)}) copy-start(bf16[16,2,12,4,1440]{4,3,2,1,0:T(4,128)(2,1)} %pert_ref.7) | copy-start | bytes 13271044
  47.7 40.2 %collective-permute-start.8 = (bf16[6,45,16,128]{3,2,1,0:T(8,128)(2,1)S(1)}, bf16[6,45,16,128]{3,2,1,0:T(8,128)(2,1)S(1)}, u32[]{:S(2)}, u32[]{:S(2)}) collective-permute-start(bf16[6,45,16,128]{3,2,1,0:T(8,128)(2,1)S(1)} %get-tuple-element.37.own_ref), channel_id=1, source_target_pairs={{1,0},{2,1},{3,2},{4,3},{5,4},{6,5},{7,6},{8,7},{9,8},{10,9},{11,1... | collective-permute-start | bytes 3317768 | tf_op jit(solution)/shard_map/ppermute | solution.py:365
  58.0 49.1 %collective-permute-start.5 = (bf16[6,45,16,128]{3,2,1,0:T(8,128)(2,1)S(1)}, bf16[6,45,16,128]{3,2,1,0:T(8,128)(2,1)S(1)}, u32[]{:S(2)}, u32[]{:S(2)}) collective-permute-start(bf16[6,45,16,128]{3,2,1,0:T(8,128)(2,1)S(1)} %get-tuple-element.37.own_ref), channel_id=1, source_target_pairs={{0,1},{1,2},{2,3},{3,4},{4,5},{5,6},{6,7},{7,8},{8,9},{9,10},{10,1... | collective-permute-start | bytes 3317768 | tf_op jit(solution)/shard_map/ppermute | solution.py:365
  59.9 3.5 %collective-permute-start.3 = (f32[3,2,2,4,1440]{4,3,2,1,0:T(4,128)S(1)}, f32[3,2,2,4,1440]{4,3,2,1,0:T(4,128)S(1)}, u32[]{:S(2)}, u32[]{:S(2)}) collective-permute-start(f32[3,2,2,4,1440]{4,3,2,1,0:T(4,128)S(1)} %pad_maximum_fusion.grad_ref), channel_id=1, source_target_pairs={{0,128},{128,0},{256,384},{384,256},{512,640},{640,512},{1,129},{1... | collective-permute-start | bytes 829448 | tf_op jit(solution)/shard_map/ppermute | solution.py:384
  64.7 58.7 %collective-permute-start.10 = (bf16[2,45,16,128]{3,2,1,0:T(8,128)(2,1)S(1)}, bf16[2,45,16,128]{3,2,1,0:T(8,128)(2,1)S(1)}, u32[]{:S(2)}, u32[]{:S(2)}) collective-permute-start(bf16[2,45,16,128]{3,2,1,0:T(8,128)(2,1)S(1)} %get-tuple-element.39.own_ref), channel_id=1, source_target_pairs={{0,1},{1,2},{2,3},{3,4},{4,5},{5,6},{6,7},{7,8},{8,9},{9,10},{10,1... | collective-permute-start | bytes 1105928 | tf_op jit(solution)/shard_map/ppermute | solution.py:365
  66.7 56.7 %collective-permute-start.11 = (bf16[2,45,16,128]{3,2,1,0:T(8,128)(2,1)S(1)}, bf16[2,45,16,128]{3,2,1,0:T(8,128)(2,1)S(1)}, u32[]{:S(2)}, u32[]{:S(2)}) collective-permute-start(bf16[2,45,16,128]{3,2,1,0:T(8,128)(2,1)S(1)} %get-tuple-element.39.own_ref), channel_id=1, source_target_pairs={{1,0},{2,1},{3,2},{4,3},{5,4},{6,5},{7,6},{8,7},{9,8},{10,9},{11,1... | collective-permute-start | bytes 1105928 | tf_op jit(solution)/shard_map/ppermute | solution.py:365
  76.6 3.5 %copy-start.4 = (bf16[2,45,16,128]{3,2,1,0:T(8,128)(2,1)S(1)}, bf16[2,45,16,128]{3,2,1,0:T(8,128)(2,1)}, u32[]{:S(2)}) copy-start(bf16[2,45,16,128]{3,2,1,0:T(8,128)(2,1)} %get-tuple-element.26.own_ref) | copy-start | bytes 1105924
  77.9 2.1 %copy-start.1 = (bf16[12,4,2,16,1440]{4,3,2,1,0:T(8,128)(2,1)}, bf16[12,4,2,16,1440]{4,3,2,1,0:T(8,128)(2,1)S(1)}, u32[]{:S(2)}) copy-start(bf16[12,4,2,16,1440]{4,3,2,1,0:T(8,128)(2,1)S(1)} %get-tuple-element.34.pert_ref) | copy-start | bytes 13271044
  80.1 2.3 %copy-start.2 = (bf16[12,4,2,16,1440]{4,3,2,1,0:T(8,128)(2,1)S(1)}, bf16[12,4,2,16,1440]{4,3,2,1,0:T(8,128)(2,1)}, u32[]{:S(2)}) copy-start(bf16[12,4,2,16,1440]{4,3,2,1,0:T(8,128)(2,1)} %copy-done.1) | copy-start | bytes 13271044
  87.9 42.3 %collective-permute-start.9 = (bf16[2,45,16,128]{3,2,1,0:T(8,128)(2,1)S(1)}, bf16[2,45,16,128]{3,2,1,0:T(8,128)(2,1)S(1)}, u32[]{:S(2)}, u32[]{:S(2)}) collective-permute-start(bf16[2,45,16,128]{3,2,1,0:T(8,128)(2,1)S(1)} %get-tuple-element.38.own_ref), channel_id=1, source_target_pairs={{1,0},{2,1},{3,2},{4,3},{5,4},{6,5},{7,6},{8,7},{9,8},{10,9},{11,1... | collective-permute-start | bytes 1105928 | tf_op jit(solution)/shard_map/ppermute | solution.py:365
  107.1 30.6 %collective-permute-start.7 = (bf16[2,45,16,128]{3,2,1,0:T(8,128)(2,1)S(1)}, bf16[2,45,16,128]{3,2,1,0:T(8,128)(2,1)S(1)}, u32[]{:S(2)}, u32[]{:S(2)}) collective-permute-start(bf16[2,45,16,128]{3,2,1,0:T(8,128)(2,1)S(1)} %get-tuple-element.38.own_ref), channel_id=1, source_target_pairs={{0,1},{1,2},{2,3},{3,4},{4,5},{5,6},{6,7},{7,8},{8,9},{9,10},{10,1... | collective-permute-start | bytes 1105928 | tf_op jit(solution)/shard_map/ppermute | solution.py:365
  142.1 3.7 %collective-permute-start.12 = (f32[2,6,4,1440]{3,2,1,0:T(4,128)S(1)}, f32[2,6,4,1440]{3,2,1,0:T(4,128)S(1)}, u32[]{:S(2)}, u32[]{:S(2)}) collective-permute-start(f32[2,6,4,1440]{3,2,1,0:T(4,128)S(1)} %get-tuple-element.46), channel_id=1, source_target_pairs={{0,128},{128,0},{256,384},{384,256},{512,640},{640,512},{1,129},{1... | collective-permute-start | bytes 829448 | tf_op jit(solution)/shard_map/ppermute | solution.py:403
  145.9 10.0 %collective-permute-start.13 = (bf16[2,2,4,1440]{3,2,1,0:T(4,128)(2,1)S(1)}, bf16[2,2,4,1440]{3,2,1,0:T(4,128)(2,1)S(1)}, u32[]{:S(2)}, u32[]{:S(2)}) collective-permute-start(bf16[2,2,4,1440]{3,2,1,0:T(4,128)(2,1)S(1)} %get-tuple-element.49), channel_id=1, source_target_pairs={{0,256},{128,384},{256,512},{384,640},{512,0},{640,128},{1,257},{1... | collective-permute-start | bytes 138248 | tf_op jit(solution)/shard_map/ppermute | solution.py:404
  149.7 11.5 %collective-permute-start.14 = (bf16[2,2,4,1440]{3,2,1,0:T(4,128)(2,1)S(1)}, bf16[2,2,4,1440]{3,2,1,0:T(4,128)(2,1)S(1)}, u32[]{:S(2)}, u32[]{:S(2)}) collective-permute-start(bf16[2,2,4,1440]{3,2,1,0:T(4,128)(2,1)S(1)} %get-tuple-element.50), channel_id=1, source_target_pairs={{256,0},{384,128},{512,256},{640,384},{0,512},{128,640},{257,1},{3... | collective-permute-start | bytes 138248 | tf_op jit(solution)/shard_map/ppermute | solution.py:405
